TPU v7x, 32 devices: a whole 2x2x4 slice. The times are simulated.
32 devices in a mesh: fsdp: 8 (over y, x, core), ctx: 4 (over z).
Axes of the slice: x: 2, y: 2, z: 4, core: 2. Of those that a mesh axis runs over, the one named last changes fastest.
Arguments:
- activations: float32 [8192, 1536], P(('fsdp', 'ctx')), may hold values from -6 to 6
- in_weight: bfloat16 [2, 1536, 6448], P(None, 'fsdp'), may hold values from -0.15625 to 0.15625
- out_weight: bfloat16 [2, 3072, 1536], P(None, 'fsdp'), may hold values from -0.109375 to 0.109375
- norm_gain: float32 [2, 1536], replicated, may hold values from 0.25 to 1.75
- conv_weight: float32 [2, 4, 3328], replicated, may hold values from -3 to 3
- conv_bias: float32 [2, 3328], replicated, may hold values from -3 to 3
- step_bias: float32 [2, 48], replicated, may hold values from -9 to -3
- decay_log: float32 [2, 48], replicated, may hold values from -1.5 to 2
- skip_gain: float32 [2, 48], replicated, may hold values from 0.5 to 1.5
- gate_gain: float32 [2, 3072], replicated, may hold values from 0.25 to 1.75
- cotangent: float32 [8192, 1536], P(('fsdp', 'ctx')), may hold values from -6 to 6
Outputs:
- block_out: float32 [8192, 1536], P(('fsdp', 'ctx'))
- grad_input: float32 [8192, 1536], P(('fsdp', 'ctx'))
- grad_in_weight: float32 [2, 1536, 6448], P(None, ('fsdp', 'ctx'))
- grad_out_weight: float32 [2, 3072, 1536], P(None, ('fsdp', 'ctx'))
- grad_norm_gain: float32 [2, 1536], replicated
- grad_conv_weight: float32 [2, 4, 3328], replicated
- grad_conv_bias: float32 [2, 3328], replicated
- grad_step_bias: float32 [2, 48], replicated
- grad_decay_log: float32 [2, 48], replicated
- grad_skip_gain: float32 [2, 48], replicated
- grad_gate_gain: float32 [2, 3072], replicated
All inputs are finite; a program needn't handle non-finite values.
Results may differ from a plain program's by a relative error of at most 0.0097.
Values may be sent and summed in bfloat16 or wider, within the bound.
No kernel may reach another device: no remote copies, remote signals or barrier semaphores. Data moves between devices by JAX's collectives and lax.ppermute only.
A program may use at most 384 MiB of HBM per device.

v0:
```python
import jax
import jax.numpy as jnp
from jax import lax
from jax.sharding import PartitionSpec as P

H = 48
P_SIZE = 64
N = 128
CONV = 4
GROUP = 256
LAYERS = 2
DI = 3072
CC = 3328


EPS = 1e-05
HIGH = lax.Precision.HIGHEST


def passed_along(value, axis, steps):
    count = lax.axis_size(axis)
    initial, last = (max(0, -steps), min(count, count - steps))
    return lax.ppermute(value, axis, [(source, source + steps) for source in range(initial, last)])


def rms_norm(values, gain_row):
    return values * lax.rsqrt(jnp.mean(values * values, axis=-1, keepdims=True) + EPS) * gain_row


def gated_norm(ssm_out, gate_in, gain_row):
    gated = ssm_out * jax.nn.silu(gate_in)
    return gated * lax.rsqrt(jnp.mean(gated * gated, axis=-1, keepdims=True) + EPS) * gain_row


def conv_act(extended, taps, bias_row):
    length = extended.shape[0] - (CONV - 1)
    summed = jnp.zeros((length, extended.shape[1]), jnp.float32) + bias_row[None, :]
    for offset in range(CONV):
        summed = summed + extended[offset : offset + length] * taps[offset][None, :]
    return jax.nn.silu(summed)


def block_scan(x_heads, b_rows, c_rows, step_sizes, log_decay, skip_row, start):
    blocks = x_heads.shape[0] // GROUP
    x_blocks = x_heads.reshape(blocks, GROUP, H, P_SIZE)
    b_blocks = b_rows.reshape(blocks, GROUP, N)
    c_blocks = c_rows.reshape(blocks, GROUP, N)
    step_blocks = jnp.transpose(step_sizes.reshape(blocks, GROUP, H), (0, 2, 1))
    cum_decay = jnp.cumsum(jnp.transpose(log_decay.reshape(blocks, GROUP, H), (0, 2, 1)), axis=2)
    scores = jnp.einsum("bln,bsn->bls", c_blocks, b_blocks, precision=HIGH)
    causal = jnp.arange(GROUP)[:, None] >= jnp.arange(GROUP)[None, :]
    decay_gaps = cum_decay[:, :, :, None] - cum_decay[:, :, None, :]
    decays = jnp.where(causal, jnp.exp(jnp.where(causal, decay_gaps, 0.0)), 0.0)
    mixing = scores[:, None, :, :] * decays * step_blocks[:, :, None, :]
    intra_out = jnp.einsum("bhls,bshp->blhp", mixing, x_blocks, precision=HIGH)
    tail_weight = jnp.exp(cum_decay[:, :, -1:] - cum_decay) * step_blocks
    weighted = x_blocks * jnp.transpose(tail_weight, (0, 2, 1))[:, :, :, None]
    states = jnp.einsum("bshp,bsn->bhpn", weighted, b_blocks, precision=HIGH)
    totals = jnp.exp(cum_decay[:, :, -1])

    def advance(state_now, block_items):
        factor, new_state = block_items
        return (factor[:, None, None] * state_now + new_state, state_now)

    last_state, entering = lax.scan(advance, start, (totals, states))
    inter_out = jnp.einsum("bln,bhpn->blhp", c_blocks, entering, precision=HIGH)
    inter_out = inter_out * jnp.exp(jnp.transpose(cum_decay, (0, 2, 1)))[:, :, :, None]
    result = intra_out + inter_out + skip_row[None, None, :, None] * x_blocks
    return (result.reshape(blocks * GROUP, H * P_SIZE), last_state)


def mixer(activated, raw_steps, bias_row, log_row, skip_row, start):
    x_heads = activated[:, :DI].reshape(-1, H, P_SIZE)
    b_rows = activated[:, DI : DI + N]
    c_rows = activated[:, DI + N :]
    step_sizes = jax.nn.softplus(raw_steps + bias_row[None, :])
    log_decay = -step_sizes * jnp.exp(log_row)[None, :]
    return block_scan(x_heads, b_rows, c_rows, step_sizes, log_decay, skip_row, start)


def rows_product(left, right):
    return lax.dot_general(
        left, right, (((0,), (0,)), ((), ())), preferred_element_type=jnp.float32
    )


def right_transposed(left, right):
    return lax.dot_general(
        left, right, (((1,), (1,)), ((), ())), preferred_element_type=jnp.float32
    )


def carry_forward(totals, local_state):
    incoming = jnp.zeros_like(local_state)
    for hop_index in range(lax.axis_size("ctx") - 1):
        incoming = passed_along(totals[:, None, None] * incoming + local_state, "ctx", 1)
    return incoming


def carry_backward(totals, local_grad):
    outgoing = jnp.zeros_like(local_grad)
    for hop_index in range(lax.axis_size("ctx") - 1):
        outgoing = passed_along(totals[:, None, None] * outgoing + local_grad, "ctx", -1)
    return outgoing


def weight_gradients(normed, d_proj, gnormed, grad_bf):
    tok_rows = normed.shape[0]
    fsdp_count = lax.axis_size("fsdp")
    ctx_count = lax.axis_size("ctx")
    width_in = d_proj.shape[1]
    inner = gnormed.shape[1]
    tile_rows = inner // (fsdp_count * ctx_count)
    all_rows = (
        lax.all_gather(normed, "ctx", axis=0, tiled=True),
        lax.all_gather(grad_bf, "ctx", axis=0, tiled=True),
    )
    proj_split = d_proj.reshape(tok_rows, 1, ctx_count, width_in // ctx_count)
    gate_split = gnormed.reshape(tok_rows, fsdp_count, ctx_count, tile_rows)
    cols = (
        lax.all_to_all(proj_split, "ctx", split_axis=2, concat_axis=0, tiled=True),
        lax.all_to_all(gate_split, "ctx", split_axis=2, concat_axis=0, tiled=True),
    )
    proj_cols = cols[0].reshape(ctx_count * tok_rows, width_in // ctx_count)
    gate_cols = cols[1].reshape(ctx_count * tok_rows, fsdp_count * tile_rows)
    part_in = rows_product(all_rows[0], proj_cols)
    part_out = rows_product(gate_cols, all_rows[1])
    summed = (
        lax.psum_scatter(part_in, "fsdp", scatter_dimension=0, tiled=True),
        lax.psum_scatter(part_out, "fsdp", scatter_dimension=0, tiled=True),
    )
    owned_in = lax.all_to_all(summed[0], "ctx", split_axis=0, concat_axis=1, tiled=True)
    return (owned_in, summed[1])


def local(
    activations,
    in_weight,
    out_weight,
    norm_gain,
    conv_weight,
    conv_bias,
    step_bias,
    decay_log,
    skip_gain,
    gate_gain,
    cotangent,
):
    tok_rows = activations.shape[0]
    edge_count = CONV - 1
    stream = activations
    kept = []
    for layer_index in range(LAYERS):
        full_in, full_out = (
            lax.all_gather(in_weight[layer_index], "fsdp", axis=0, tiled=True),
            lax.all_gather(out_weight[layer_index], "fsdp", axis=0, tiled=True),
        )
        normed = rms_norm(stream, norm_gain[layer_index]).astype(jnp.bfloat16)
        projected = jnp.dot(normed, full_in, preferred_element_type=jnp.float32)
        gate_in = projected[:, :DI]
        conv_in = projected[:, DI : DI + CC].astype(jnp.bfloat16)
        raw_steps = projected[:, DI + CC :]
        edge_in = passed_along(conv_in[tok_rows - edge_count :], "ctx", 1)
        extended = jnp.concatenate([edge_in, conv_in], 0).astype(jnp.float32)
        activated = conv_act(extended, conv_weight[layer_index], conv_bias[layer_index])
        local_out, local_state = mixer(
            activated,
            raw_steps,
            step_bias[layer_index],
            decay_log[layer_index],
            skip_gain[layer_index],
            jnp.zeros((H, P_SIZE, N), jnp.float32),
        )
        step_sizes = jax.nn.softplus(raw_steps + step_bias[layer_index][None, :])
        piece_decay = jnp.cumsum(-step_sizes * jnp.exp(decay_log[layer_index])[None, :], axis=0)
        totals = jnp.exp(piece_decay[-1])
        incoming = carry_forward(totals, local_state)
        carried = jnp.einsum("tn,hpn->thp", activated[:, DI + N :], incoming, precision=HIGH)
        carried = carried * jnp.exp(piece_decay)[:, :, None]
        ssm_out = local_out + carried.reshape(tok_rows, DI)
        gnormed = gated_norm(ssm_out, gate_in, gate_gain[layer_index]).astype(jnp.bfloat16)
        kept.append(
            (
                full_in,
                full_out,
                stream,
                normed,
                gate_in,
                extended,
                activated,
                raw_steps,
                incoming,
                piece_decay,
                totals,
                ssm_out,
                gnormed,
            )
        )
        stream = stream + jnp.dot(gnormed, full_out, preferred_element_type=jnp.float32)
    grad_stream = cotangent
    collected = []
    for layer_index in reversed(range(LAYERS)):
        (
            kept_in,
            kept_out,
            stream_in,
            normed,
            gate_in,
            extended,
            activated,
            raw_steps,
            incoming,
            piece_decay,
            totals,
            ssm_out,
            gnormed,
        ) = kept[layer_index]
        back_in, back_out = (
            lax.all_gather(in_weight[layer_index], "fsdp", axis=0, tiled=True),
            lax.all_gather(out_weight[layer_index], "fsdp", axis=0, tiled=True),
        )
        grad_bf = grad_stream.astype(jnp.bfloat16)
        d_gnormed = right_transposed(grad_bf, back_out)
        unused_out, pullback = jax.vjp(gated_norm, ssm_out, gate_in, gate_gain[layer_index])
        d_ssm, d_gate, g_gate = pullback(d_gnormed)
        weighted_grad = d_ssm.reshape(tok_rows, H, P_SIZE) * jnp.exp(piece_decay)[:, :, None]
        local_grad = jnp.einsum(
            "thp,tn->hpn", weighted_grad, activated[:, DI + N :], precision=HIGH
        )
        outgoing = carry_backward(totals, local_grad)

        def mix_from(act_in, steps_in, bias_in, log_in, skip_in):
            return mixer(act_in, steps_in, bias_in, log_in, skip_in, incoming)

        unused_mix, pullback = jax.vjp(
            mix_from,
            activated,
            raw_steps,
            step_bias[layer_index],
            decay_log[layer_index],
            skip_gain[layer_index],
        )
        d_act, d_steps, g_bias, g_log, g_skip = pullback((d_ssm, outgoing))
        unused_act, pullback = jax.vjp(
            conv_act, extended, conv_weight[layer_index], conv_bias[layer_index]
        )
        d_ext, g_taps, g_cbias = pullback(d_act)
        edge_back = passed_along(d_ext[:edge_count], "ctx", -1)
        d_conv_in = d_ext[edge_count:] + jnp.concatenate(
            [jnp.zeros((tok_rows - edge_count, CC), jnp.float32), edge_back], 0
        )
        d_proj = jnp.concatenate([d_gate, d_conv_in, d_steps], 1).astype(jnp.bfloat16)
        d_normed = right_transposed(d_proj, back_in)
        unused_norm, pullback = jax.vjp(rms_norm, stream_in, norm_gain[layer_index])
        d_stream, g_norm = pullback(d_normed)
        grad_stream = grad_stream + d_stream
        owned_in, owned_out = weight_gradients(normed, d_proj, gnormed, grad_bf)
        collected.append(
            (owned_in, owned_out, g_norm, g_taps, g_cbias, g_bias, g_log, g_skip, g_gate)
        )
    collected = collected[::-1]
    stacked = [jnp.stack([entry[member] for entry in collected], 0) for member in range(9)]
    summed = lax.psum(
        (stacked[2], stacked[3], stacked[4], stacked[5], stacked[6], stacked[7], stacked[8]),
        ("fsdp", "ctx"),
    )
    return (
        stream,
        grad_stream,
        stacked[0],
        stacked[1],
        summed[0],
        summed[1],
        summed[2],
        summed[3],
        summed[4],
        summed[5],
        summed[6],
    )


def solution(mesh):
    placed = (
        P(("fsdp", "ctx"), None),
        P(None, "fsdp", None),
        P(None, "fsdp", None),
        P(),
        P(),
        P(),
        P(),
        P(),
        P(),
        P(),
        P(("fsdp", "ctx"), None),
    )
    return jax.shard_map(
        local,
        mesh=mesh,
        in_specs=placed,
        out_specs=(
            P(("fsdp", "ctx"), None),
            P(("fsdp", "ctx"), None),
            P(None, ("fsdp", "ctx"), None),
            P(None, ("fsdp", "ctx"), None),
            P(),
            P(),
            P(),
            P(),
            P(),
            P(),
            P(),
        ),
        check_vma=False,
    )
```

profile of v0, /device:TPU:0, one launch (start us, length us, event | category | flops | bytes accessed | tf_op | source)
XLA Modules:
  0.0 1522.2 jit_solution(14111896596998684746)
XLA Ops:
  7.2 5.1 fusion.200
  20.2 98.5 %all-gather.21.cloned.1.call-done = bf16[1,1536,6448]{2,1,0:T(8,128)(2,1)} async-done(((bf16[1,192,6448]{2,1,0:T(8,128)(2,1)}), bf16[1,1536,6448]{2,1,0:T(8,128)(2,1)}) %all-gather.21.cloned.1.call-update) | async-done | bytes 19808272 | tf_op jit(solution)/shard_map/all_gather | solution.py:155
  118.8 14.3 fusion.205
  147.7 7.0 fusion.63
  163.6 33.7 %collective-permute-done.1 = f32[48,64,128]{2,1,0:T(8,128)S(1)} collective-permute-done((f32[48,64,128]{2,1,0:T(8,128)S(1)}, f32[48,64,128]{2,1,0:T(8,128)S(1)}, u32[]{:S(2)}, u32[]{:S(2)}) %collective-permute-start.1) | collective-permute-done | bytes 1572896 | tf_op jit(solution)/shard_map/ppermute | solution.py:23
  198.6 5.5 collective-permute-start.2
  213.2 23.1 %collective-permute-done.2 = f32[48,64,128]{2,1,0:T(8,128)} collective-permute-done((f32[48,64,128]{2,1,0:T(8,128)}, f32[48,64,128]{2,1,0:T(8,128)}, u32[]{:S(2)}, u32[]{:S(2)}) %collective-permute-start.2) | collective-permute-done | bytes 1572896 | tf_op jit(solution)/shard_map/ppermute | solution.py:23
  238.6 4.6 collective-permute-start.3
  246.3 14.9 fusion.69
  261.2 13.9 collective-permute-done.3
  275.1 4.3 broadcast_multiply_fusion.9
  286.1 5.6 multiply_reduce_fusion.28
  293.1 15.7 %fusion.206 = (bf16[256,6448]{0,1:T(8,128)(2,1)}, f32[256,6448]{0,1:T(8,128)}) fusion(bf16[256,1536]{1,0:T(8,128)(2,1)S(1)} %multiply_convert_fusion.2, bf16[1,1536,6448]{2,1,0:T(8,128)(2,1)} %all-gather.25.cloned.1.call-done), kind=kOutput, calls=%fused_computation.389 | convolution fusion | flops 5072564224 | bytes 30498816 | tf_op jit(solution)/shard_map/dot_general | solution.py:159
  325.0 7.2 fusion.62
  340.9 50.2 %collective-permute-done.5 = f32[48,64,128]{2,1,0:T(8,128)S(1)} collective-permute-done((f32[48,64,128]{2,1,0:T(8,128)S(1)}, f32[48,64,128]{2,1,0:T(8,128)S(1)}, u32[]{:S(2)}, u32[]{:S(2)}) %collective-permute-start.5) | collective-permute-done | bytes 1572896 | tf_op jit(solution)/shard_map/ppermute | solution.py:23
  392.5 19.9 %collective-permute-start.6 = (f32[48,64,128]{2,1,0:T(8,128)}, f32[48,64,128]{2,1,0:T(8,128)}, u32[]{:S(2)}, u32[]{:S(2)}) collective-permute-start(f32[48,64,128]{2,1,0:T(8,128)} %multiply_add_fusion.7), channel_id=1, source_target_pairs={{0,1},{1,2},{2,3},{4,5},{5,6},{6,7},{8,9},{9,10},{10,11},{12,13},{... | collective-permute-start | bytes 4718600 | tf_op jit(solution)/shard_map/ppermute | solution.py:23
  424.2 32.3 %collective-permute-done.6 = f32[48,64,128]{2,1,0:T(8,128)} collective-permute-done((f32[48,64,128]{2,1,0:T(8,128)}, f32[48,64,128]{2,1,0:T(8,128)}, u32[]{:S(2)}, u32[]{:S(2)}) %collective-permute-start.6) | collective-permute-done | bytes 1572896 | tf_op jit(solution)/shard_map/ppermute | solution.py:23
  458.8 4.7 collective-permute-start.7
  466.6 14.9 fusion.68
  481.5 47.6 %collective-permute-done.7 = f32[48,64,128]{2,1,0:T(8,128)S(1)} collective-permute-done((f32[48,64,128]{2,1,0:T(8,128)S(1)}, f32[48,64,128]{2,1,0:T(8,128)S(1)}, u32[]{:S(2)}, u32[]{:S(2)}) %collective-permute-start.7) | collective-permute-done | bytes 1572896 | tf_op jit(solution)/shard_map/ppermute | solution.py:23
  529.1 4.4 broadcast_multiply_fusion.8
  537.8 8.5 multiply_reduce_fusion.12
  546.4 7.2 multiply_reduce_fusion.14
  559.1 96.3 %collective-permute-done.8 = f32[48,64,128]{2,1,0:T(8,128)} collective-permute-done((f32[48,64,128]{2,1,0:T(8,128)}, f32[48,64,128]{2,1,0:T(8,128)}, u32[]{:S(2)}, u32[]{:S(2)}) %collective-permute-start.8) | collective-permute-done | bytes 1572896 | tf_op jit(solution)/shard_map/ppermute | solution.py:23
  658.9 21.9 %fusion.31 = (f32[48,256]{1,0:T(8,128)}, f32[48,256]{1,0:T(8,128)}, f32[48,256]{1,0:T(8,128)}, f32[256,256]{1,0:T(8,128)S(1)}) fusion(f32[48,256]{1,0:T(8,128)} %copy.419, f32[48,256]{1,0:T(8,128)} %copy-done.147, f32[256,256]{1,0:T(8,128)} %copy-done.91, pred[256,256]{1,0:T(8,128)(4,1)} %iota_compare_fusion, f32[48,64,256]{2,1,0:T(8,128)S(1)} %bitcast.652, ...), kind=kOutput, calls=%fused_computation.35 | convolution fusion | flops 2463002624 | bytes 7127040 | tf_op jit(solution)/shard_map/transpose(jvp(bhls,bshp->blhp))/dot_general | solution.py:55
  684.2 8.3 collective-permute-done.9
  703.8 5.3 fusion.106
  709.2 6.9 fusion.65
  716.1 13.7 collective-permute-done.10
  729.8 4.8 fusion.73
  734.6 12.7 bitcast_add_fusion.1
  747.3 4.3 fusion.105
  751.6 8.4 multiply_reduce_fusion.7
  763.4 5.8 pad_add_fusion.1
  785.9 6.7 all-to-all-start.2
  792.6 11.8 multiply_reduce_fusion.22
  804.5 4.3 fusion.196
  808.8 7.3 multiply_reduce_fusion.13
  816.2 5.7 multiply_reduce_fusion.15
  827.7 22.8 %fusion.33 = (f32[48,256]{1,0:T(8,128)}, f32[48,256]{1,0:T(8,128)}, f32[48,256]{1,0:T(8,128)}, f32[256,256]{1,0:T(8,128)S(1)}) fusion(f32[48,256]{1,0:T(8,128)S(1)} %copy-done.143, f32[48,256]{1,0:T(8,128)} %copy-done.144, f32[256,256]{1,0:T(8,128)S(1)} %copy-done.89, pred[256,256]{1,0:T(8,128)(4,1)S(1)} %copy-done.137, f32[48,64,256]{2,1,0:T(8,128)} %bitcast.647, ...), kind=kOutput, calls=%fused_computation.37 | convolution fusion | flops 2463002624 | bytes 7127040 | tf_op jit(solution)/shard_map/transpose(jvp(bhls,bshp->blhp))/dot_general | solution.py:55
  850.5 77.7 %collective-permute-done.12 = f32[48,64,128]{2,1,0:T(8,128)} collective-permute-done((f32[48,64,128]{2,1,0:T(8,128)}, f32[48,64,128]{2,1,0:T(8,128)}, u32[]{:S(2)}, u32[]{:S(2)}) %collective-permute-start.12) | collective-permute-done | bytes 1572896 | tf_op jit(solution)/shard_map/ppermute | solution.py:23
  937.5 4.6 fusion.67
  942.1 42.4 %collective-permute-done.13 = f32[48,64,128]{2,1,0:T(8,128)S(1)} collective-permute-done((f32[48,64,128]{2,1,0:T(8,128)S(1)}, f32[48,64,128]{2,1,0:T(8,128)S(1)}, u32[]{:S(2)}, u32[]{:S(2)}) %collective-permute-start.13) | collective-permute-done | bytes 1572896 | tf_op jit(solution)/shard_map/ppermute | solution.py:23
  987.3 4.8 copy.480
  992.1 9.9 fusion.208
  1012.2 10.7 collective-permute-done.14
  1022.9 7.4 fusion.71
  1039.1 5.5 fusion.103
  1044.7 13.7 bitcast_add_fusion
  1058.4 8.0 multiply_reduce_fusion.11
  1078.7 8.4 pad_add_fusion
  1098.8 77.0 %all_to_all.92 = bf16[256,1,4,1612]{0,3,1,2:T(8,128)(2,1)S(1)} all-to-all(bf16[256,1,4,1612]{0,3,1,2:T(8,128)(2,1)} %bitcast.664), channel_id=1, replica_groups=mesh['fsdp'=8,'ctx'=4] {'ctx'}, dimensions={2} | all-to-all | bytes 6602752 | tf_op jit(solution)/shard_map/all_to_all | solution.py:121
  1179.5 10.8 fusion.207
  1191.8 38.1 %all_to_all.93 = bf16[256,8,4,96]{0,3,1,2:T(8,128)(2,1)S(1)} all-to-all(bf16[256,8,4,96]{0,3,1,2:T(8,128)(2,1)S(1)} %copy.484), channel_id=1, replica_groups=mesh['fsdp'=8,'ctx'=4] {'ctx'}, dimensions={2} | all-to-all | bytes 3145728 | tf_op jit(solution)/shard_map/all_to_all | solution.py:122
  1231.6 6.1 fusion.210
  1239.2 39.1 %all_to_all.94 = bf16[256,8,4,96]{0,3,1,2:T(8,128)(2,1)S(1)} all-to-all(bf16[256,8,4,96]{0,3,1,2:T(8,128)(2,1)S(1)} %copy.482), channel_id=1, replica_groups=mesh['fsdp'=8,'ctx'=4] {'ctx'}, dimensions={2} | all-to-all | bytes 3145728 | tf_op jit(solution)/shard_map/all_to_all | solution.py:122
  1279.9 6.5 fusion.209
  1288.0 7.5 fusion.83
  1298.5 4.3 all-to-all-start.3
  1305.9 26.4 %all-to-all-done.3 = f32[4,48,1612]{2,1,0:T(8,128)} async-done(((f32[4,48,1612]{2,1,0:T(8,128)}), f32[4,48,1612]{2,1,0:T(8,128)}, u32[]{:S(2)}, u32[]{:S(2)}) %all-to-all-start.3) | async-done | bytes 1238048 | tf_op jit(solution)/shard_map/all_to_all | solution.py:132
  1332.3 4.3 all-to-all-start.1
  1336.7 12.8 multiply_reduce_fusion.23
  1349.6 43.2 %all-reduce.28 = (f32[2,1536]{1,0:T(2,128)}, f32[2,3328]{1,0:T(2,128)}, f32[2,48]{1,0:T(2,128)}, f32[2,48]{1,0:T(2,128)}, f32[2,48]{1,0:T(2,128)}, /*index=5*/f32[2,3072]{1,0:T(2,128)}) all-reduce(f32[2,1536]{1,0:T(2,128)S(1)} %pad_maximum_fusion.5, ...), channel_id=1, replica_groups=mesh['fsdp'=8,'ctx'=4] {'fsdp','ctx'}, use_global_device_ids=true, to_apply=%region_46.48 | all-reduce | flops 16160 | bytes 129280 | tf_op jit(solution)/shard_map/psum | solution.py:263
  1407.5 106.1 %all-reduce.31.cloned.1.call-done = f32[2,4,3328]{2,1,0:T(4,128)} async-done(((f32[2,4,3328]{2,1,0:T(4,128)}), f32[2,4,3328]{2,1,0:T(4,128)}) %all-reduce.31.cloned.1.call-update) | async-done | bytes 106512 | tf_op jit(solution)/shard_map/psum | solution.py:263
  (684 shorter events, 239.2 us)
Async XLA Ops:
  7.2 111.6 %all-gather.21.cloned.1.call-start = ((), (), s32[]{:S(2)}) async-start(), calls=%async_computation.19 | async-start | bytes 22560768 | tf_op jit(solution)/shard_map/all_gather | solution.py:155
  12.3 273.5 %all-gather.23.cloned.1.call-start = ((), (), s32[]{:S(2)}) async-start(), calls=%async_computation.20 | async-start | bytes 10616832 | tf_op jit(solution)/shard_map/all_gather | solution.py:156
  15.6 277.6 %all-gather.25.cloned.1.call-start = ((), (), s32[]{:S(2)}) async-start(), calls=%async_computation.21 | async-start | bytes 22560768 | tf_op jit(solution)/shard_map/all_gather | solution.py:155
  16.3 521.4 %all-gather.27.cloned.1.call-start = ((), (), s32[]{:S(2)}) async-start(), calls=%async_computation.22 | async-start | bytes 10616832 | tf_op jit(solution)/shard_map/all_gather | solution.py:156
  16.9 975.2 %all-gather.15.cloned.1.call-start = ((), (), s32[]{:S(2)}) async-start(), calls=%async_computation.12 | async-start | bytes 3932160 | tf_op jit(solution)/shard_map/all_gather | solution.py:115
  19.6 113.6 %copy-start.64 = (bf16[256,1536]{1,0:T(8,128)(2,1)}, bf16[256,1536]{1,0:T(8,128)(2,1)S(1)}, u32[]{:S(2)}) copy-start(bf16[256,1536]{1,0:T(8,128)(2,1)S(1)} %multiply_convert_fusion.3) | copy-start | bytes 2359300
  20.2 113.8 %copy-start.189 = (f32[48]{0:T(128)}, f32[48]{0:T(128)S(1)}, u32[]{:S(2)}) copy-start(f32[48]{0:T(128)S(1)} %get-tuple-element.254) | copy-start | bytes 580
  20.2 123.3 %copy-start.154 = (f32[48]{0:T(128)}, f32[48]{0:T(128)S(1)}, u32[]{:S(2)}) copy-start(f32[48]{0:T(128)S(1)} %get-tuple-element.225) | copy-start | bytes 580
  137.6 8.4 collective-permute-start
  154.7 120.4 %copy-start.9 = (f32[256,3328]{0,1:T(8,128)}, f32[256,3328]{0,1:T(8,128)S(1)}, u32[]{:S(2)}) copy-start(f32[256,3328]{0,1:T(8,128)S(1)} %get-tuple-element.193) | copy-start | bytes 10223620
  157.1 40.1 %copy-start.161 = (f32[48]{0:T(128)S(1)}, f32[48]{0:T(128)}, u32[]{:S(2)}) copy-start(f32[48]{0:T(128)} %copy-done.160) | copy-start | bytes 580
  159.9 44.9 %copy-start.198 = (f32[2,48]{1,0:T(2,128)S(1)}, f32[2,48]{1,0:T(2,128)}, u32[]{:S(2)}) copy-start(f32[2,48]{1,0:T(2,128)} %param.20) | copy-start | bytes 1156
  159.9 45.5 %copy-start.153 = (f32[2,3072]{1,0:T(2,128)S(1)}, f32[2,3072]{1,0:T(2,128)}, u32[]{:S(2)}) copy-start(f32[2,3072]{1,0:T(2,128)} %param.21) | copy-start | bytes 73732
  159.9 46.7 %copy-start.176 = (f32[48,2]{0,1:T(2,128)S(1)}, f32[48,2]{0,1:T(2,128)}, u32[]{:S(2)}) copy-start(f32[48,2]{0,1:T(2,128)} %copy-done.175) | copy-start | bytes 1156
  160.0 37.3 %collective-permute-start.1 = (f32[48,64,128]{2,1,0:T(8,128)S(1)}, f32[48,64,128]{2,1,0:T(8,128)S(1)}, u32[]{:S(2)}, u32[]{:S(2)}) collective-permute-start(f32[48,64,128]{2,1,0:T(8,128)S(1)} %get-tuple-element.230), channel_id=1, source_target_pairs={{0,1},{1,2},{2,3},{4,5},{5,6},{6,7},{8,9},{9,10},{10,11},{12,13},{... | collective-permute-start | bytes 4718600 | tf_op jit(solution)/shard_map/ppermute | solution.py:23
  198.6 37.7 %collective-permute-start.2 = (f32[48,64,128]{2,1,0:T(8,128)}, f32[48,64,128]{2,1,0:T(8,128)}, u32[]{:S(2)}, u32[]{:S(2)}) collective-permute-start(f32[48,64,128]{2,1,0:T(8,128)} %multiply_add_fusion.9), channel_id=1, source_target_pairs={{0,1},{1,2},{2,3},{4,5},{5,6},{6,7},{8,9},{9,10},{10,11},{12,13},{... | collective-permute-start | bytes 4718600 | tf_op jit(solution)/shard_map/ppermute | solution.py:23
  212.3 62.8 %copy-start.83 = (f32[256,48]{0,1:T(8,128)}, f32[256,48]{0,1:T(8,128)S(1)}, u32[]{:S(2)}) copy-start(f32[256,48]{0,1:T(8,128)S(1)} %fusion.184) | copy-start | bytes 147460
  238.6 36.6 %collective-permute-start.3 = (f32[48,64,128]{2,1,0:T(8,128)S(1)}, f32[48,64,128]{2,1,0:T(8,128)S(1)}, u32[]{:S(2)}, u32[]{:S(2)}) collective-permute-start(f32[48,64,128]{2,1,0:T(8,128)S(1)} %multiply_add_fusion.8), channel_id=1, source_target_pairs={{0,1},{1,2},{2,3},{4,5},{5,6},{6,7},{8,9},{9,10},{10,11},{12,13},{... | collective-permute-start | bytes 4718600 | tf_op jit(solution)/shard_map/ppermute | solution.py:23
  313.6 9.7 collective-permute-start.4
  323.2 856.3 %all-gather.13.cloned.1.call-start = ((), (), s32[]{:S(2)}) async-start(), calls=%async_computation.10 | async-start | bytes 3932160 | tf_op jit(solution)/shard_map/all_gather | solution.py:115
  332.2 197.0 %copy-start.7 = (f32[256,3328]{0,1:T(8,128)}, f32[256,3328]{0,1:T(8,128)S(1)}, u32[]{:S(2)}) copy-start(f32[256,3328]{0,1:T(8,128)S(1)} %get-tuple-element.187) | copy-start | bytes 10223620
  334.6 56.5 %copy-start.164 = (f32[48]{0:T(128)S(1)}, f32[48]{0:T(128)}, u32[]{:S(2)}) copy-start(f32[48]{0:T(128)} %copy-done.163) | copy-start | bytes 580
  337.4 53.8 %copy-start.32 = (f32[48,64,128]{2,1,0:T(8,128)}, f32[48,64,128]{2,1,0:T(8,128)S(1)}, u32[]{:S(2)}) copy-start(f32[48,64,128]{2,1,0:T(8,128)S(1)} %get-tuple-element.239) | copy-start | bytes 4718596
  337.4 53.7 %collective-permute-start.5 = (f32[48,64,128]{2,1,0:T(8,128)S(1)}, f32[48,64,128]{2,1,0:T(8,128)S(1)}, u32[]{:S(2)}, u32[]{:S(2)}) collective-permute-start(f32[48,64,128]{2,1,0:T(8,128)S(1)} %get-tuple-element.238), channel_id=1, source_target_pairs={{0,1},{1,2},{2,3},{4,5},{5,6},{6,7},{8,9},{9,10},{10,11},{12,13},{... | collective-permute-start | bytes 4718600 | tf_op jit(solution)/shard_map/ppermute | solution.py:23
  392.5 64.0 %collective-permute-start.6 = (f32[48,64,128]{2,1,0:T(8,128)}, f32[48,64,128]{2,1,0:T(8,128)}, u32[]{:S(2)}, u32[]{:S(2)}) collective-permute-start(f32[48,64,128]{2,1,0:T(8,128)} %multiply_add_fusion.7), channel_id=1, source_target_pairs={{0,1},{1,2},{2,3},{4,5},{5,6},{6,7},{8,9},{9,10},{10,11},{12,13},{... | collective-permute-start | bytes 4718600 | tf_op jit(solution)/shard_map/ppermute | solution.py:23
  412.4 819.2 %all-gather.19.cloned.1.call-start = ((), (), s32[]{:S(2)}) async-start(), calls=%async_computation.16 | async-start | bytes 3932160 | tf_op jit(solution)/shard_map/all_gather | solution.py:116
  423.3 105.8 %copy-start.85 = (f32[256,48]{0,1:T(8,128)}, f32[256,48]{0,1:T(8,128)S(1)}, u32[]{:S(2)}) copy-start(f32[256,48]{0,1:T(8,128)S(1)} %fusion.185) | copy-start | bytes 147460
  424.1 42.4 %copy-start.147 = (f32[48,256]{1,0:T(8,128)}, f32[48,256]{1,0:T(8,128)S(1)}, u32[]{:S(2)}) copy-start(f32[48,256]{1,0:T(8,128)S(1)} %bitcast_add_fusion.18) | copy-start | bytes 147460
  424.1 42.4 %copy-start.49 = (f32[256,3072]{0,1:T(8,128)S(1)}, f32[256,3072]{0,1:T(8,128)}, u32[]{:S(2)}) copy-start(f32[256,3072]{0,1:T(8,128)} %get-tuple-element.205) | copy-start | bytes 9437188
  424.2 42.4 %copy-start.98 = (f32[256,48]{0,1:T(8,128)S(1)}, f32[256,48]{0,1:T(8,128)}, u32[]{:S(2)}) copy-start(f32[256,48]{0,1:T(8,128)} %copy.422) | copy-start | bytes 147460
  424.2 42.4 %copy-start.135 = (pred[256,256]{1,0:T(8,128)(4,1)S(1)}, pred[256,256]{1,0:T(8,128)(4,1)}, u32[]{:S(2)}) copy-start(pred[256,256]{1,0:T(8,128)(4,1)} %iota_compare_fusion) | copy-start | bytes 196612
  424.2 42.4 %copy-start.145 = (f32[48,256]{1,0:T(8,128)S(1)}, f32[48,256]{1,0:T(8,128)}, u32[]{:S(2)}) copy-start(f32[48,256]{1,0:T(8,128)} %copy.419) | copy-start | bytes 147460
  424.2 42.4 %copy-start.202 = (f32[48]{0:T(128)S(1)}, f32[48]{0:T(128)}, u32[]{:S(2)}) copy-start(f32[48]{0:T(128)} %get-tuple-element.222) | copy-start | bytes 580
  458.8 70.3 %collective-permute-start.7 = (f32[48,64,128]{2,1,0:T(8,128)S(1)}, f32[48,64,128]{2,1,0:T(8,128)S(1)}, u32[]{:S(2)}, u32[]{:S(2)}) collective-permute-start(f32[48,64,128]{2,1,0:T(8,128)S(1)} %multiply_add_fusion.6), channel_id=1, source_target_pairs={{0,1},{1,2},{2,3},{4,5},{5,6},{6,7},{8,9},{9,10},{10,11},{12,13},{... | collective-permute-start | bytes 4718600 | tf_op jit(solution)/shard_map/ppermute | solution.py:23
  481.5 52.1 %copy-start.44 = (f32[1,256,48,64]{1,3,2,0:T(8,128)}, f32[1,256,48,64]{1,3,2,0:T(8,128)S(1)}, u32[]{:S(2)}) copy-start(f32[1,256,48,64]{1,3,2,0:T(8,128)S(1)} %fusion.68) | copy-start | bytes 9437188
  553.5 101.9 %copy-start.165 = (f32[48]{0:T(128)S(1)}, f32[48]{0:T(128)}, u32[]{:S(2)}) copy-start(f32[48]{0:T(128)} %copy-done.163) | copy-start | bytes 580
  557.8 97.6 %collective-permute-start.8 = (f32[48,64,128]{2,1,0:T(8,128)}, f32[48,64,128]{2,1,0:T(8,128)}, u32[]{:S(2)}, u32[]{:S(2)}) collective-permute-start(f32[48,64,128]{2,1,0:T(8,128)} %get-tuple-element.243), channel_id=1, source_target_pairs={{1,0},{2,1},{3,2},{5,4},{6,5},{7,6},{9,8},{10,9},{11,10},{13,12},{... | collective-permute-start | bytes 4718600 | tf_op jit(solution)/shard_map/ppermute | solution.py:23
  559.1 99.7 %copy-start.50 = (f32[256,3072]{0,1:T(8,128)S(1)}, f32[256,3072]{0,1:T(8,128)}, u32[]{:S(2)}) copy-start(f32[256,3072]{0,1:T(8,128)} %get-tuple-element.205) | copy-start | bytes 9437188
  657.6 34.9 %collective-permute-start.9 = (f32[48,64,128]{2,1,0:T(8,128)S(1)}, f32[48,64,128]{2,1,0:T(8,128)S(1)}, u32[]{:S(2)}, u32[]{:S(2)}) collective-permute-start(f32[48,64,128]{2,1,0:T(8,128)S(1)} %multiply_add_fusion.5), channel_id=1, source_target_pairs={{1,0},{2,1},{3,2},{5,4},{6,5},{7,6},{9,8},{10,9},{11,10},{13,12},{... | collective-permute-start | bytes 4718600 | tf_op jit(solution)/shard_map/ppermute | solution.py:23
  693.9 35.9 %collective-permute-start.10 = (f32[48,64,128]{2,1,0:T(8,128)}, f32[48,64,128]{2,1,0:T(8,128)}, u32[]{:S(2)}, u32[]{:S(2)}) collective-permute-start(f32[48,64,128]{2,1,0:T(8,128)} %multiply_add_fusion.4), channel_id=1, source_target_pairs={{1,0},{2,1},{3,2},{5,4},{6,5},{7,6},{9,8},{10,9},{11,10},{13,12},{... | collective-permute-start | bytes 4718600 | tf_op jit(solution)/shard_map/ppermute | solution.py:23
  770.3 7.4 collective-permute-start.11
  785.9 201.4 %all-to-all-start.2 = ((bf16[256,1,4,1612]{0,3,1,2:T(8,128)(2,1)}), bf16[256,1,4,1612]{0,3,1,2:T(8,128)(2,1)}, u32[]{:S(2)}, u32[]{:S(2)}) async-start(bf16[256,1,4,1612]{0,3,1,2:T(8,128)(2,1)} %bitcast.663), calls=%async_computation.3 | async-start | bytes 6619136 | tf_op jit(solution)/shard_map/all_to_all | solution.py:121
  792.6 487.3 %all-gather.17.cloned.1.call-start = ((), (), s32[]{:S(2)}) async-start(), calls=%async_computation.14 | async-start | bytes 3932160 | tf_op jit(solution)/shard_map/all_gather | solution.py:116
  826.2 101.9 %collective-permute-start.12 = (f32[48,64,128]{2,1,0:T(8,128)}, f32[48,64,128]{2,1,0:T(8,128)}, u32[]{:S(2)}, u32[]{:S(2)}) collective-permute-start(f32[48,64,128]{2,1,0:T(8,128)} %get-tuple-element.249), channel_id=1, source_target_pairs={{1,0},{2,1},{3,2},{5,4},{6,5},{7,6},{9,8},{10,9},{11,10},{13,12},{... | collective-permute-start | bytes 4718600 | tf_op jit(solution)/shard_map/ppermute | solution.py:23
  827.6 470.9 %reduce-scatter.7.cloned.1.call-start = ((), (), s32[]{:S(2)}) async-start(), calls=%async_computation.13 | async-start | bytes 11501568 | tf_op jit(solution)/shard_map/reduce_scatter | solution.py:129
  827.6 100.5 %copy-start.31 = (f32[48,64,128]{2,1,0:T(8,128)S(1)}, f32[48,64,128]{2,1,0:T(8,128)}, u32[]{:S(2)}) copy-start(f32[48,64,128]{2,1,0:T(8,128)} %get-tuple-element.250) | copy-start | bytes 4718596
  827.6 100.5 %copy-start.162 = (f32[48]{0:T(128)S(1)}, f32[48]{0:T(128)}, u32[]{:S(2)}) copy-start(f32[48]{0:T(128)} %copy-done.160) | copy-start | bytes 580
  850.4 80.7 %copy-start.69 = (f32[256,256]{1,0:T(8,128)}, f32[256,256]{1,0:T(8,128)S(1)}, u32[]{:S(2)}) copy-start(f32[256,256]{1,0:T(8,128)S(1)} %get-tuple-element.119) | copy-start | bytes 786436
  850.5 82.0 %copy-start.5 = (f32[256,3072]{0,1:T(8,128)S(1)}, f32[256,3072]{0,1:T(8,128)}, u32[]{:S(2)}) copy-start(f32[256,3072]{0,1:T(8,128)} %copy-done.4) | copy-start | bytes 9437188
  850.5 82.0 %copy-start.95 = (f32[256,48]{0,1:T(8,128)S(1)}, f32[256,48]{0,1:T(8,128)}, u32[]{:S(2)}) copy-start(f32[256,48]{0,1:T(8,128)} %copy-done.94) | copy-start | bytes 147460
  929.8 54.8 %collective-permute-start.13 = (f32[48,64,128]{2,1,0:T(8,128)S(1)}, f32[48,64,128]{2,1,0:T(8,128)S(1)}, u32[]{:S(2)}, u32[]{:S(2)}) collective-permute-start(f32[48,64,128]{2,1,0:T(8,128)S(1)} %multiply_add_fusion.3), channel_id=1, source_target_pairs={{1,0},{2,1},{3,2},{5,4},{6,5},{7,6},{9,8},{10,9},{11,10},{13,12},{... | collective-permute-start | bytes 4718600 | tf_op jit(solution)/shard_map/ppermute | solution.py:23
  986.0 37.0 %collective-permute-start.14 = (f32[48,64,128]{2,1,0:T(8,128)}, f32[48,64,128]{2,1,0:T(8,128)}, u32[]{:S(2)}, u32[]{:S(2)}) collective-permute-start(f32[48,64,128]{2,1,0:T(8,128)} %multiply_add_fusion.2), channel_id=1, source_target_pairs={{1,0},{2,1},{3,2},{5,4},{6,5},{7,6},{9,8},{10,9},{11,10},{13,12},{... | collective-permute-start | bytes 4718600 | tf_op jit(solution)/shard_map/ppermute | solution.py:23
  1002.0 330.3 %reduce-scatter.5.cloned.1.call-start = ((), (), s32[]{:S(2)}) async-start(), calls=%async_computation.11 | async-start | bytes 11501568 | tf_op jit(solution)/shard_map/reduce_scatter | solution.py:129
  1077.3 12.6 collective-permute-start.15
  1190.3 205.9 %reduce-scatter.11.cloned.1.call-start = ((), (), s32[]{:S(2)}) async-start(), calls=%async_computation.17 | async-start | bytes 5308416 | tf_op jit(solution)/shard_map/reduce_scatter | solution.py:130
  1237.7 158.5 %reduce-scatter.9.cloned.1.call-start = ((), (), s32[]{:S(2)}) async-start(), calls=%async_computation.15 | async-start | bytes 5308416 | tf_op jit(solution)/shard_map/reduce_scatter | solution.py:130
  1295.5 41.2 %copy-start.27 = (f32[256,1536]{1,0:T(8,128)S(1)}, f32[256,1536]{1,0:T(8,128)}, u32[]{:S(2)}) copy-start(f32[256,1536]{1,0:T(8,128)} %param.12) | copy-start | bytes 4718596
  1295.5 41.2 %copy-start.53 = (bf16[256,3328]{0,1:T(8,128)(2,1)S(1)}, bf16[256,3328]{0,1:T(8,128)(2,1)}, u32[]{:S(2)}) copy-start(bf16[256,3328]{0,1:T(8,128)(2,1)} %copy-done.52) | copy-start | bytes 5111812
  1295.5 41.2 %copy-start.122 = (f32[1536]{0:T(1024)S(1)}, f32[1536]{0:T(1024)}, u32[]{:S(2)}) copy-start(f32[1536]{0:T(1024)} %copy-done.121) | copy-start | bytes 18436
  1295.5 41.2 %copy-start.170 = (f32[256]{0:T(256)S(1)}, f32[256]{0:T(256)}, u32[]{:S(2)}) copy-start(f32[256]{0:T(256)} %copy-done.169) | copy-start | bytes 3076
  1298.5 33.9 %all-to-all-start.3 = ((f32[4,48,1612]{2,1,0:T(8,128)}), f32[4,48,1612]{2,1,0:T(8,128)}, u32[]{:S(2)}, u32[]{:S(2)}) async-start(f32[4,48,1612]{2,1,0:T(8,128)} %bitcast.685), calls=%async_computation.5 | async-start | bytes 2555904 | tf_op jit(solution)/shard_map/all_to_all | solution.py:132
  1302.8 210.8 %all-reduce.31.cloned.1.call-start = ((), (), s32[]{:S(2)}) async-start(), calls=%async_computation.18 | async-start | bytes 212992 | tf_op jit(solution)/shard_map/psum | solution.py:263
  1332.3 68.7 %all-to-all-start.1 = ((f32[4,48,1612]{2,1,0:T(8,128)}), f32[4,48,1612]{2,1,0:T(8,128)}, u32[]{:S(2)}, u32[]{:S(2)}) async-start(f32[4,48,1612]{2,1,0:T(8,128)} %bitcast.686), calls=%async_computation.2 | async-start | bytes 2555904 | tf_op jit(solution)/shard_map/all_to_all | solution.py:132
  1336.7 56.1 %copy-start.184 = (f32[256]{0:T(256)S(1)}, f32[256]{0:T(256)}, u32[]{:S(2)}) copy-start(f32[256]{0:T(256)} %copy-done.183) | copy-start | bytes 3076
  (178 other events, 1410.0 us)
Sparse Core Ops, SparseCore 0:
  12.4 106.2 all-gather.20
  120.7 58.6 all-gather.22
  181.8 103.5 all-gather.24
  287.8 58.7 all-gather.26
  348.0 98.4 all-gather.14
  447.9 94.1 all-gather.12
  559.3 101.1 all-gather.18
  827.7 100.7 all-gather.16
  1002.1 81.5 reduce-scatter.6
  1190.4 79.2 reduce-scatter.4
  1273.2 53.7 reduce-scatter.10
  1330.2 54.5 reduce-scatter.8
  1391.0 122.6 all-reduce.30
where the time goes:
time: 1530 us; the launch traced here: 1520 us
  waiting for transfers between devices  683 us (45%)
  matrix products  285 us (19%)
  blocking collectives  197 us (13%)
  other arithmetic  168 us (11%)
  local copies, waits for them, and re-layouts  96.6 us (6%)
  starting transfers between devices  76.3 us (5%)
  between operations  17.2 us (1%)
    ppermute x16, waiting for transfers between devices, passed_along(): lax.ppermute(value, axis, [(source, source + steps) for source in range(i...  450 us
    psum x1, waiting for transfers between devices, local(): lax.psum((stacked[2], stacked[3], stacked[4], stacked[5], stacked[6], sta...  106 us
    dot_general x6, matrix products, block_scan(): intra_out = jnp.einsum('bhls,bshp->blhp', mixing, x_blocks, precision=HIGH)  101 us
    all_gather x2, waiting for transfers between devices, local(): lax.all_gather(in_weight[layer_index], 'fsdp', axis=0, tiled=True)  98.6 us
    all_to_all x2, blocking collectives, weight_gradients(): lax.all_to_all(gate_split, 'ctx', split_axis=2, concat_axis=0, tiled=True)  77.2 us
    all_to_all x1, blocking collectives, weight_gradients(): lax.all_to_all(proj_split, 'ctx', split_axis=2, concat_axis=0, tiled=True)  77 us
    ppermute x16, starting transfers between devices, passed_along(): lax.ppermute(value, axis, [(source, source + steps) for source in range(i...  60.4 us
    psum x1, blocking collectives, local(): lax.psum((stacked[2], stacked[3], stacked[4], stacked[5], stacked[6], sta...  43.2 us
  transfers between devices with their start and end apart: 32, of which 15 were waited for; matrix products, arithmetic and copies ran while one was open for 34% of the time, Pallas kernels for 0%

commit v1 on v0

v1 whole, which is shorter than its diff:
```python
import functools

import jax
import jax.numpy as jnp
from jax import lax
from jax.experimental import pallas as pl
from jax.experimental.pallas import tpu as pltpu
from jax.sharding import PartitionSpec as P

H = 48
P_SIZE = 64
N = 128
CONV = 4
LAYERS = 2
DI = 3072
CC = 3328
W = 256
G = DI // W
K = W // P_SIZE

EPS = 1e-05
HIGH = lax.Precision.HIGHEST
F32 = jnp.float32
BF = jnp.bfloat16


def mm(a, b):
    return lax.dot_general(a.astype(BF), b.astype(BF), (((1,), (0,)), ((), ())), preferred_element_type=F32)


def mm_nt(a, b):
    return lax.dot_general(a.astype(BF), b.astype(BF), (((1,), (1,)), ((), ())), preferred_element_type=F32)


def mm_tn(a, b):
    return lax.dot_general(a.astype(BF), b.astype(BF), (((0,), (0,)), ((), ())), preferred_element_type=F32)


def extend(halo_ref, conv_ref):
    return jnp.concatenate([halo_ref[...], conv_ref[...].astype(F32)], 0)


def conv_pre(ext, taps_ref, bias_ref, rows):
    acc = bias_ref[...] + ext[5 : 5 + rows] * taps_ref[0:1, :]
    for j in range(1, CONV):
        acc = acc + ext[5 + j : 5 + j + rows] * taps_ref[j : j + 1, :]
    return acc


def sigmoid(v):
    return 1.0 / (1.0 + jnp.exp(-v))


def pair_cols(col, first, low):
    return jnp.where(low, col[:, first : first + 1], col[:, first + 1 : first + 2])


def masked_scores(c_rows, b_rows):
    s = mm_nt(c_rows, b_rows)
    r = lax.broadcasted_iota(jnp.int32, s.shape, 0)
    q = lax.broadcasted_iota(jnp.int32, s.shape, 1)
    return jnp.where(r >= q, s, 0.0)


def scan_fwd_kernel(conv_ref, conv_bc_ref, halo_ref, halo_bc_ref, taps_ref, taps_bc_ref, bias_ref, bias_bc_ref,
                    col_ref, row_ref, skip_ref, y_ref, state_ref, bc_ref, s_ref):
    rows = conv_ref.shape[0]

    @pl.when(pl.program_id(0) == 0)
    def _():
        pre = conv_pre(extend(halo_bc_ref, conv_bc_ref), taps_bc_ref, bias_bc_ref, rows)
        bc = pre * sigmoid(pre)
        bc_ref[...] = bc
        s_ref[...] = masked_scores(bc[:, N:], bc[:, :N])

    pre = conv_pre(extend(halo_ref, conv_ref), taps_ref, bias_ref, rows)
    x = pre * sigmoid(pre)
    low = lax.broadcasted_iota(jnp.int32, (rows, 2 * P_SIZE), 1) < P_SIZE
    col = col_ref[0]
    row = row_ref[0]
    b_bf = bc_ref[:, :N].astype(BF)
    for pair in range(K // 2):
        h0 = 2 * pair
        cols = slice(pair * 128, pair * 128 + 128)
        x2 = x[:, cols]
        xs = x2 * pair_cols(col, K + h0, low)
        mixes, parts = [], []
        for i in range(2):
            h = h0 + i
            decay = jnp.exp(jnp.minimum(col[:, h : h + 1] - row[h : h + 1, :], 0.0))
            mixes.append((s_ref[...] * decay).astype(BF))
            parts.append(jnp.where(low if i == 0 else ~low, xs, 0.0).astype(BF))
        y = mm(jnp.concatenate(mixes, 1), jnp.concatenate(parts, 0))
        y_ref[:, cols] = y + skip_ref[:, cols] * x2
        last = jnp.where(low[:1], row[h0 : h0 + 1, rows - 1 : rows], row[h0 + 1 : h0 + 2, rows - 1 : rows])
        tail = jnp.exp(last - pair_cols(col, h0, low))
        state_ref[cols, :] = mm_tn(xs * tail, b_bf)


def gate_fwd_kernel(y_ref, gate_ref, in_ref, bc_ref, col_ref, gain_ref, ssm_ref, gn_ref, gated_ref, acc_ref):
    g = pl.program_id(0)
    rows = y_ref.shape[0]

    @pl.when(g == 0)
    def _():
        acc_ref[...] = jnp.zeros_like(acc_ref)

    low = lax.broadcasted_iota(jnp.int32, (rows, 2 * P_SIZE), 1) < P_SIZE
    col = col_ref[0]
    z = mm_nt(bc_ref[:, N:], in_ref[...])
    e = jnp.concatenate([jnp.exp(pair_cols(col, 2 * p, low)) for p in range(K // 2)], 1)
    ssm = y_ref[...] + e * z
    ssm_ref[...] = ssm
    gate = gate_ref[...]
    gated = ssm * (gate * sigmoid(gate))
    gated_ref[g] = gated
    acc_ref[...] += gated * gated

    @pl.when(g == G - 1)
    def _():
        r = lax.rsqrt(jnp.sum(acc_ref[...], 1, keepdims=True) / DI + EPS)
        for i in range(G):
            cols = slice(i * W, i * W + W)
            gn_ref[:, cols] = (gated_ref[i] * r * gain_ref[:, cols]).astype(BF)


def gate_bwd_kernel(ssm_ref, gate_ref, dn_ref, gain_ref, col_ref, bc_ref, dssm_ref, dgate_ref, ggain_ref, lg_ref,
                    sq_ref, dot_ref, r_ref, k_ref):
    phase = pl.program_id(0)
    g = pl.program_id(1)
    rows = ssm_ref.shape[0]
    ssm = ssm_ref[...]
    gate = gate_ref[...]
    sig = sigmoid(gate)
    act = gate * sig
    gated = ssm * act
    dn = dn_ref[...]
    dng = dn * gain_ref[...]

    @pl.when((phase == 0) & (g == 0))
    def _():
        sq_ref[...] = jnp.zeros_like(sq_ref)
        dot_ref[...] = jnp.zeros_like(dot_ref)

    @pl.when(phase == 0)
    def _():
        sq_ref[...] += gated * gated
        dot_ref[...] += dng * gated

    @pl.when((phase == 1) & (g == 0))
    def _():
        r = lax.rsqrt(jnp.sum(sq_ref[...], 1, keepdims=True) / DI + EPS)
        r_ref[...] = r
        k_ref[...] = r * r * r * jnp.sum(dot_ref[...], 1, keepdims=True) / DI

    @pl.when(phase == 1)
    def _():
        r = r_ref[...]
        dgated = r * dng - gated * k_ref[...]
        dssm = dgated * act
        dssm_ref[...] = dssm
        dgate_ref[...] = (dgated * ssm * (sig * (1.0 + gate * (1.0 - sig)))).astype(BF)
        ggain_ref[...] = jnp.sum(dn * (gated * r), 0, keepdims=True)
        low = lax.broadcasted_iota(jnp.int32, (rows, 2 * P_SIZE), 1) < P_SIZE
        col = col_ref[0]
        e = jnp.concatenate([jnp.exp(pair_cols(col, 2 * p, low)) for p in range(K // 2)], 1)
        lg_ref[...] = mm_tn(dssm * e, bc_ref[:, N:])


def conv_back(d_act, pre, sig, ext, taps_ref, rows):
    d_pre = d_act * (sig * (1.0 + pre * (1.0 - sig)))
    zero = jnp.zeros((8, d_pre.shape[1]), F32)
    below = jnp.concatenate([d_pre, zero], 0)
    above = jnp.concatenate([zero, d_pre[:8]], 0)
    d_conv = below[3 : 3 + rows] * taps_ref[0:1, :]
    edge = above[8:16] * taps_ref[0:1, :]
    terms = [jnp.sum(d_pre * ext[5 : 5 + rows], 0, keepdims=True)]
    for j in range(1, CONV):
        d_conv = d_conv + below[3 - j : 3 - j + rows] * taps_ref[j : j + 1, :]
        edge = edge + above[8 - j : 16 - j] * taps_ref[j : j + 1, :]
        terms.append(jnp.sum(d_pre * ext[5 + j : 5 + j + rows], 0, keepdims=True))
    terms.append(jnp.sum(d_pre, 0, keepdims=True))
    return d_conv, edge, terms


def scan_bwd_kernel(conv_ref, conv_bc_ref, halo_ref, halo_bc_ref, taps_ref, taps_bc_ref, bias_ref, bias_bc_ref,
                    col_ref, row_ref, skip_ref, bc_ref, dy_ref, in_ref, out_ref,
                    dconv_ref, edge_ref, gt_ref, dconv_bc_ref, edge_bc_ref, gt_bc_ref, colo_ref, rowo_ref, misc_ref,
                    s_ref, ds_ref, dbc_ref):
    g = pl.program_id(0)
    rows = conv_ref.shape[0]

    @pl.when(g == 0)
    def _():
        s_ref[...] = masked_scores(bc_ref[:, N:], bc_ref[:, :N])
        ds_ref[...] = jnp.zeros_like(ds_ref)
        dbc_ref[...] = jnp.zeros_like(dbc_ref)

    ext = extend(halo_ref, conv_ref)
    pre = conv_pre(ext, taps_ref, bias_ref, rows)
    sig = sigmoid(pre)
    x = pre * sig
    low = lax.broadcasted_iota(jnp.int32, (rows, 2 * P_SIZE), 1) < P_SIZE
    lane = lax.broadcasted_iota(jnp.int32, (rows, 2 * K), 1)
    col = col_ref[0]
    row = row_ref[0]
    b_bf = bc_ref[:, :N].astype(BF)
    c_bf = bc_ref[:, N:].astype(BF)
    colo = jnp.zeros((rows, 2 * K), F32)
    dxs = []
    misc_ref[...] = jnp.zeros_like(misc_ref)
    rowo_ref[...] = jnp.zeros_like(rowo_ref)
    for pair in range(K // 2):
        h0 = 2 * pair
        cols = slice(pair * 128, pair * 128 + 128)
        x2 = x[:, cols]
        step = pair_cols(col, K + h0, low)
        xs = x2 * step
        xs_bf = xs.astype(BF)
        dy = dy_ref[:, cols]
        h_in = in_ref[cols, :]
        h_out = out_ref[cols, :]
        cum = pair_cols(col, h0, low)
        e = jnp.exp(cum)
        last = jnp.where(low[:1], row[h0 : h0 + 1, rows - 1 : rows], row[h0 + 1 : h0 + 2, rows - 1 : rows])
        tail = jnp.exp(last - cum)
        edy = e * dy
        txs = tail * xs
        inter = edy * mm_nt(c_bf, h_in)
        u = mm_nt(b_bf, h_out)
        r = txs * u
        dbc_ref[:, N:] += mm(edy, h_in)
        dbc_ref[:, :N] += mm(txs, h_out)
        d_xs = tail * u
        side = inter - r
        for i in range(2):
            h = h0 + i
            keep = low if i == 0 else ~low
            dyh = jnp.where(keep, dy, 0.0).astype(BF)
            d_mix = mm_nt(dyh, xs_bf)
            decay = jnp.exp(jnp.minimum(col[:, h : h + 1] - row[h : h + 1, :], 0.0))
            d_ld = d_mix * decay
            ds_ref[...] += d_ld
            s = s_ref[...]
            weight = d_ld * s
            d_xs = d_xs + mm_tn(s * decay, dyh)
            rowo_ref[0, h : h + 1, :] = jnp.sum(weight, 0, keepdims=True)
            folded = weight[:, :128] + weight[:, 128:] + jnp.where(keep, side, 0.0)
            colo = jnp.where(lane == h, jnp.sum(folded, 1, keepdims=True), colo)
        prod = x2 * d_xs
        for i in range(2):
            keep = low if i == 0 else ~low
            s_sum = jnp.sum(jnp.where(keep, prod, 0.0), 1, keepdims=True)
            colo = jnp.where(lane == K + h0 + i, s_sum, colo)
        dxs.append(step * d_xs + skip_ref[:, cols] * dy)
        hg = h_in.astype(F32) * h_out.astype(F32)
        misc_ref[0, 0:1, cols] = jnp.sum(dy * x2, 0, keepdims=True)
        misc_ref[0, 1:2, cols] = jnp.sum(r, 0, keepdims=True)
        misc_ref[0, 2:3, cols] = jnp.sum(hg[:P_SIZE], 0, keepdims=True)
        misc_ref[0, 3:4, cols] = jnp.sum(hg[P_SIZE:], 0, keepdims=True)
    colo_ref[0] = colo
    d_conv, edge, terms = conv_back(jnp.concatenate(dxs, 1), pre, sig, ext, taps_ref, rows)
    dconv_ref[...] = d_conv
    edge_ref[...] = edge
    gt_ref[...] = jnp.zeros_like(gt_ref)
    for j, term in enumerate(terms):
        gt_ref[j : j + 1, :] = term

    @pl.when(g == G - 1)
    def _():
        r_i = lax.broadcasted_iota(jnp.int32, ds_ref.shape, 0)
        q_i = lax.broadcasted_iota(jnp.int32, ds_ref.shape, 1)
        ds = jnp.where(r_i >= q_i, ds_ref[...], 0.0).astype(BF)
        d_c = dbc_ref[:, N:] + mm(ds, b_bf)
        d_b = dbc_ref[:, :N] + mm_tn(ds, c_bf)
        ext2 = extend(halo_bc_ref, conv_bc_ref)
        pre2 = conv_pre(ext2, taps_bc_ref, bias_bc_ref, rows)
        d_conv2, edge2, terms2 = conv_back(
            jnp.concatenate([d_b, d_c], 1), pre2, sigmoid(pre2), ext2, taps_bc_ref, rows)
        dconv_bc_ref[...] = d_conv2
        edge_bc_ref[...] = edge2
        gt_bc_ref[...] = jnp.zeros_like(gt_bc_ref)
        for j, term in enumerate(terms2):
            gt_bc_ref[j : j + 1, :] = term


def col_block(rows):
    return pl.BlockSpec((rows, W), lambda g: (0, g))


def bc_block(rows):
    return pl.BlockSpec((rows, W), lambda g: (0, G))


def fixed(shape):
    return pl.BlockSpec(shape, lambda g: (0,) * len(shape))


def packs(rows):
    return [pl.BlockSpec((1, rows, 2 * K), lambda g: (g, 0, 0)), pl.BlockSpec((1, 2 * K, rows), lambda g: (g, 0, 0))]


def conv_specs(rows):
    return [col_block(rows), bc_block(rows), col_block(8), bc_block(8), col_block(CONV), bc_block(CONV),
            col_block(1), bc_block(1)] + packs(rows) + [col_block(1)]


STATE = pl.BlockSpec((W, N), lambda g: (g, 0))


def sds(shape, dtype=F32):
    return jax.ShapeDtypeStruct(shape, dtype)


def scan_fwd(conv_in, halo, taps, bias, col, row, skip):
    rows = conv_in.shape[0]
    return pl.pallas_call(
        scan_fwd_kernel,
        grid=(G,),
        in_specs=conv_specs(rows),
        out_specs=[col_block(rows), STATE, fixed((rows, 2 * N))],
        out_shape=[sds((rows, DI)), sds((DI, N)), sds((rows, 2 * N))],
        scratch_shapes=[pltpu.VMEM((rows, rows), F32)],
        name="scan_fwd",
    )(conv_in, conv_in, halo, halo, taps, taps, bias, bias, col, row, skip)


def gate_fwd(y, gate, incoming, bc, col, gain):
    rows = y.shape[0]
    return pl.pallas_call(
        gate_fwd_kernel,
        grid=(G,),
        in_specs=[col_block(rows), col_block(rows), STATE, fixed((rows, 2 * N)), packs(rows)[0], fixed((1, DI))],
        out_specs=[col_block(rows), fixed((rows, DI))],
        out_shape=[sds((rows, DI)), sds((rows, DI), BF)],
        scratch_shapes=[pltpu.VMEM((G, rows, W), F32), pltpu.VMEM((rows, W), F32)],
        name="gate_fwd",
    )(y, gate, incoming, bc, col, gain)


def gate_bwd(ssm, gate, dn, gain, col, bc):
    rows = ssm.shape[0]
    block = pl.BlockSpec((rows, W), lambda p, g: (0, g))
    late = pl.BlockSpec((rows, W), lambda p, g: (0, p * g))
    return pl.pallas_call(
        gate_bwd_kernel,
        grid=(2, G),
        in_specs=[block, block, block, pl.BlockSpec((1, W), lambda p, g: (0, g)),
                  pl.BlockSpec((1, rows, 2 * K), lambda p, g: (g, 0, 0)),
                  pl.BlockSpec((rows, 2 * N), lambda p, g: (0, 0))],
        out_specs=[late, late, pl.BlockSpec((1, W), lambda p, g: (0, p * g)),
                   pl.BlockSpec((W, N), lambda p, g: (p * g, 0))],
        out_shape=[sds((rows, DI)), sds((rows, DI), BF), sds((1, DI)), sds((DI, N))],
        scratch_shapes=[pltpu.VMEM((rows, W), F32), pltpu.VMEM((rows, W), F32),
                        pltpu.VMEM((rows, 1), F32), pltpu.VMEM((rows, 1), F32)],
        name="gate_bwd",
    )(ssm, gate, dn, gain, col, bc)


def scan_bwd(conv_in, halo, taps, bias, col, row, skip, bc, dy, incoming, outgoing):
    rows = conv_in.shape[0]
    return pl.pallas_call(
        scan_bwd_kernel,
        grid=(G,),
        in_specs=conv_specs(rows) + [fixed((rows, 2 * N)), col_block(rows), STATE, STATE],
        out_specs=[col_block(rows), col_block(8), col_block(8), fixed((rows, W)), fixed((8, W)), fixed((8, W))]
        + packs(rows) + [pl.BlockSpec((1, 8, W), lambda g: (g, 0, 0))],
        out_shape=[sds((rows, DI)), sds((8, DI)), sds((8, DI)), sds((rows, W)), sds((8, W)), sds((8, W)),
                   sds((G, rows, 2 * K)), sds((G, 2 * K, rows)), sds((G, 8, W))],
        scratch_shapes=[pltpu.VMEM((rows, rows), F32), pltpu.VMEM((rows, rows), F32), pltpu.VMEM((rows, 2 * N), F32)],
        name="scan_bwd",
    )(conv_in, conv_in, halo, halo, taps, taps, bias, bias, col, row, skip, bc, dy, incoming, outgoing)


def passed_along(value, axis, steps):
    count = lax.axis_size(axis)
    initial, last = (max(0, -steps), min(count, count - steps))
    return lax.ppermute(value, axis, [(source, source + steps) for source in range(initial, last)])


CHUNKS = 2


def carry(totals, local_state, steps):
    hops = lax.axis_size("ctx") - 1
    size = DI // CHUNKS
    parts = []
    for chunk in range(CHUNKS):
        rows = slice(chunk * size, chunk * size + size)
        own, factor = local_state[rows], totals[rows]
        incoming = passed_along(own.astype(BF), "ctx", steps)
        for _ in range(hops - 1):
            incoming = passed_along((factor * incoming.astype(F32) + own).astype(BF), "ctx", steps)
        parts.append(incoming)
    return jnp.concatenate(parts, 0)


def all_sum(value):
    for axis in ("fsdp", "ctx"):
        count = lax.axis_size(axis)
        if count & (count - 1):
            value = lax.psum(value, axis)
            continue
        bit = 1
        while bit < count:
            value = value + lax.ppermute(value, axis, [(i, i ^ bit) for i in range(count)])
            bit *= 2
    return value


def rms_norm(values, gain_row):
    return values * lax.rsqrt(jnp.mean(values * values, axis=-1, keepdims=True) + EPS) * gain_row


def rows_product(left, right):
    return lax.dot_general(left, right, (((0,), (0,)), ((), ())), preferred_element_type=F32)


def right_transposed(left, right):
    return lax.dot_general(left, right, (((1,), (1,)), ((), ())), preferred_element_type=F32)


def weight_gradients(normed, d_proj, gnormed, grad_bf):
    tok_rows = normed.shape[0]
    fsdp_count = lax.axis_size("fsdp")
    ctx_count = lax.axis_size("ctx")
    width_in = d_proj.shape[1]
    inner = gnormed.shape[1]
    tile_rows = inner // (fsdp_count * ctx_count)
    all_rows = (
        lax.all_gather(normed, "ctx", axis=0, tiled=True),
        lax.all_gather(grad_bf, "ctx", axis=0, tiled=True),
    )
    proj_split = d_proj.reshape(tok_rows, 1, ctx_count, width_in // ctx_count)
    gate_split = gnormed.reshape(tok_rows, fsdp_count, ctx_count, tile_rows)
    cols = (
        lax.all_to_all(proj_split, "ctx", split_axis=2, concat_axis=0, tiled=True),
        lax.all_to_all(gate_split, "ctx", split_axis=2, concat_axis=0, tiled=True),
    )
    proj_cols = cols[0].reshape(ctx_count * tok_rows, width_in // ctx_count)
    gate_cols = cols[1].reshape(ctx_count * tok_rows, fsdp_count * tile_rows)
    part_in = rows_product(all_rows[0], proj_cols)
    part_out = rows_product(gate_cols, all_rows[1])
    summed = (
        lax.psum_scatter(part_in, "fsdp", scatter_dimension=0, tiled=True),
        lax.psum_scatter(part_out, "fsdp", scatter_dimension=0, tiled=True),
    )
    owned_in = lax.all_to_all(summed[0], "ctx", split_axis=0, concat_axis=1, tiled=True)
    return (owned_in, summed[1])


def grouped(cum, steps):
    rows = cum.shape[0]
    both = jnp.stack([cum.reshape(rows, G, K), steps.reshape(rows, G, K)], 2).reshape(rows, G, 2 * K)
    return jnp.transpose(both, (1, 0, 2)), jnp.transpose(both, (1, 2, 0))


def local(
    activations,
    in_weight,
    out_weight,
    norm_gain,
    conv_weight,
    conv_bias,
    step_bias,
    decay_log,
    skip_gain,
    gate_gain,
    cotangent,
):
    rows = activations.shape[0]
    edge_count = CONV - 1
    order = jnp.arange(rows)
    lower = (order[:, None] >= order[None, :]).astype(F32)
    weights = []
    for k in range(LAYERS):
        weights.append(
            (
                lax.all_gather(in_weight[k][:, DI:], "fsdp", axis=0, tiled=True),
                lax.all_gather(in_weight[k][:, :DI], "fsdp", axis=0, tiled=True),
                lax.all_gather(out_weight[k], "fsdp", axis=0, tiled=True),
            )
        )
    stream = activations
    kept = []
    for k in range(LAYERS):
        w_conv, w_gate, w_out = weights[k]
        normed = rms_norm(stream, norm_gain[k]).astype(BF)
        proj = jnp.dot(normed, w_conv, preferred_element_type=F32)
        conv_in = proj[:, :CC].astype(BF)
        raw_steps = proj[:, CC:]
        edge_in = passed_along(conv_in[rows - edge_count :], "ctx", 1)
        halo = jnp.concatenate([jnp.zeros((8 - edge_count, CC), F32), edge_in.astype(F32)], 0)
        steps = jax.nn.softplus(raw_steps + step_bias[k][None, :])
        cum = jnp.dot(lower, -steps * jnp.exp(decay_log[k])[None, :], precision=HIGH)
        col, row = grouped(cum, steps)
        totals = jnp.repeat(jnp.exp(cum[-1]), P_SIZE)[:, None]
        skip = jnp.repeat(skip_gain[k], P_SIZE)[None, :]
        bias = conv_bias[k][None, :]
        y, state, bc = scan_fwd(conv_in, halo, conv_weight[k], bias, col, row, skip)
        gate_in = jnp.dot(normed, w_gate, preferred_element_type=F32)
        incoming = carry(totals, state, 1)
        ssm, gnormed = gate_fwd(y, gate_in, incoming, bc, col, gate_gain[k][None, :])
        kept.append((stream, normed, gate_in, conv_in, halo, raw_steps, steps, col, row, totals, skip, bias, bc,
                     incoming, ssm, gnormed))
        stream = stream + jnp.dot(gnormed, w_out, preferred_element_type=F32)
    grad_stream = cotangent
    collected = []
    for k in reversed(range(LAYERS)):
        w_conv, w_gate, w_out = weights[k]
        (stream_in, normed, gate_in, conv_in, halo, raw_steps, steps, col, row, totals, skip, bias, bc,
         incoming, ssm, gnormed) = kept[k]
        grad_bf = grad_stream.astype(BF)
        d_gnormed = right_transposed(grad_bf, w_out)
        d_ssm, d_gate, g_gate, local_grad = gate_bwd(ssm, gate_in, d_gnormed, gate_gain[k][None, :], col, bc)
        outgoing = carry(totals, local_grad, -1)
        d_x, edge_x, gt_x, d_bc, edge_bc, gt_bc, colo, rowo, misc = scan_bwd(
            conv_in, halo, conv_weight[k], bias, col, row, skip, bc, d_ssm, incoming, outgoing)
        edges = jnp.concatenate([edge_x[:edge_count], edge_bc[:edge_count]], 1)
        edge_back = passed_along(edges, "ctx", -1)
        taps_grad = jnp.concatenate([gt_x, gt_bc], 1)
        colf = jnp.transpose(colo, (1, 0, 2))
        d_cum = colf[:, :, :K].reshape(rows, H) - jnp.transpose(rowo[:, :K], (2, 0, 1)).reshape(rows, H)
        g_skip = misc[:, 0].reshape(H, P_SIZE).sum(1)
        r_sum = misc[:, 1].reshape(H, P_SIZE).sum(1)
        hg = jnp.transpose(misc[:, 2:4].reshape(G, 2, 2, N), (0, 2, 1, 3)).sum(-1).reshape(H)
        d_last = r_sum + totals[::P_SIZE, 0] * hg
        d_cum = d_cum + jnp.where(order[:, None] == rows - 1, d_last[None, :], 0.0)
        d_log = jnp.dot(lower.T, d_cum, precision=HIGH)
        rate = jnp.exp(decay_log[k])[None, :]
        d_step = colf[:, :, K:].reshape(rows, H) - d_log * rate
        d_raw = d_step * jax.nn.sigmoid(raw_steps + step_bias[k][None, :])
        g_bias = d_raw.sum(0)
        g_log = -(d_log * steps * rate).sum(0)
        d_conv = jnp.concatenate([d_x, d_bc], 1)
        d_conv = d_conv + jnp.pad(edge_back, ((rows - edge_count, 0), (0, 0)))
        d_rest = jnp.concatenate([d_conv, d_raw], 1).astype(BF)
        d_normed = right_transposed(d_gate, w_gate) + right_transposed(d_rest, w_conv)
        _, pullback = jax.vjp(rms_norm, stream_in, norm_gain[k])
        d_stream, g_norm = pullback(d_normed)
        grad_stream = grad_stream + d_stream
        owned_in, owned_out = weight_gradients(normed, jnp.concatenate([d_gate, d_rest], 1), gnormed, grad_bf)
        small = [g_norm, taps_grad[:CONV].reshape(-1), taps_grad[CONV], g_bias, g_log, g_skip, g_gate.reshape(-1)]
        sizes = [part.shape[0] for part in small]
        flat = jnp.concatenate(small)
        flat = all_sum(jnp.pad(flat, (0, -flat.shape[0] % 1024)).reshape(-1, 128)).reshape(-1)
        parts, at = [], 0
        for size in sizes:
            parts.append(flat[at : at + size])
            at += size
        parts[1] = parts[1].reshape(CONV, CC)
        collected.append((owned_in, owned_out, *parts))
    collected = collected[::-1]
    stacked = [jnp.stack([entry[member] for entry in collected], 0) for member in range(9)]
    return (stream, grad_stream, *stacked)


def solution(mesh):
    tokens = P(("fsdp", "ctx"), None)
    sharded = P(None, "fsdp", None)
    owned = P(None, ("fsdp", "ctx"), None)
    return jax.shard_map(
        local,
        mesh=mesh,
        in_specs=(tokens, sharded, sharded) + (P(),) * 7 + (tokens,),
        out_specs=(tokens, tokens, owned, owned) + (P(),) * 7,
        check_vma=False,
    )
```

time: 1530 us -> 1250 us (0.82)
  Pallas kernels: 0 us -> 153 us
  waiting for transfers between devices: 683 us -> 530 us
  matrix products: 285 us -> 135 us
  other arithmetic: 168 us -> 49.2 us
  blocking collectives: 197 us -> 113 us
  starting transfers between devices: 76.3 us -> 110 us
  local copies, waits for them, and re-layouts: 96.6 us -> 127 us
    ppermute x16 -> x28, waiting for transfers between devices: 450 us -> 183 us  [passed_along(): lax.ppermute(value, axis, [(source, source + steps) for source in range(i...]
    dot_general x30 -> x10, matrix products: 211 us -> 47.5 us  [the longest x2 16.4 us: local(): gate_in = jnp.dot(normed, w_gate, preferred_element_type=F32)]
    pallas_call x0 -> x8, Pallas kernels: none -> 153 us  [the longest x2 53.8 us: scan_bwd(): pl.pallas_call(scan_bwd_kernel, grid=(G,), in_specs=conv_specs(rows) + [f...]
    all_to_all x1, waiting for transfers between devices: 0.01 us -> 114 us  [weight_gradients(): lax.all_to_all(proj_split, 'ctx', split_axis=2, concat_axis=0, tiled=True)]
    psum x1 -> x0, waiting for transfers between devices: 106 us -> none  [local(): lax.psum((stacked[2], stacked[3], stacked[4], stacked[5], stacked[6], sta...]
    all_gather x4 -> x6, waiting for transfers between devices: 98.6 us -> 156 us  [the longest x2 107 us: local(): lax.all_gather(in_weight[k][:, DI:], 'fsdp', axis=0, tiled=True)]
    reduce_sum x16 -> x6, other arithmetic: 49.4 us -> 1.19 us  [the longest x2 0.74 us: local(): g_skip = misc[:, 0].reshape(H, P_SIZE).sum(1)]
    psum x1 -> x0, blocking collectives: 43.2 us -> none  [local(): lax.psum((stacked[2], stacked[3], stacked[4], stacked[5], stacked[6], sta...]
  transfers between devices with their start and end apart: 32 -> 56, of which waited for: 15 -> 34; matrix products, arithmetic and copies ran while one was open for 34% -> 24% of each run, Pallas kernels for 0% -> 12%
where the time goes in v1:
time: 1250 us; the launch traced here: 1230 us
  waiting for transfers between devices  530 us (42%)
  Pallas kernels  153 us (12%)
  matrix products  135 us (11%)
  local copies, waits for them, and re-layouts  127 us (10%)
  blocking collectives  113 us (9%)
  starting transfers between devices  110 us (9%)
  other arithmetic  49.2 us (4%)
  between operations  15.9 us (1%)
    ppermute x28, waiting for transfers between devices, passed_along(): lax.ppermute(value, axis, [(source, source + steps) for source in range(i...  183 us
    all_to_all x1, waiting for transfers between devices, weight_gradients(): lax.all_to_all(proj_split, 'ctx', split_axis=2, concat_axis=0, tiled=True)  114 us
    all_gather x2, waiting for transfers between devices, local(): lax.all_gather(in_weight[k][:, DI:], 'fsdp', axis=0, tiled=True)  107 us
    all_to_all x1, blocking collectives, weight_gradients(): lax.all_to_all(proj_split, 'ctx', split_axis=2, concat_axis=0, tiled=True)  75.4 us
    ppermute x28, starting transfers between devices, passed_along(): lax.ppermute(value, axis, [(source, source + steps) for source in range(i...  73.3 us
    pallas_call x2, Pallas kernels, scan_bwd(): pl.pallas_call(scan_bwd_kernel, grid=(G,), in_specs=conv_specs(rows) + [f...  53.8 us
    dot_general x6, matrix products, right_transposed(): lax.dot_general(left, right, (((1,), (1,)), ((), ())), preferred_element_...  51.1 us
    pallas_call x2, Pallas kernels, gate_bwd(): pl.pallas_call(gate_bwd_kernel, grid=(2, G), in_specs=[block, block, bloc...  47.4 us
  transfers between devices with their start and end apart: 56, of which 34 were waited for; matrix products, arithmetic and copies ran while one was open for 24% of the time, Pallas kernels for 12%

profile of v1, /device:TPU:0, one launch (start us, length us, event | category | flops | bytes accessed | tf_op | source)
XLA Modules:
  0.0 1233.7 jit_solution(4744279655514361703)
XLA Ops:
  30.3 50.4 %all-gather.13.cloned.1.call-done = bf16[1536,3376]{1,0:T(8,128)(2,1)} async-done(((bf16[192,3376]{1,0:T(8,128)(2,1)}), bf16[1536,3376]{1,0:T(8,128)(2,1)}) %all-gather.13.cloned.1.call-update) | async-done | bytes 10371088 | tf_op jit(solution)/shard_map/all_gather | solution.py:479
  80.7 5.9 fusion.67
  97.1 14.4 %scan_fwd.2 = (f32[256,3072]{1,0:T(8,128)}, f32[3072,128]{1,0:T(8,128)}, f32[256,256]{1,0:T(8,128)}) custom-call(bf16[256,3328]{1,0:T(8,128)(2,1)} %slice.363.conv_ref.conv_bc_ref, bf16[256,3328]{1,0:T(8,128)(2,1)} %slice.363.conv_ref.conv_bc_ref, f32[8,3328]{1,0:T(8,128)} %pad_convert_fusion.1.halo_ref.halo_bc_ref, ...), custom_call_target="tpu_custom_call" | custom-call | tf_op jit(solution)/shard_map/scan_fwd/pallas_call | solution.py:317
  121.7 5.4 collective-permute-done.4
  129.1 5.2 collective-permute-start.5
  136.5 6.4 collective-permute-done.5
  153.7 4.7 collective-permute-done.2
  163.8 8.2 fusion.69.gate_ref
  175.6 11.4 gate_fwd.2
  186.9 15.6 %all-gather.29.cloned.1.call-done = bf16[1,3072,1536]{2,1,0:T(8,128)(2,1)} async-done(((bf16[1,384,1536]{2,1,0:T(8,128)(2,1)}), bf16[1,3072,1536]{2,1,0:T(8,128)(2,1)}) %all-gather.29.cloned.1.call-update) | async-done | bytes 9437200 | tf_op jit(solution)/shard_map/all_gather | solution.py:481
  202.5 5.8 multiply_reduce_fusion.4
  211.7 56.3 %all-gather.17.cloned.1.call-done = bf16[1536,3376]{1,0:T(8,128)(2,1)} async-done(((bf16[192,3376]{1,0:T(8,128)(2,1)}), bf16[1536,3376]{1,0:T(8,128)(2,1)}) %all-gather.17.cloned.1.call-update) | async-done | bytes 10371088 | tf_op jit(solution)/shard_map/all_gather | solution.py:479
  268.0 6.1 fusion.68
  286.4 14.7 %scan_fwd.3 = (f32[256,3072]{1,0:T(8,128)}, f32[3072,128]{1,0:T(8,128)}, f32[256,256]{1,0:T(8,128)}) custom-call(bf16[256,3328]{1,0:T(8,128)(2,1)} %slice.371.conv_ref.conv_bc_ref, bf16[256,3328]{1,0:T(8,128)(2,1)} %slice.371.conv_ref.conv_bc_ref, f32[8,3328]{1,0:T(8,128)} %pad_convert_fusion.halo_ref.halo_bc_ref, ...), custom_call_target="tpu_custom_call" | custom-call | tf_op jit(solution)/shard_map/scan_fwd/pallas_call | solution.py:317
  311.0 5.2 collective-permute-done.11
  318.2 5.2 collective-permute-start.12
  325.9 6.1 collective-permute-done.12
  334.5 5.1 collective-permute-start.9
  339.7 8.3 fusion.dn_ref
  355.5 33.4 %all-gather.19.cloned.1.call-done = bf16[1536,3072]{1,0:T(8,128)(2,1)} async-done(((bf16[192,3072]{1,0:T(8,128)(2,1)}), bf16[1536,3072]{1,0:T(8,128)(2,1)}) %all-gather.19.cloned.1.call-update) | async-done | bytes 9437200 | tf_op jit(solution)/shard_map/all_gather | solution.py:480
  388.9 8.2 fusion.70.gate_ref
  399.2 11.5 gate_fwd.3
  410.6 23.1 %gate_bwd.2 = (f32[256,3072]{1,0:T(8,128)}, bf16[256,3072]{1,0:T(8,128)(2,1)}, f32[1,3072]{1,0:T(1,128)}, f32[3072,128]{1,0:T(8,128)}) custom-call(f32[256,3072]{1,0:T(8,128)} %get-tuple-element.55.ssm_ref, f32[256,3072]{1,0:T(8,128)} %fusion.70.gate_ref, f32[256,3072]{1,0:T(8,128)} %fusion.dn_ref, f32[1,3072]{1,0:T(1,128)} %get-tuple-element.143.gain_ref, ...), custom_call_target="tpu_custom_call" | custom-call | tf_op jit(solution)/shard_map/gate_bwd/pallas_call | solution.py:345
  437.9 22.2 %collective-permute-done.14 = bf16[1536,128]{1,0:T(8,128)(2,1)S(1)} collective-permute-done((bf16[1536,128]{1,0:T(8,128)(2,1)S(1)}, bf16[1536,128]{1,0:T(8,128)(2,1)S(1)}, u32[]{:S(2)}, u32[]{:S(2)}) %collective-permute-start.14) | collective-permute-done | bytes 393248 | tf_op jit(solution)/shard_map/ppermute | solution.py:378
  461.7 6.8 collective-permute-done.17
  468.6 8.4 collective-permute-done.15
  481.7 29.6 %collective-permute-done.18 = bf16[1536,128]{1,0:T(8,128)(2,1)} collective-permute-done((bf16[1536,128]{1,0:T(8,128)(2,1)}, bf16[1536,128]{1,0:T(8,128)(2,1)}, u32[]{:S(2)}, u32[]{:S(2)}) %collective-permute-start.18) | collective-permute-done | bytes 393248 | tf_op jit(solution)/shard_map/ppermute | solution.py:378
  513.9 8.0 fusion.71
  521.9 16.5 %collective-permute-done.16 = bf16[1536,128]{1,0:T(8,128)(2,1)S(1)} collective-permute-done((bf16[1536,128]{1,0:T(8,128)(2,1)}, bf16[1536,128]{1,0:T(8,128)(2,1)S(1)}, u32[]{:S(2)}, u32[]{:S(2)}) %collective-permute-start.16) | collective-permute-done | bytes 393248 | tf_op jit(solution)/shard_map/ppermute | solution.py:378
  538.4 15.1 %collective-permute-done.19 = bf16[1536,128]{1,0:T(8,128)(2,1)S(1)} collective-permute-done((bf16[1536,128]{1,0:T(8,128)(2,1)S(1)}, bf16[1536,128]{1,0:T(8,128)(2,1)S(1)}, u32[]{:S(2)}, u32[]{:S(2)}) %collective-permute-start.19) | collective-permute-done | bytes 393248 | tf_op jit(solution)/shard_map/ppermute | solution.py:378
  554.5 26.9 %scan_bwd.2 = (f32[256,3072]{1,0:T(8,128)}, f32[8,3072]{1,0:T(8,128)}, f32[8,3072]{1,0:T(8,128)}, f32[256,256]{1,0:T(8,128)}, f32[8,256]{1,0:T(8,128)}, /*index=...) custom-call(bf16[256,3328]{1,0:T(8,128)(2,1)} %slice.371.conv_ref.conv_bc_ref, ...), custom_call_target="tpu_custom_call" | custom-call | tf_op jit(solution)/shard_map/scan_bwd/pallas_call | solution.py:362
  588.3 5.7 collective-permute-done.20
  598.4 8.3 reshape.236
  606.7 6.7 copy.161
  613.4 4.7 all-to-all-start.2
  618.3 8.9 multiply_reduce_fusion
  629.2 113.6 %all-to-all-done.2 = bf16[256,1,4,1612]{0,3,1,2:T(8,128)(2,1)} async-done(((bf16[256,1,4,1612]{0,3,1,2:T(8,128)(2,1)}), bf16[256,1,4,1612]{0,3,1,2:T(8,128)(2,1)}, u32[]{:S(2)}, u32[]{:S(2)}) %all-to-all-start.2) | async-done | bytes 3301408 | tf_op jit(solution)/shard_map/all_to_all | solution.py:437
  742.8 5.5 copy.162
  748.3 10.8 fusion.74
  760.2 9.0 fusion.4.dn_ref
  769.1 24.4 %gate_bwd.3 = (f32[256,3072]{1,0:T(8,128)}, bf16[256,3072]{1,0:T(8,128)(2,1)}, f32[1,3072]{1,0:T(1,128)}, f32[3072,128]{1,0:T(8,128)}) custom-call(f32[256,3072]{1,0:T(8,128)} %get-tuple-element.66.ssm_ref, f32[256,3072]{1,0:T(8,128)} %fusion.69.gate_ref, f32[256,3072]{1,0:T(8,128)} %fusion.4.dn_ref, f32[1,3072]{1,0:T(1,128)} %get-tuple-element.144.gain_ref, ...), custom_call_target="tpu_custom_call" | custom-call | tf_op jit(solution)/shard_map/gate_bwd/pallas_call | solution.py:345
  797.8 11.3 collective-permute-done.21
  810.6 6.8 collective-permute-done.24
  817.5 5.7 collective-permute-done.22
  826.3 11.3 collective-permute-done.25
  839.9 6.1 collective-permute-done.23
  846.0 4.9 collective-permute-done.26
  851.8 26.9 %scan_bwd.3 = (f32[256,3072]{1,0:T(8,128)}, f32[8,3072]{1,0:T(8,128)}, f32[8,3072]{1,0:T(8,128)}, f32[256,256]{1,0:T(8,128)}, f32[8,256]{1,0:T(8,128)}, /*index=...) custom-call(bf16[256,3328]{1,0:T(8,128)(2,1)} %slice.363.conv_ref.conv_bc_ref, ...), custom_call_target="tpu_custom_call" | custom-call | tf_op jit(solution)/shard_map/scan_bwd/pallas_call | solution.py:362
  892.6 8.3 reshape.235
  900.9 6.7 copy.157
  907.6 75.4 %all_to_all.92 = bf16[256,1,4,1612]{0,3,1,2:T(8,128)(2,1)} all-to-all(bf16[256,1,4,1612]{0,3,1,2:T(8,128)(2,1)} %copy.157), channel_id=1, replica_groups=mesh['fsdp'=8,'ctx'=4] {'ctx'}, dimensions={2} | all-to-all | bytes 6602752 | tf_op jit(solution)/shard_map/all_to_all | solution.py:437
  983.1 5.5 copy.158
  988.6 10.8 fusion.73
  1003.6 37.7 %all_to_all.93 = bf16[256,8,4,96]{0,3,1,2:T(8,128)(2,1)S(1)} all-to-all(bf16[256,8,4,96]{0,3,1,2:T(8,128)(2,1)S(1)} %copy.168), channel_id=1, replica_groups=mesh['fsdp'=8,'ctx'=4] {'ctx'}, dimensions={2} | all-to-all | bytes 3145728 | tf_op jit(solution)/shard_map/all_to_all | solution.py:438
  1044.0 7.3 fusion.76
  1066.0 5.1 collective-permute-done.34
  1073.2 24.1 %all-to-all-done.4 = bf16[256,8,4,96]{0,3,1,2:T(8,128)(2,1)} async-done(((bf16[256,8,4,96]{0,3,1,2:T(8,128)(2,1)}), bf16[256,8,4,96]{0,3,1,2:T(8,128)(2,1)}, u32[]{:S(2)}, u32[]{:S(2)}) %all-to-all-start.4) | async-done | bytes 1572896 | tf_op jit(solution)/shard_map/all_to_all | solution.py:438
  1101.8 7.3 fusion.75
  1109.1 8.4 fusion.13
  1119.5 7.6 fusion.72
  1130.7 9.4 multiply_reduce_fusion.1
  1157.1 18.5 %collective-permute-done.31 = f32[168,128]{1,0:T(8,128)S(1)} collective-permute-done((f32[168,128]{1,0:T(8,128)S(1)}, f32[168,128]{1,0:T(8,128)S(1)}, u32[]{:S(2)}, u32[]{:S(2)}) %collective-permute-start.31) | collective-permute-done | bytes 86048 | tf_op jit(solution)/shard_map/ppermute | solution.py:406
  1175.6 4.6 collective-permute-start.32
  1202.3 19.5 %all-to-all-done.1 = f32[4,48,1612]{2,1,0:T(8,128)S(1)} async-done(((f32[4,48,1612]{2,1,0:T(8,128)}), f32[4,48,1612]{2,1,0:T(8,128)S(1)}, u32[]{:S(2)}, u32[]{:S(2)}) %all-to-all-start.1) | async-done | bytes 1238048 | tf_op jit(solution)/shard_map/all_to_all | solution.py:448
  (448 shorter events, 241.0 us)
Async XLA Ops:
  7.2 73.5 %all-gather.13.cloned.1.call-start = ((), (), s32[]{:S(2)}) async-start(), calls=%async_computation.10 | async-start | bytes 11943936 | tf_op jit(solution)/shard_map/all_gather | solution.py:479
  14.1 149.7 %all-gather.15.cloned.1.call-start = ((), (), s32[]{:S(2)}) async-start(), calls=%async_computation.11 | async-start | bytes 10616832 | tf_op jit(solution)/shard_map/all_gather | solution.py:480
  16.6 186.0 %all-gather.29.cloned.1.call-start = ((), (), s32[]{:S(2)}) async-start(), calls=%async_computation.22 | async-start | bytes 10616832 | tf_op jit(solution)/shard_map/all_gather | solution.py:481
  19.9 248.1 %all-gather.17.cloned.1.call-start = ((), (), s32[]{:S(2)}) async-start(), calls=%async_computation.12 | async-start | bytes 11943936 | tf_op jit(solution)/shard_map/all_gather | solution.py:479
  22.5 317.2 %all-gather.31.cloned.1.call-start = ((), (), s32[]{:S(2)}) async-start(), calls=%async_computation.23 | async-start | bytes 10616832 | tf_op jit(solution)/shard_map/all_gather | solution.py:481
  23.1 365.8 %all-gather.19.cloned.1.call-start = ((), (), s32[]{:S(2)}) async-start(), calls=%async_computation.13 | async-start | bytes 10616832 | tf_op jit(solution)/shard_map/all_gather | solution.py:480
  25.9 722.4 %all-gather.23.cloned.1.call-start = ((), (), s32[]{:S(2)}) async-start(), calls=%async_computation.16 | async-start | bytes 3932160 | tf_op jit(solution)/shard_map/all_gather | solution.py:431
  28.7 62.5 %copy-start.57 = (f32[48]{0:T(128)}, f32[48]{0:T(128)S(1)}, u32[]{:S(2)}) copy-start(f32[48]{0:T(128)S(1)} %get-tuple-element.159) | copy-start | bytes 580
  28.7 62.7 %copy-start.55 = (f32[48]{0:T(128)}, f32[48]{0:T(128)S(1)}, u32[]{:S(2)}) copy-start(f32[48]{0:T(128)S(1)} %get-tuple-element.148) | copy-start | bytes 580
  28.9 57.6 %copy-start.14 = (bf16[256,1536]{1,0:T(8,128)(2,1)}, bf16[256,1536]{1,0:T(8,128)(2,1)S(1)}, u32[]{:S(2)}) copy-start(bf16[256,1536]{1,0:T(8,128)(2,1)S(1)} %multiply_convert_fusion.1) | copy-start | bytes 2359300
  87.8 8.7 collective-permute-start
  114.5 12.6 %collective-permute-start.4 = (bf16[1536,128]{1,0:T(8,128)(2,1)}, bf16[1536,128]{1,0:T(8,128)(2,1)}, u32[]{:S(2)}, u32[]{:S(2)}) collective-permute-start(bf16[1536,128]{1,0:T(8,128)(2,1)} %get-tuple-element.121), channel_id=1, source_target_pairs={{0,1},{1,2},{2,3},{4,5},{5,6},{6,7},{8,9},{9,10},{10,11},{12,13},{... | collective-permute-start | bytes 1179656 | tf_op jit(solution)/shard_map/ppermute | solution.py:378
  119.0 16.7 %collective-permute-start.1 = (bf16[1536,128]{1,0:T(8,128)(2,1)}, bf16[1536,128]{1,0:T(8,128)(2,1)S(1)}, u32[]{:S(2)}, u32[]{:S(2)}) collective-permute-start(bf16[1536,128]{1,0:T(8,128)(2,1)} %get-tuple-element.122), channel_id=1, source_target_pairs={{0,1},{1,2},{2,3},{4,5},{5,6},{6,7},{8,9},{9,10},{10,11},{12,13},{... | collective-permute-start | bytes 1179656 | tf_op jit(solution)/shard_map/ppermute | solution.py:378
  129.1 13.8 %collective-permute-start.5 = (bf16[1536,128]{1,0:T(8,128)(2,1)}, bf16[1536,128]{1,0:T(8,128)(2,1)}, u32[]{:S(2)}, u32[]{:S(2)}) collective-permute-start(bf16[1536,128]{1,0:T(8,128)(2,1)} %add_convert_fusion.13), channel_id=1, source_target_pairs={{0,1},{1,2},{2,3},{4,5},{5,6},{6,7},{8,9},{9,10},{10,11},{12,13},{... | collective-permute-start | bytes 1179656 | tf_op jit(solution)/shard_map/ppermute | solution.py:378
  144.5 13.9 %collective-permute-start.2 = (bf16[1536,128]{1,0:T(8,128)(2,1)S(1)}, bf16[1536,128]{1,0:T(8,128)(2,1)S(1)}, u32[]{:S(2)}, u32[]{:S(2)}) collective-permute-start(bf16[1536,128]{1,0:T(8,128)(2,1)S(1)} %get-tuple-element.120), channel_id=1, source_target_pairs={{0,1},{1,2},{2,3},{4,5},{5,6},{6,7},{8,9},{9,10},{10,11},{12,13},{... | collective-permute-start | bytes 1179656 | tf_op jit(solution)/shard_map/ppermute | solution.py:378
  149.6 24.0 %collective-permute-start.6 = (bf16[1536,128]{1,0:T(8,128)(2,1)S(1)}, bf16[1536,128]{1,0:T(8,128)(2,1)}, u32[]{:S(2)}, u32[]{:S(2)}) collective-permute-start(bf16[1536,128]{1,0:T(8,128)(2,1)S(1)} %get-tuple-element.119), channel_id=1, source_target_pairs={{0,1},{1,2},{2,3},{4,5},{5,6},{6,7},{8,9},{9,10},{10,11},{12,13},{... | collective-permute-start | bytes 1179656 | tf_op jit(solution)/shard_map/ppermute | solution.py:378
  159.4 14.1 %collective-permute-start.3 = (bf16[1536,128]{1,0:T(8,128)(2,1)}, bf16[1536,128]{1,0:T(8,128)(2,1)S(1)}, u32[]{:S(2)}, u32[]{:S(2)}) collective-permute-start(bf16[1536,128]{1,0:T(8,128)(2,1)} %add_convert_fusion.14), channel_id=1, source_target_pairs={{0,1},{1,2},{2,3},{4,5},{5,6},{6,7},{8,9},{9,10},{10,11},{12,13},{... | collective-permute-start | bytes 1179656 | tf_op jit(solution)/shard_map/ppermute | solution.py:378
  208.3 65.7 %copy-start.51 = (f32[256]{0:T(256)}, f32[256]{0:T(256)S(1)}, u32[]{:S(2)}) copy-start(f32[256]{0:T(256)S(1)} %get-tuple-element.153) | copy-start | bytes 3076
  210.6 778.0 %all-gather.21.cloned.1.call-start = ((), (), s32[]{:S(2)}) async-start(), calls=%async_computation.14 | async-start | bytes 3932160 | tf_op jit(solution)/shard_map/all_gather | solution.py:431
  211.7 67.1 %copy-start.60 = (f32[48]{0:T(128)S(1)}, f32[48]{0:T(128)}, u32[]{:S(2)}) copy-start(f32[48]{0:T(128)} %get-tuple-element.160) | copy-start | bytes 580
  274.8 10.3 collective-permute-start.7
  303.7 12.5 %collective-permute-start.11 = (bf16[1536,128]{1,0:T(8,128)(2,1)}, bf16[1536,128]{1,0:T(8,128)(2,1)}, u32[]{:S(2)}, u32[]{:S(2)}) collective-permute-start(bf16[1536,128]{1,0:T(8,128)(2,1)} %get-tuple-element.117), channel_id=1, source_target_pairs={{0,1},{1,2},{2,3},{4,5},{5,6},{6,7},{8,9},{9,10},{10,11},{12,13},{... | collective-permute-start | bytes 1179656 | tf_op jit(solution)/shard_map/ppermute | solution.py:378
  307.5 18.4 %collective-permute-start.8 = (bf16[1536,128]{1,0:T(8,128)(2,1)}, bf16[1536,128]{1,0:T(8,128)(2,1)}, u32[]{:S(2)}, u32[]{:S(2)}) collective-permute-start(bf16[1536,128]{1,0:T(8,128)(2,1)} %get-tuple-element.118), channel_id=1, source_target_pairs={{0,1},{1,2},{2,3},{4,5},{5,6},{6,7},{8,9},{9,10},{10,11},{12,13},{... | collective-permute-start | bytes 1179656 | tf_op jit(solution)/shard_map/ppermute | solution.py:378
  318.2 13.9 %collective-permute-start.12 = (bf16[1536,128]{1,0:T(8,128)(2,1)}, bf16[1536,128]{1,0:T(8,128)(2,1)}, u32[]{:S(2)}, u32[]{:S(2)}) collective-permute-start(bf16[1536,128]{1,0:T(8,128)(2,1)} %add_convert_fusion.9), channel_id=1, source_target_pairs={{0,1},{1,2},{2,3},{4,5},{5,6},{6,7},{8,9},{9,10},{10,11},{12,13},{... | collective-permute-start | bytes 1179656 | tf_op jit(solution)/shard_map/ppermute | solution.py:378
  323.4 720.7 %all-gather.27.cloned.1.call-start = ((), (), s32[]{:S(2)}) async-start(), calls=%async_computation.20 | async-start | bytes 3932160 | tf_op jit(solution)/shard_map/all_gather | solution.py:432
  334.5 17.2 %collective-permute-start.9 = (bf16[1536,128]{1,0:T(8,128)(2,1)}, bf16[1536,128]{1,0:T(8,128)(2,1)}, u32[]{:S(2)}, u32[]{:S(2)}) collective-permute-start(bf16[1536,128]{1,0:T(8,128)(2,1)} %get-tuple-element.116), channel_id=1, source_target_pairs={{0,1},{1,2},{2,3},{4,5},{5,6},{6,7},{8,9},{9,10},{10,11},{12,13},{... | collective-permute-start | bytes 1179656 | tf_op jit(solution)/shard_map/ppermute | solution.py:378
  347.9 49.2 %collective-permute-start.13 = (bf16[1536,128]{1,0:T(8,128)(2,1)}, bf16[1536,128]{1,0:T(8,128)(2,1)}, u32[]{:S(2)}, u32[]{:S(2)}) collective-permute-start(bf16[1536,128]{1,0:T(8,128)(2,1)} %get-tuple-element.115), channel_id=1, source_target_pairs={{0,1},{1,2},{2,3},{4,5},{5,6},{6,7},{8,9},{9,10},{10,11},{12,13},{... | collective-permute-start | bytes 1179656 | tf_op jit(solution)/shard_map/ppermute | solution.py:378
  353.8 43.3 %collective-permute-start.10 = (bf16[1536,128]{1,0:T(8,128)(2,1)}, bf16[1536,128]{1,0:T(8,128)(2,1)S(1)}, u32[]{:S(2)}, u32[]{:S(2)}) collective-permute-start(bf16[1536,128]{1,0:T(8,128)(2,1)} %add_convert_fusion.10), channel_id=1, source_target_pairs={{0,1},{1,2},{2,3},{4,5},{5,6},{6,7},{8,9},{9,10},{10,11},{12,13},{... | collective-permute-start | bytes 1179656 | tf_op jit(solution)/shard_map/ppermute | solution.py:378
  435.3 24.8 %collective-permute-start.14 = (bf16[1536,128]{1,0:T(8,128)(2,1)S(1)}, bf16[1536,128]{1,0:T(8,128)(2,1)S(1)}, u32[]{:S(2)}, u32[]{:S(2)}) collective-permute-start(bf16[1536,128]{1,0:T(8,128)(2,1)S(1)} %get-tuple-element.113), channel_id=1, source_target_pairs={{1,0},{2,1},{3,2},{5,4},{6,5},{7,6},{9,8},{10,9},{11,10},{13,12},{... | collective-permute-start | bytes 1179656 | tf_op jit(solution)/shard_map/ppermute | solution.py:378
  436.6 31.9 %collective-permute-start.17 = (bf16[1536,128]{1,0:T(8,128)(2,1)S(1)}, bf16[1536,128]{1,0:T(8,128)(2,1)S(1)}, u32[]{:S(2)}, u32[]{:S(2)}) collective-permute-start(bf16[1536,128]{1,0:T(8,128)(2,1)S(1)} %get-tuple-element.114), channel_id=1, source_target_pairs={{1,0},{2,1},{3,2},{5,4},{6,5},{7,6},{9,8},{10,9},{11,10},{13,12},{... | collective-permute-start | bytes 1179656 | tf_op jit(solution)/shard_map/ppermute | solution.py:378
  460.4 16.6 %collective-permute-start.15 = (bf16[1536,128]{1,0:T(8,128)(2,1)S(1)}, bf16[1536,128]{1,0:T(8,128)(2,1)S(1)}, u32[]{:S(2)}, u32[]{:S(2)}) collective-permute-start(bf16[1536,128]{1,0:T(8,128)(2,1)S(1)} %add_convert_fusion.7), channel_id=1, source_target_pairs={{1,0},{2,1},{3,2},{5,4},{6,5},{7,6},{9,8},{10,9},{11,10},{13,12},{... | collective-permute-start | bytes 1179656 | tf_op jit(solution)/shard_map/ppermute | solution.py:378
  478.4 33.0 %collective-permute-start.18 = (bf16[1536,128]{1,0:T(8,128)(2,1)}, bf16[1536,128]{1,0:T(8,128)(2,1)}, u32[]{:S(2)}, u32[]{:S(2)}) collective-permute-start(bf16[1536,128]{1,0:T(8,128)(2,1)} %get-tuple-element.112), channel_id=1, source_target_pairs={{1,0},{2,1},{3,2},{5,4},{6,5},{7,6},{9,8},{10,9},{11,10},{13,12},{... | collective-permute-start | bytes 1179656 | tf_op jit(solution)/shard_map/ppermute | solution.py:378
  480.1 106.2 %copy-start.75 = (pred[256]{0:T(512)(128)(4,1)}, pred[256]{0:T(512)(128)(4,1)S(1)}, u32[]{:S(2)}) copy-start(pred[256]{0:T(512)(128)(4,1)S(1)} %iota_compare_fusion.5) | copy-start | bytes 772
  480.4 58.0 %collective-permute-start.16 = (bf16[1536,128]{1,0:T(8,128)(2,1)}, bf16[1536,128]{1,0:T(8,128)(2,1)S(1)}, u32[]{:S(2)}, u32[]{:S(2)}) collective-permute-start(bf16[1536,128]{1,0:T(8,128)(2,1)} %get-tuple-element.111), channel_id=1, source_target_pairs={{1,0},{2,1},{3,2},{5,4},{6,5},{7,6},{9,8},{10,9},{11,10},{13,12},{... | collective-permute-start | bytes 1179656 | tf_op jit(solution)/shard_map/ppermute | solution.py:378
  512.6 40.9 %collective-permute-start.19 = (bf16[1536,128]{1,0:T(8,128)(2,1)S(1)}, bf16[1536,128]{1,0:T(8,128)(2,1)S(1)}, u32[]{:S(2)}, u32[]{:S(2)}) collective-permute-start(bf16[1536,128]{1,0:T(8,128)(2,1)S(1)} %add_convert_fusion.4), channel_id=1, source_target_pairs={{1,0},{2,1},{3,2},{5,4},{6,5},{7,6},{9,8},{10,9},{11,10},{13,12},{... | collective-permute-start | bytes 1179656 | tf_op jit(solution)/shard_map/ppermute | solution.py:378
  585.0 8.9 collective-permute-start.20
  613.4 129.4 %all-to-all-start.2 = ((bf16[256,1,4,1612]{0,3,1,2:T(8,128)(2,1)}), bf16[256,1,4,1612]{0,3,1,2:T(8,128)(2,1)}, u32[]{:S(2)}, u32[]{:S(2)}) async-start(bf16[256,1,4,1612]{0,3,1,2:T(8,128)(2,1)} %copy.161), calls=%async_computation.3 | async-start | bytes 6619136 | tf_op jit(solution)/shard_map/all_to_all | solution.py:437
  618.1 483.7 %all-gather.25.cloned.1.call-start = ((), (), s32[]{:S(2)}) async-start(), calls=%async_computation.18 | async-start | bytes 3932160 | tf_op jit(solution)/shard_map/all_gather | solution.py:432
  629.1 519.9 %reduce-scatter.7.cloned.1.call-start = ((), (), s32[]{:S(2)}) async-start(), calls=%async_computation.17 | async-start | bytes 11501568 | tf_op jit(solution)/shard_map/reduce_scatter | solution.py:445
  759.1 428.9 %reduce-scatter.5.cloned.1.call-start = ((), (), s32[]{:S(2)}) async-start(), calls=%async_computation.15 | async-start | bytes 11501568 | tf_op jit(solution)/shard_map/reduce_scatter | solution.py:445
  795.2 13.9 %collective-permute-start.21 = (bf16[1536,128]{1,0:T(8,128)(2,1)S(1)}, bf16[1536,128]{1,0:T(8,128)(2,1)S(1)}, u32[]{:S(2)}, u32[]{:S(2)}) collective-permute-start(bf16[1536,128]{1,0:T(8,128)(2,1)S(1)} %get-tuple-element.109), channel_id=1, source_target_pairs={{1,0},{2,1},{3,2},{5,4},{6,5},{7,6},{9,8},{10,9},{11,10},{13,12},{... | collective-permute-start | bytes 1179656 | tf_op jit(solution)/shard_map/ppermute | solution.py:378
  796.5 21.0 %collective-permute-start.24 = (bf16[1536,128]{1,0:T(8,128)(2,1)S(1)}, bf16[1536,128]{1,0:T(8,128)(2,1)S(1)}, u32[]{:S(2)}, u32[]{:S(2)}) collective-permute-start(bf16[1536,128]{1,0:T(8,128)(2,1)S(1)} %get-tuple-element.110), channel_id=1, source_target_pairs={{1,0},{2,1},{3,2},{5,4},{6,5},{7,6},{9,8},{10,9},{11,10},{13,12},{... | collective-permute-start | bytes 1179656 | tf_op jit(solution)/shard_map/ppermute | solution.py:378
  809.3 30.2 %copy-start.53 = (f32[48]{0:T(128)S(1)}, f32[48]{0:T(128)}, u32[]{:S(2)}) copy-start(f32[48]{0:T(128)} %get-tuple-element.137) | copy-start | bytes 580
  809.3 13.9 %collective-permute-start.22 = (bf16[1536,128]{1,0:T(8,128)(2,1)S(1)}, bf16[1536,128]{1,0:T(8,128)(2,1)S(1)}, u32[]{:S(2)}, u32[]{:S(2)}) collective-permute-start(bf16[1536,128]{1,0:T(8,128)(2,1)S(1)} %add_convert_fusion.3), channel_id=1, source_target_pairs={{1,0},{2,1},{3,2},{5,4},{6,5},{7,6},{9,8},{10,9},{11,10},{13,12},{... | collective-permute-start | bytes 1179656 | tf_op jit(solution)/shard_map/ppermute | solution.py:378
  823.7 13.9 %collective-permute-start.25 = (bf16[1536,128]{1,0:T(8,128)(2,1)S(1)}, bf16[1536,128]{1,0:T(8,128)(2,1)S(1)}, u32[]{:S(2)}, u32[]{:S(2)}) collective-permute-start(bf16[1536,128]{1,0:T(8,128)(2,1)S(1)} %get-tuple-element.108), channel_id=1, source_target_pairs={{1,0},{2,1},{3,2},{5,4},{6,5},{7,6},{9,8},{10,9},{11,10},{13,12},{... | collective-permute-start | bytes 1179656 | tf_op jit(solution)/shard_map/ppermute | solution.py:378
  825.0 21.0 %collective-permute-start.23 = (bf16[1536,128]{1,0:T(8,128)(2,1)S(1)}, bf16[1536,128]{1,0:T(8,128)(2,1)S(1)}, u32[]{:S(2)}, u32[]{:S(2)}) collective-permute-start(bf16[1536,128]{1,0:T(8,128)(2,1)S(1)} %get-tuple-element.107), channel_id=1, source_target_pairs={{1,0},{2,1},{3,2},{5,4},{6,5},{7,6},{9,8},{10,9},{11,10},{13,12},{... | collective-permute-start | bytes 1179656 | tf_op jit(solution)/shard_map/ppermute | solution.py:378
  837.8 13.0 %collective-permute-start.26 = (bf16[1536,128]{1,0:T(8,128)(2,1)S(1)}, bf16[1536,128]{1,0:T(8,128)(2,1)S(1)}, u32[]{:S(2)}, u32[]{:S(2)}) collective-permute-start(bf16[1536,128]{1,0:T(8,128)(2,1)S(1)} %add_convert_fusion), channel_id=1, source_target_pairs={{1,0},{2,1},{3,2},{5,4},{6,5},{7,6},{9,8},{10,9},{11,10},{13,12},{... | collective-permute-start | bytes 1179656 | tf_op jit(solution)/shard_map/ppermute | solution.py:378
  882.5 6.0 collective-permute-start.27
  999.5 196.0 %reduce-scatter.11.cloned.1.call-start = ((), (), s32[]{:S(2)}) async-start(), calls=%async_computation.21 | async-start | bytes 5308416 | tf_op jit(solution)/shard_map/reduce_scatter | solution.py:446
  1056.7 40.6 %all-to-all-start.4 = ((bf16[256,8,4,96]{0,3,1,2:T(8,128)(2,1)}), bf16[256,8,4,96]{0,3,1,2:T(8,128)(2,1)}, u32[]{:S(2)}, u32[]{:S(2)}) async-start(bf16[256,8,4,96]{0,3,1,2:T(8,128)(2,1)} %copy.165), calls=%async_computation.6 | async-start | bytes 3145728 | tf_op jit(solution)/shard_map/all_to_all | solution.py:438
  1061.2 135.3 %reduce-scatter.9.cloned.1.call-start = ((), (), s32[]{:S(2)}) async-start(), calls=%async_computation.19 | async-start | bytes 5308416 | tf_op jit(solution)/shard_map/reduce_scatter | solution.py:446
  1061.9 1.3 collective-permute-start.33
  1063.3 7.8 collective-permute-start.34
  1071.1 30.6 %collective-permute-start.35 = (f32[168,128]{1,0:T(8,128)S(1)}, f32[168,128]{1,0:T(8,128)S(1)}, u32[]{:S(2)}, u32[]{:S(2)}) collective-permute-start(f32[168,128]{1,0:T(8,128)S(1)} %fusion.104), channel_id=1, source_target_pairs={{0,16},{4,20},{8,24},{12,28},{16,0},{20,4},{24,8},{28,12},{1,17},{... | collective-permute-start | bytes 258056 | tf_op jit(solution)/shard_map/ppermute | solution.py:406
  1101.7 15.9 %collective-permute-start.36 = (f32[168,128]{1,0:T(8,128)S(1)}, f32[168,128]{1,0:T(8,128)S(1)}, u32[]{:S(2)}, u32[]{:S(2)}) collective-permute-start(f32[168,128]{1,0:T(8,128)S(1)} %add.252), channel_id=1, source_target_pairs={{0,1},{1,0},{2,3},{3,2},{4,5},{5,4},{6,7},{7,6},{8,9},{9,8},{10,11... | collective-permute-start | bytes 258056 | tf_op jit(solution)/shard_map/ppermute | solution.py:406
  1117.6 9.6 collective-permute-start.37
  1140.2 1.3 collective-permute-start.28
  1141.5 5.5 collective-permute-start.29
  1147.0 33.2 %copy-start.9 = (f32[256,1536]{1,0:T(8,128)S(1)}, f32[256,1536]{1,0:T(8,128)}, u32[]{:S(2)}) copy-start(f32[256,1536]{1,0:T(8,128)} %get-tuple-element.102) | copy-start | bytes 4718596
  1147.1 7.2 collective-permute-start.30
  1149.0 39.0 %all-to-all-start.3 = ((f32[4,48,1612]{2,1,0:T(8,128)}), f32[4,48,1612]{2,1,0:T(8,128)}, u32[]{:S(2)}, u32[]{:S(2)}) async-start(f32[4,48,1612]{2,1,0:T(8,128)} %bitcast.205), calls=%async_computation.5 | async-start | bytes 2555904 | tf_op jit(solution)/shard_map/all_to_all | solution.py:448
  1154.3 21.3 %collective-permute-start.31 = (f32[168,128]{1,0:T(8,128)S(1)}, f32[168,128]{1,0:T(8,128)S(1)}, u32[]{:S(2)}, u32[]{:S(2)}) collective-permute-start(f32[168,128]{1,0:T(8,128)S(1)} %add.247), channel_id=1, source_target_pairs={{0,1},{1,0},{2,3},{3,2},{4,5},{5,4},{6,7},{7,6},{8,9},{9,8},{10,11... | collective-permute-start | bytes 258056 | tf_op jit(solution)/shard_map/ppermute | solution.py:406
  1175.6 11.7 collective-permute-start.32
  1188.0 33.8 %all-to-all-start.1 = ((f32[4,48,1612]{2,1,0:T(8,128)}), f32[4,48,1612]{2,1,0:T(8,128)S(1)}, u32[]{:S(2)}, u32[]{:S(2)}) async-start(f32[4,48,1612]{2,1,0:T(8,128)} %bitcast.206), calls=%async_computation.2 | async-start | bytes 2555904 | tf_op jit(solution)/shard_map/all_to_all | solution.py:448
  (69 other events, 383.1 us)
Sparse Core Ops, SparseCore 0:
  14.3 66.3 all-gather.12
  83.2 58.7 all-gather.14
  143.8 58.6 all-gather.28
  204.3 63.6 all-gather.16
  269.7 58.6 all-gather.30
  330.2 58.6 all-gather.18
  390.5 68.0 all-gather.22
  460.1 90.4 all-gather.20
  552.2 67.9 all-gather.26
  629.2 107.3 all-gather.24
  759.2 78.6 reduce-scatter.6
  999.6 82.5 reduce-scatter.4
  1085.6 53.7 reduce-scatter.10
  1142.7 53.7 reduce-scatter.8

commit v2 on v1

--- a/solution.py
+++ b/solution.py
@@ -420,33 +420,61 @@
     return lax.dot_general(left, right, (((1,), (1,)), ((), ())), preferred_element_type=F32)
 
 
-def weight_gradients(normed, d_proj, gnormed, grad_bf):
-    tok_rows = normed.shape[0]
+def gathered(value):
+    return lax.all_gather(value, "fsdp", axis=0, tiled=True)
+
+
+def to_owners(split):
+    moved = lax.all_to_all(jnp.transpose(split, (1, 0, 2)), "fsdp", split_axis=0, concat_axis=0, tiled=True)
+    return moved.reshape(-1, split.shape[2])
+
+
+def by_run(part):
+    fsdp_count, ctx_count = lax.axis_size("fsdp"), lax.axis_size("ctx")
+    rows, width = part.shape
+    own = rows // (fsdp_count * ctx_count)
+    blocks = part.astype(BF).reshape(fsdp_count, ctx_count, own, width)
+    return jnp.transpose(blocks, (1, 0, 2, 3)).reshape(ctx_count, fsdp_count * own, width)
+
+
+def run_sum(blocks):
+    flat = blocks.reshape(-1, blocks.shape[2])
+    return lax.psum_scatter(flat, "ctx", scatter_dimension=0, tiled=True)
+
+
+def early_gradients(normed_all, grad_all, d_gate, gnormed):
+    fsdp_count, ctx_count = lax.axis_size("fsdp"), lax.axis_size("ctx")
+    rows = d_gate.shape[0]
+    width = DI // fsdp_count
+    gate_cols = to_owners(d_gate.reshape(rows, fsdp_count, width))
+    norm_cols = to_owners(gnormed.reshape(rows, fsdp_count, width))
+    part_gate = by_run(rows_product(normed_all, gate_cols))
+    part_out = rows_product(norm_cols, grad_all).astype(BF)
+    tile = width // ctx_count
+    model = part_out.shape[1]
+    part_out = jnp.transpose(part_out.reshape(ctx_count, tile, model // width, width), (0, 2, 1, 3))
+    part_out = part_out.reshape(ctx_count, -1, width)
+    summed = run_sum(jnp.concatenate([part_gate, part_out], 1))
+    in_rows = part_gate.shape[1]
+    owned_out = jnp.transpose(summed[in_rows:].reshape(model // width, tile, width), (1, 0, 2))
+    return summed[:in_rows], owned_out.reshape(tile, model).astype(F32)
+
+
+def late_gradients(normed_all, d_x, d_small, gate_sum):
     fsdp_count = lax.axis_size("fsdp")
-    ctx_count = lax.axis_size("ctx")
-    width_in = d_proj.shape[1]
-    inner = gnormed.shape[1]
-    tile_rows = inner // (fsdp_count * ctx_count)
-    all_rows = (
-        lax.all_gather(normed, "ctx", axis=0, tiled=True),
-        lax.all_gather(grad_bf, "ctx", axis=0, tiled=True),
-    )
-    proj_split = d_proj.reshape(tok_rows, 1, ctx_count, width_in // ctx_count)
-    gate_split = gnormed.reshape(tok_rows, fsdp_count, ctx_count, tile_rows)
-    cols = (
-        lax.all_to_all(proj_split, "ctx", split_axis=2, concat_axis=0, tiled=True),
-        lax.all_to_all(gate_split, "ctx", split_axis=2, concat_axis=0, tiled=True),
-    )
-    proj_cols = cols[0].reshape(ctx_count * tok_rows, width_in // ctx_count)
-    gate_cols = cols[1].reshape(ctx_count * tok_rows, fsdp_count * tile_rows)
-    part_in = rows_product(all_rows[0], proj_cols)
-    part_out = rows_product(gate_cols, all_rows[1])
-    summed = (
-        lax.psum_scatter(part_in, "fsdp", scatter_dimension=0, tiled=True),
-        lax.psum_scatter(part_out, "fsdp", scatter_dimension=0, tiled=True),
-    )
-    owned_in = lax.all_to_all(summed[0], "ctx", split_axis=0, concat_axis=1, tiled=True)
-    return (owned_in, summed[1])
+    rows = d_x.shape[0]
+    width, extra = DI // fsdp_count, d_small.shape[1] // fsdp_count
+    split = jnp.concatenate([d_x.reshape(rows, fsdp_count, width), d_small.reshape(rows, fsdp_count, extra)], 2)
+    split = jnp.pad(split, ((0, 0), (0, 0), (0, -(width + extra) % 128)))
+    part = rows_product(normed_all, to_owners(split))[:, : width + extra]
+    rest_sum = run_sum(by_run(part))
+    both = jnp.concatenate([gate_sum, rest_sum], 1)
+    both = both.reshape(fsdp_count, -1, both.shape[1])
+    both = lax.all_to_all(both, "fsdp", split_axis=0, concat_axis=0, tiled=True)
+    both = jnp.transpose(both, (1, 0, 2))
+    own = both.shape[0]
+    parts = (both[:, :, :width], both[:, :, width : 2 * width], both[:, :, 2 * width :])
+    return jnp.concatenate([part.reshape(own, -1) for part in parts], 1).astype(F32)
 
 
 def grouped(cum, steps):
@@ -472,15 +500,23 @@
     edge_count = CONV - 1
     order = jnp.arange(rows)
     lower = (order[:, None] >= order[None, :]).astype(F32)
-    weights = []
-    for k in range(LAYERS):
-        weights.append(
-            (
-                lax.all_gather(in_weight[k][:, DI:], "fsdp", axis=0, tiled=True),
-                lax.all_gather(in_weight[k][:, :DI], "fsdp", axis=0, tiled=True),
-                lax.all_gather(out_weight[k], "fsdp", axis=0, tiled=True),
-            )
-        )
+    in_rows = in_weight.shape[1]
+    model = out_weight.shape[2]
+
+    def side_by_side(k):
+        return jnp.concatenate([out_weight[k, :in_rows], out_weight[k, in_rows:]], 1)
+
+    def stacked_rows(full):
+        blocks = jnp.transpose(full.reshape(-1, in_rows, 2, model), (0, 2, 1, 3))
+        return blocks.reshape(DI, model)
+
+    first = gathered(in_weight[0])
+    middle = gathered(jnp.concatenate([side_by_side(0), in_weight[1, :, DI:]], 1))
+    last = gathered(jnp.concatenate([in_weight[1, :, :DI], side_by_side(1)], 1))
+    weights = [
+        (first[:, DI:], first[:, :DI], stacked_rows(middle[:, :DI])),
+        (middle[:, DI:], last[:, :DI], stacked_rows(last[:, DI:])),
+    ]
     stream = activations
     kept = []
     for k in range(LAYERS):
@@ -505,6 +541,7 @@
                      incoming, ssm, gnormed))
         stream = stream + jnp.dot(gnormed, w_out, preferred_element_type=F32)
     grad_stream = cotangent
+    token_rows = gathered(jnp.concatenate([kept[0][1], kept[1][1], cotangent.astype(BF)], 1))
     collected = []
     for k in reversed(range(LAYERS)):
         w_conv, w_gate, w_out = weights[k]
@@ -514,6 +551,9 @@
         d_gnormed = right_transposed(grad_bf, w_out)
         d_ssm, d_gate, g_gate, local_grad = gate_bwd(ssm, gate_in, d_gnormed, gate_gain[k][None, :], col, bc)
         outgoing = carry(totals, local_grad, -1)
+        normed_all = token_rows[:, k * model : (k + 1) * model]
+        grad_all = token_rows[:, LAYERS * model :] if k == LAYERS - 1 else gathered(grad_bf)
+        gate_sum, owned_out = early_gradients(normed_all, grad_all, d_gate, gnormed)
         d_x, edge_x, gt_x, d_bc, edge_bc, gt_bc, colo, rowo, misc = scan_bwd(
             conv_in, halo, conv_weight[k], bias, col, row, skip, bc, d_ssm, incoming, outgoing)
         edges = jnp.concatenate([edge_x[:edge_count], edge_bc[:edge_count]], 1)
@@ -539,7 +579,7 @@
         _, pullback = jax.vjp(rms_norm, stream_in, norm_gain[k])
         d_stream, g_norm = pullback(d_normed)
         grad_stream = grad_stream + d_stream
-        owned_in, owned_out = weight_gradients(normed, jnp.concatenate([d_gate, d_rest], 1), gnormed, grad_bf)
+        owned_in = late_gradients(normed_all, d_rest[:, :DI], d_rest[:, DI:], gate_sum)
         small = [g_norm, taps_grad[:CONV].reshape(-1), taps_grad[CONV], g_bias, g_log, g_skip, g_gate.reshape(-1)]
         sizes = [part.shape[0] for part in small]
         flat = jnp.concatenate(small)

time: 1250 us -> 960 us (0.77)
  waiting for transfers between devices: 530 us -> 288 us
  blocking collectives: 113 us -> 0 us
  local copies, waits for them, and re-layouts: 127 us -> 171 us
  other arithmetic: 49.2 us -> 62.5 us
  starting transfers between devices: 110 us -> 123 us
    all_to_all x4 -> x8, waiting for transfers between devices: 157 us -> 42.8 us  [the longest x6 33.6 us: to_owners(): lax.all_to_all(jnp.transpose(split, (1, 0, 2)), 'fsdp', split_axis=0, con...]
    all_to_all x2 -> x0, blocking collectives: 113 us -> none  [the longest x1 75.4 us: weight_gradients(): lax.all_to_all(proj_split, 'ctx', split_axis=2, concat_axis=0, tiled=True)]
    ppermute x28, waiting for transfers between devices: 183 us -> 93.6 us  [passed_along(): lax.ppermute(value, axis, [(source, source + steps) for source in range(i...]
    all_gather x10 -> x5, waiting for transfers between devices: 156 us -> 107 us  [gathered(): return lax.all_gather(value, 'fsdp', axis=0, tiled=True)]
    reshape x6 -> x18, local copies, waits for them, and re-layouts: 34.3 us -> 62.1 us  [the longest x2 43.4 us: stacked_rows(): blocks = jnp.transpose(full.reshape(-1, in_rows, 2, model), (0, 2, 1, 3))]
    reduce_scatter x4, waiting for transfers between devices: 1.09 us -> 24.8 us  [run_sum(): return lax.psum_scatter(flat, 'ctx', scatter_dimension=0, tiled=True)]
    transpose x0 -> x4, local copies, waits for them, and re-layouts: none -> 22 us  [the longest x2 19.4 us: stacked_rows(): blocks = jnp.transpose(full.reshape(-1, in_rows, 2, model), (0, 2, 1, 3))]
    all_to_all x6 -> x0, local copies, waits for them, and re-layouts: 17.4 us -> none  [the longest x2 11 us: weight_gradients(): lax.all_to_all(proj_split, 'ctx', split_axis=2, concat_axis=0, tiled=True)]
  transfers between devices with their start and end apart: 56 -> 55, of which waited for: 34 -> 28; matrix products, arithmetic and copies ran while one was open for 24% -> 37% of each run, Pallas kernels for 12% -> 16%
where the time goes in v2:
time: 960 us; the launch traced here: 948 us
  waiting for transfers between devices  288 us (30%)
  local copies, waits for them, and re-layouts  171 us (18%)
  Pallas kernels  152 us (16%)
  matrix products  135 us (14%)
  starting transfers between devices  123 us (13%)
  other arithmetic  62.5 us (7%)
  between operations  16.1 us (2%)
    all_gather x5, waiting for transfers between devices, gathered(): return lax.all_gather(value, 'fsdp', axis=0, tiled=True)  107 us
    ppermute x28, waiting for transfers between devices, passed_along(): lax.ppermute(value, axis, [(source, source + steps) for source in range(i...  93.6 us
    ppermute x28, starting transfers between devices, passed_along(): lax.ppermute(value, axis, [(source, source + steps) for source in range(i...  73.1 us
    pallas_call x2, Pallas kernels, scan_bwd(): pl.pallas_call(scan_bwd_kernel, grid=(G,), in_specs=conv_specs(rows) + [f...  53.8 us
    dot_general x6, matrix products, right_transposed(): lax.dot_general(left, right, (((1,), (1,)), ((), ())), preferred_element_...  47.7 us
    pallas_call x2, Pallas kernels, gate_bwd(): pl.pallas_call(gate_bwd_kernel, grid=(2, G), in_specs=[block, block, bloc...  46.1 us
    reshape x2, local copies, waits for them, and re-layouts, stacked_rows(): blocks = jnp.transpose(full.reshape(-1, in_rows, 2, model), (0, 2, 1, 3))  43.4 us
    dot_general x6, matrix products, rows_product(): lax.dot_general(left, right, (((0,), (0,)), ((), ())), preferred_element_...  41.1 us
  transfers between devices with their start and end apart: 55, of which 28 were waited for; matrix products, arithmetic and copies ran while one was open for 37% of the time, Pallas kernels for 16%

profile of v2, /device:TPU:0, one launch (start us, length us, event | category | flops | bytes accessed | tf_op | source)
XLA Modules:
  0.0 948.3 jit_solution(6937714711639470298)
XLA Ops:
  24.0 93.1 %all-gather.15.cloned.1.call-done = bf16[1,1536,6448]{2,1,0:T(8,128)(2,1)} async-done(((bf16[1,192,6448]{2,1,0:T(8,128)(2,1)}), bf16[1,1536,6448]{2,1,0:T(8,128)(2,1)}) %all-gather.15.cloned.1.call-update) | async-done | bytes 19808272 | tf_op jit(solution)/shard_map/all_gather | solution.py:424
  117.0 5.9 fusion.105
  133.5 14.4 %scan_fwd.2 = (f32[256,3072]{1,0:T(8,128)}, f32[3072,128]{1,0:T(8,128)}, f32[256,256]{1,0:T(8,128)}) custom-call(bf16[256,3328]{1,0:T(8,128)(2,1)} %slice.461.conv_ref.conv_bc_ref, bf16[256,3328]{1,0:T(8,128)(2,1)} %slice.461.conv_ref.conv_bc_ref, f32[8,3328]{1,0:T(8,128)} %pad_convert_fusion.1.halo_ref.halo_bc_ref, ...), custom_call_target="tpu_custom_call" | custom-call | tf_op jit(solution)/shard_map/scan_fwd/pallas_call | solution.py:317
  150.4 4.2 collective-permute-start.4
  158.3 5.3 collective-permute-done.4
  165.7 5.1 collective-permute-start.5
  174.0 5.4 collective-permute-done.5
  181.0 4.6 collective-permute-start.2
  190.4 4.7 collective-permute-done.2
  196.1 4.9 collective-permute-start.3
  201.0 7.9 fusion.14.gate_ref
  209.0 13.6 %all-gather.7.cloned.1.call-done = bf16[1536,6448]{1,0:T(8,128)(2,1)} async-done(((bf16[192,6448]{1,0:T(8,128)(2,1)}), bf16[1536,6448]{1,0:T(8,128)(2,1)}) %all-gather.7.cloned.1.call-update) | async-done | bytes 19808272 | tf_op jit(solution)/shard_map/all_gather | solution.py:424
  222.5 8.2 slice.468
  230.7 21.8 %reshape.398 = bf16[8,192,2,1536]{3,2,1,0:T(2,128)(2,1)} reshape(bf16[1536,3072]{1,0:T(8,128)(2,1)} %slice.468) | data formatting | bytes 18874368 | tf_op jit(solution)/shard_map/reshape | solution.py:510
  252.5 9.2 copy.215
  263.6 11.9 %gate_fwd.2 = (f32[256,3072]{1,0:T(8,128)}, bf16[256,3072]{1,0:T(8,128)(2,1)}) custom-call(f32[256,3072]{1,0:T(8,128)} %get-tuple-element.47.y_ref, f32[256,3072]{1,0:T(8,128)} %fusion.14.gate_ref, bf16[3072,128]{1,0:T(8,128)(2,1)} %copy-done.10, f32[256,256]{1,0:T(8,128)} %get-tuple-element.49.bc_ref, f32[12,256,8]{2,1,0:T(8,128)} %copy.213.col_ref, ...), custom_call_target="tpu_custom_call" | custom-call | tf_op jit(solution)/shard_map/gate_fwd/pallas_call | solution.py:330
  275.6 5.9 multiply_reduce_fusion.4
  286.5 5.9 fusion.106
  303.0 14.7 %scan_fwd.3 = (f32[256,3072]{1,0:T(8,128)}, f32[3072,128]{1,0:T(8,128)}, f32[256,256]{1,0:T(8,128)}) custom-call(bf16[256,3328]{1,0:T(8,128)(2,1)} %slice.470.conv_ref.conv_bc_ref, bf16[256,3328]{1,0:T(8,128)(2,1)} %slice.470.conv_ref.conv_bc_ref, f32[8,3328]{1,0:T(8,128)} %pad_convert_fusion.halo_ref.halo_bc_ref, ...), custom_call_target="tpu_custom_call" | custom-call | tf_op jit(solution)/shard_map/scan_fwd/pallas_call | solution.py:317
  328.3 5.2 collective-permute-done.11
  335.5 5.1 collective-permute-start.12
  340.7 8.2 slice.477
  348.9 21.6 %reshape.401 = bf16[8,192,2,1536]{3,2,1,0:T(2,128)(2,1)} reshape(bf16[1536,3072]{1,0:T(8,128)(2,1)} %slice.477) | data formatting | bytes 18874368 | tf_op jit(solution)/shard_map/reshape | solution.py:510
  370.5 10.2 %copy.223 = bf16[8,2,192,1536]{3,2,1,0:T(8,128)(2,1)} copy(bf16[8,2,192,1536]{3,1,2,0:T(2,128)(2,1)} %bitcast.231) | data formatting | bytes 18874368 | tf_op jit(solution)/shard_map/transpose | solution.py:510
  386.2 8.1 convolution_bitcast_fusion.dn_ref
  399.6 7.9 fusion.10.gate_ref
  407.6 4.2 collective-permute-done.10
  412.7 11.3 %gate_fwd.3 = (f32[256,3072]{1,0:T(8,128)}, bf16[256,3072]{1,0:T(8,128)(2,1)}) custom-call(f32[256,3072]{1,0:T(8,128)} %get-tuple-element.51.y_ref, f32[256,3072]{1,0:T(8,128)} %fusion.10.gate_ref, bf16[3072,128]{1,0:T(8,128)(2,1)} %copy-done.11, f32[256,256]{1,0:T(8,128)} %get-tuple-element.53.bc_ref, f32[12,256,8]{2,1,0:T(8,128)} %copy.221.col_ref, ...), custom_call_target="tpu_custom_call" | custom-call | tf_op jit(solution)/shard_map/gate_fwd/pallas_call | solution.py:330
  424.1 23.2 %gate_bwd.2 = (f32[256,3072]{1,0:T(8,128)}, bf16[256,3072]{1,0:T(8,128)(2,1)}, f32[1,3072]{1,0:T(1,128)}, f32[3072,128]{1,0:T(8,128)}) custom-call(f32[256,3072]{1,0:T(8,128)} %get-tuple-element.55.ssm_ref, f32[256,3072]{1,0:T(8,128)} %fusion.10.gate_ref, f32[256,3072]{1,0:T(8,128)} %convolution_bitcast_fusion.dn_ref, ...), custom_call_target="tpu_custom_call" | custom-call | tf_op jit(solution)/shard_map/gate_bwd/pallas_call | solution.py:345
  451.4 11.8 %collective-permute-done.14 = bf16[1536,128]{1,0:T(8,128)(2,1)S(1)} collective-permute-done((bf16[1536,128]{1,0:T(8,128)(2,1)S(1)}, bf16[1536,128]{1,0:T(8,128)(2,1)S(1)}, u32[]{:S(2)}, u32[]{:S(2)}) %collective-permute-start.14) | collective-permute-done | bytes 393248 | tf_op jit(solution)/shard_map/ppermute | solution.py:378
  464.8 6.8 collective-permute-done.17
  471.7 4.8 collective-permute-done.15
  480.8 11.3 %collective-permute-done.18 = bf16[1536,128]{1,0:T(8,128)(2,1)} collective-permute-done((bf16[1536,128]{1,0:T(8,128)(2,1)}, bf16[1536,128]{1,0:T(8,128)(2,1)}, u32[]{:S(2)}, u32[]{:S(2)}) %collective-permute-start.18) | collective-permute-done | bytes 393248 | tf_op jit(solution)/shard_map/ppermute | solution.py:378
  494.6 7.9 fusion.8
  505.3 26.9 %scan_bwd.2 = (f32[256,3072]{1,0:T(8,128)}, f32[8,3072]{1,0:T(8,128)}, f32[8,3072]{1,0:T(8,128)}, f32[256,256]{1,0:T(8,128)}, f32[8,256]{1,0:T(8,128)}, /*index=...) custom-call(bf16[256,3328]{1,0:T(8,128)(2,1)} %slice.470.conv_ref.conv_bc_ref, ...), custom_call_target="tpu_custom_call" | custom-call | tf_op jit(solution)/shard_map/scan_bwd/pallas_call | solution.py:362
  544.6 6.2 multiply_reduce_fusion
  553.1 8.2 fusion.107.dn_ref
  561.3 23.0 %gate_bwd.3 = (f32[256,3072]{1,0:T(8,128)}, bf16[256,3072]{1,0:T(8,128)(2,1)}, f32[1,3072]{1,0:T(1,128)}, f32[3072,128]{1,0:T(8,128)}) custom-call(f32[256,3072]{1,0:T(8,128)} %get-tuple-element.66.ssm_ref, f32[256,3072]{1,0:T(8,128)} %fusion.14.gate_ref, f32[256,3072]{1,0:T(8,128)} %fusion.107.dn_ref, f32[1,3072]{1,0:T(1,128)} %get-tuple-element.152.gain_ref, ...), custom_call_target="tpu_custom_call" | custom-call | tf_op jit(solution)/shard_map/gate_bwd/pallas_call | solution.py:345
  592.4 4.4 all-to-all-start.5
  603.5 8.3 convolution_add_fusion
  613.1 5.3 all-to-all-done.5
  618.4 4.3 all-to-all-start.4
  629.6 6.9 fusion.38
  643.8 6.7 fusion.35
  653.5 7.9 fusion.12
  668.2 4.8 collective-permute-done.36
  678.2 4.5 all-to-all-start.6
  692.2 19.3 %collective-permute-done.23 = bf16[1536,128]{1,0:T(8,128)(2,1)S(1)} collective-permute-done((bf16[1536,128]{1,0:T(8,128)(2,1)S(1)}, bf16[1536,128]{1,0:T(8,128)(2,1)S(1)}, u32[]{:S(2)}, u32[]{:S(2)}) %collective-permute-start.23) | collective-permute-done | bytes 393248 | tf_op jit(solution)/shard_map/ppermute | solution.py:378
  711.6 10.0 %collective-permute-done.26 = bf16[1536,128]{1,0:T(8,128)(2,1)S(1)} collective-permute-done((bf16[1536,128]{1,0:T(8,128)(2,1)S(1)}, bf16[1536,128]{1,0:T(8,128)(2,1)S(1)}, u32[]{:S(2)}, u32[]{:S(2)}) %collective-permute-start.26) | collective-permute-done | bytes 393248 | tf_op jit(solution)/shard_map/ppermute | solution.py:378
  722.5 26.9 %scan_bwd.3 = (f32[256,3072]{1,0:T(8,128)}, f32[8,3072]{1,0:T(8,128)}, f32[8,3072]{1,0:T(8,128)}, f32[256,256]{1,0:T(8,128)}, f32[8,256]{1,0:T(8,128)}, /*index=...) custom-call(bf16[256,3328]{1,0:T(8,128)(2,1)} %slice.461.conv_ref.conv_bc_ref, ...), custom_call_target="tpu_custom_call" | custom-call | tf_op jit(solution)/shard_map/scan_bwd/pallas_call | solution.py:362
  755.8 4.3 all-to-all-start.1
  761.2 6.9 fusion.18
  772.8 8.4 all-to-all-done.1
  781.2 4.3 all-to-all-start
  788.9 7.0 convolution_convert_fusion
  799.6 6.9 all-to-all-done
  806.5 6.8 fusion.32
  817.6 9.4 multiply_reduce_fusion.1
  847.0 4.5 all-to-all-start.2
  857.9 7.4 collective-permute-done.32
  866.7 11.4 %all-to-all-done.2 = bf16[8,256,512]{2,1,0:T(8,128)(2,1)} async-done(((bf16[8,256,512]{2,1,0:T(8,128)(2,1)}), bf16[8,256,512]{2,1,0:T(8,128)(2,1)}, u32[]{:S(2)}, u32[]{:S(2)}) %all-to-all-start.2) | async-done | bytes 2097184 | tf_op jit(solution)/shard_map/all_to_all | solution.py:428
  878.1 6.9 fusion.22
  896.8 24.8 %reduce-scatter.7.cloned.1.call-done = bf16[384,422]{1,0:T(8,128)(2,1)} async-done(((bf16[1536,422]{1,0:T(8,128)(2,1)}), bf16[384,422]{1,0:T(8,128)(2,1)}) %reduce-scatter.7.cloned.1.call-update) | async-done | bytes 324112 | tf_op jit(solution)/shard_map/reduce_scatter | solution.py:442
  929.5 9.2 all-to-all-done.3
  (504 shorter events, 246.3 us)
Async XLA Ops:
  7.2 109.9 %all-gather.15.cloned.1.call-start = ((), (), s32[]{:S(2)}) async-start(), calls=%async_computation.20 | async-start | bytes 22560768 | tf_op jit(solution)/shard_map/all_gather | solution.py:424
  10.6 212.0 %all-gather.7.cloned.1.call-start = ((), (), s32[]{:S(2)}) async-start(), calls=%async_computation.12 | async-start | bytes 22560768 | tf_op jit(solution)/shard_map/all_gather | solution.py:424
  15.5 325.2 %all-gather.9.cloned.1.call-start = ((), (), s32[]{:S(2)}) async-start(), calls=%async_computation.13 | async-start | bytes 21233664 | tf_op jit(solution)/shard_map/all_gather | solution.py:424
  18.6 610.9 %all-gather.11.cloned.1.call-start = ((), (), s32[]{:S(2)}) async-start(), calls=%async_computation.14 | async-start | bytes 21233664 | tf_op jit(solution)/shard_map/all_gather | solution.py:424
  21.9 105.7 %copy-start.70 = (f32[48]{0:T(128)}, f32[48]{0:T(128)S(1)}, u32[]{:S(2)}) copy-start(f32[48]{0:T(128)S(1)} %get-tuple-element.158) | copy-start | bytes 580
  22.4 105.4 %copy-start.72 = (f32[48]{0:T(128)}, f32[48]{0:T(128)S(1)}, u32[]{:S(2)}) copy-start(f32[48]{0:T(128)S(1)} %get-tuple-element.156) | copy-start | bytes 580
  22.6 100.3 %copy-start.16 = (bf16[256,1536]{1,0:T(8,128)(2,1)}, bf16[256,1536]{1,0:T(8,128)(2,1)S(1)}, u32[]{:S(2)}) copy-start(bf16[256,1536]{1,0:T(8,128)(2,1)S(1)} %multiply_convert_fusion.1) | copy-start | bytes 2359300
  124.1 8.6 collective-permute-start
  150.4 13.2 %collective-permute-start.4 = (bf16[1536,128]{1,0:T(8,128)(2,1)}, bf16[1536,128]{1,0:T(8,128)(2,1)}, u32[]{:S(2)}, u32[]{:S(2)}) collective-permute-start(bf16[1536,128]{1,0:T(8,128)(2,1)} %get-tuple-element.121), channel_id=1, source_target_pairs={{0,1},{1,2},{2,3},{4,5},{5,6},{6,7},{8,9},{9,10},{10,11},{12,13},{... | collective-permute-start | bytes 1179656 | tf_op jit(solution)/shard_map/ppermute | solution.py:378
  155.5 17.7 %collective-permute-start.1 = (bf16[1536,128]{1,0:T(8,128)(2,1)}, bf16[1536,128]{1,0:T(8,128)(2,1)S(1)}, u32[]{:S(2)}, u32[]{:S(2)}) collective-permute-start(bf16[1536,128]{1,0:T(8,128)(2,1)} %get-tuple-element.122), channel_id=1, source_target_pairs={{0,1},{1,2},{2,3},{4,5},{5,6},{6,7},{8,9},{9,10},{10,11},{12,13},{... | collective-permute-start | bytes 1179656 | tf_op jit(solution)/shard_map/ppermute | solution.py:378
  165.7 13.7 %collective-permute-start.5 = (bf16[1536,128]{1,0:T(8,128)(2,1)}, bf16[1536,128]{1,0:T(8,128)(2,1)}, u32[]{:S(2)}, u32[]{:S(2)}) collective-permute-start(bf16[1536,128]{1,0:T(8,128)(2,1)} %add_convert_fusion.13), channel_id=1, source_target_pairs={{0,1},{1,2},{2,3},{4,5},{5,6},{6,7},{8,9},{9,10},{10,11},{12,13},{... | collective-permute-start | bytes 1179656 | tf_op jit(solution)/shard_map/ppermute | solution.py:378
  173.2 27.8 %copy-start.17 = (bf16[256,1536]{1,0:T(8,128)(2,1)S(1)}, bf16[256,1536]{1,0:T(8,128)(2,1)}, u32[]{:S(2)}) copy-start(bf16[256,1536]{1,0:T(8,128)(2,1)} %copy-done.16) | copy-start | bytes 2359300
  181.0 14.1 %collective-permute-start.2 = (bf16[1536,128]{1,0:T(8,128)(2,1)S(1)}, bf16[1536,128]{1,0:T(8,128)(2,1)S(1)}, u32[]{:S(2)}, u32[]{:S(2)}) collective-permute-start(bf16[1536,128]{1,0:T(8,128)(2,1)S(1)} %get-tuple-element.120), channel_id=1, source_target_pairs={{0,1},{1,2},{2,3},{4,5},{5,6},{6,7},{8,9},{9,10},{10,11},{12,13},{... | collective-permute-start | bytes 1179656 | tf_op jit(solution)/shard_map/ppermute | solution.py:378
  186.2 75.5 %collective-permute-start.6 = (bf16[1536,128]{1,0:T(8,128)(2,1)S(1)}, bf16[1536,128]{1,0:T(8,128)(2,1)}, u32[]{:S(2)}, u32[]{:S(2)}) collective-permute-start(bf16[1536,128]{1,0:T(8,128)(2,1)S(1)} %get-tuple-element.119), channel_id=1, source_target_pairs={{0,1},{1,2},{2,3},{4,5},{5,6},{6,7},{8,9},{9,10},{10,11},{12,13},{... | collective-permute-start | bytes 1179656 | tf_op jit(solution)/shard_map/ppermute | solution.py:378
  196.1 65.6 %collective-permute-start.3 = (bf16[1536,128]{1,0:T(8,128)(2,1)}, bf16[1536,128]{1,0:T(8,128)(2,1)S(1)}, u32[]{:S(2)}, u32[]{:S(2)}) collective-permute-start(bf16[1536,128]{1,0:T(8,128)(2,1)} %add_convert_fusion.14), channel_id=1, source_target_pairs={{0,1},{1,2},{2,3},{4,5},{5,6},{6,7},{8,9},{9,10},{10,11},{12,13},{... | collective-permute-start | bytes 1179656 | tf_op jit(solution)/shard_map/ppermute | solution.py:378
  281.5 269.3 %copy-start.9 = (f32[256,1536]{1,0:T(8,128)}, f32[256,1536]{1,0:T(8,128)S(1)}, u32[]{:S(2)}) copy-start(f32[256,1536]{1,0:T(8,128)S(1)} %get-tuple-element.162) | copy-start | bytes 4718596
  285.2 503.7 %all-gather.13.cloned.1.call-start = ((), (), s32[]{:S(2)}) async-start(), calls=%async_computation.15 | async-start | bytes 7077888 | tf_op jit(solution)/shard_map/all_gather | solution.py:424
  293.7 8.6 collective-permute-start.7
  320.3 13.2 %collective-permute-start.11 = (bf16[1536,128]{1,0:T(8,128)(2,1)}, bf16[1536,128]{1,0:T(8,128)(2,1)}, u32[]{:S(2)}, u32[]{:S(2)}) collective-permute-start(bf16[1536,128]{1,0:T(8,128)(2,1)} %get-tuple-element.117), channel_id=1, source_target_pairs={{0,1},{1,2},{2,3},{4,5},{5,6},{6,7},{8,9},{9,10},{10,11},{12,13},{... | collective-permute-start | bytes 1179656 | tf_op jit(solution)/shard_map/ppermute | solution.py:378
  324.9 56.0 %collective-permute-start.8 = (bf16[1536,128]{1,0:T(8,128)(2,1)}, bf16[1536,128]{1,0:T(8,128)(2,1)}, u32[]{:S(2)}, u32[]{:S(2)}) collective-permute-start(bf16[1536,128]{1,0:T(8,128)(2,1)} %get-tuple-element.118), channel_id=1, source_target_pairs={{0,1},{1,2},{2,3},{4,5},{5,6},{6,7},{8,9},{9,10},{10,11},{12,13},{... | collective-permute-start | bytes 1179656 | tf_op jit(solution)/shard_map/ppermute | solution.py:378
  335.5 45.3 %collective-permute-start.12 = (bf16[1536,128]{1,0:T(8,128)(2,1)}, bf16[1536,128]{1,0:T(8,128)(2,1)}, u32[]{:S(2)}, u32[]{:S(2)}) collective-permute-start(bf16[1536,128]{1,0:T(8,128)(2,1)} %add_convert_fusion.9), channel_id=1, source_target_pairs={{0,1},{1,2},{2,3},{4,5},{5,6},{6,7},{8,9},{9,10},{10,11},{12,13},{... | collective-permute-start | bytes 1179656 | tf_op jit(solution)/shard_map/ppermute | solution.py:378
  382.5 14.4 %collective-permute-start.9 = (bf16[1536,128]{1,0:T(8,128)(2,1)S(1)}, bf16[1536,128]{1,0:T(8,128)(2,1)S(1)}, u32[]{:S(2)}, u32[]{:S(2)}) collective-permute-start(bf16[1536,128]{1,0:T(8,128)(2,1)S(1)} %get-tuple-element.116), channel_id=1, source_target_pairs={{0,1},{1,2},{2,3},{4,5},{5,6},{6,7},{8,9},{9,10},{10,11},{12,13},{... | collective-permute-start | bytes 1179656 | tf_op jit(solution)/shard_map/ppermute | solution.py:378
  394.2 17.5 %collective-permute-start.13 = (bf16[1536,128]{1,0:T(8,128)(2,1)S(1)}, bf16[1536,128]{1,0:T(8,128)(2,1)S(1)}, u32[]{:S(2)}, u32[]{:S(2)}) collective-permute-start(bf16[1536,128]{1,0:T(8,128)(2,1)S(1)} %get-tuple-element.115), channel_id=1, source_target_pairs={{0,1},{1,2},{2,3},{4,5},{5,6},{6,7},{8,9},{9,10},{10,11},{12,13},{... | collective-permute-start | bytes 1179656 | tf_op jit(solution)/shard_map/ppermute | solution.py:378
  397.2 14.6 %collective-permute-start.10 = (bf16[1536,128]{1,0:T(8,128)(2,1)S(1)}, bf16[1536,128]{1,0:T(8,128)(2,1)S(1)}, u32[]{:S(2)}, u32[]{:S(2)}) collective-permute-start(bf16[1536,128]{1,0:T(8,128)(2,1)S(1)} %add_convert_fusion.10), channel_id=1, source_target_pairs={{0,1},{1,2},{2,3},{4,5},{5,6},{6,7},{8,9},{9,10},{10,11},{12,13},{... | collective-permute-start | bytes 1179656 | tf_op jit(solution)/shard_map/ppermute | solution.py:378
  448.8 14.4 %collective-permute-start.14 = (bf16[1536,128]{1,0:T(8,128)(2,1)S(1)}, bf16[1536,128]{1,0:T(8,128)(2,1)S(1)}, u32[]{:S(2)}, u32[]{:S(2)}) collective-permute-start(bf16[1536,128]{1,0:T(8,128)(2,1)S(1)} %get-tuple-element.113), channel_id=1, source_target_pairs={{1,0},{2,1},{3,2},{5,4},{6,5},{7,6},{9,8},{10,9},{11,10},{13,12},{... | collective-permute-start | bytes 1179656 | tf_op jit(solution)/shard_map/ppermute | solution.py:378
  450.1 21.5 %collective-permute-start.17 = (bf16[1536,128]{1,0:T(8,128)(2,1)S(1)}, bf16[1536,128]{1,0:T(8,128)(2,1)S(1)}, u32[]{:S(2)}, u32[]{:S(2)}) collective-permute-start(bf16[1536,128]{1,0:T(8,128)(2,1)S(1)} %get-tuple-element.114), channel_id=1, source_target_pairs={{1,0},{2,1},{3,2},{5,4},{6,5},{7,6},{9,8},{10,9},{11,10},{13,12},{... | collective-permute-start | bytes 1179656 | tf_op jit(solution)/shard_map/ppermute | solution.py:378
  463.5 13.0 %collective-permute-start.15 = (bf16[1536,128]{1,0:T(8,128)(2,1)S(1)}, bf16[1536,128]{1,0:T(8,128)(2,1)S(1)}, u32[]{:S(2)}, u32[]{:S(2)}) collective-permute-start(bf16[1536,128]{1,0:T(8,128)(2,1)S(1)} %add_convert_fusion.7), channel_id=1, source_target_pairs={{1,0},{2,1},{3,2},{5,4},{6,5},{7,6},{9,8},{10,9},{11,10},{13,12},{... | collective-permute-start | bytes 1179656 | tf_op jit(solution)/shard_map/ppermute | solution.py:378
  477.9 14.2 %collective-permute-start.18 = (bf16[1536,128]{1,0:T(8,128)(2,1)}, bf16[1536,128]{1,0:T(8,128)(2,1)}, u32[]{:S(2)}, u32[]{:S(2)}) collective-permute-start(bf16[1536,128]{1,0:T(8,128)(2,1)} %get-tuple-element.112), channel_id=1, source_target_pairs={{1,0},{2,1},{3,2},{5,4},{6,5},{7,6},{9,8},{10,9},{11,10},{13,12},{... | collective-permute-start | bytes 1179656 | tf_op jit(solution)/shard_map/ppermute | solution.py:378
  479.2 58.7 %copy-start.85 = (pred[256]{0:T(512)(128)(4,1)}, pred[256]{0:T(512)(128)(4,1)S(1)}, u32[]{:S(2)}) copy-start(pred[256]{0:T(512)(128)(4,1)S(1)} %iota_compare_fusion.6) | copy-start | bytes 772
  479.5 23.1 %collective-permute-start.16 = (bf16[1536,128]{1,0:T(8,128)(2,1)}, bf16[1536,128]{1,0:T(8,128)(2,1)S(1)}, u32[]{:S(2)}, u32[]{:S(2)}) collective-permute-start(bf16[1536,128]{1,0:T(8,128)(2,1)} %get-tuple-element.111), channel_id=1, source_target_pairs={{1,0},{2,1},{3,2},{5,4},{6,5},{7,6},{9,8},{10,9},{11,10},{13,12},{... | collective-permute-start | bytes 1179656 | tf_op jit(solution)/shard_map/ppermute | solution.py:378
  493.3 11.0 %collective-permute-start.19 = (bf16[1536,128]{1,0:T(8,128)(2,1)S(1)}, bf16[1536,128]{1,0:T(8,128)(2,1)S(1)}, u32[]{:S(2)}, u32[]{:S(2)}) collective-permute-start(bf16[1536,128]{1,0:T(8,128)(2,1)S(1)} %add_convert_fusion.4), channel_id=1, source_target_pairs={{1,0},{2,1},{3,2},{5,4},{6,5},{7,6},{9,8},{10,9},{11,10},{13,12},{... | collective-permute-start | bytes 1179656 | tf_op jit(solution)/shard_map/ppermute | solution.py:378
  536.1 6.0 collective-permute-start.20
  561.3 26.7 %copy-start.55 = (f32[1,3072]{1,0:T(1,128)S(1)}, f32[1,3072]{1,0:T(1,128)}, u32[]{:S(2)}) copy-start(f32[1,3072]{1,0:T(1,128)} %get-tuple-element.82) | copy-start | bytes 36868
  561.3 27.5 %copy-start.69 = (f32[48]{0:T(128)S(1)}, f32[48]{0:T(128)}, u32[]{:S(2)}) copy-start(f32[48]{0:T(128)} %get-tuple-element.145) | copy-start | bytes 580
  586.7 13.4 %collective-permute-start.21 = (bf16[1536,128]{1,0:T(8,128)(2,1)}, bf16[1536,128]{1,0:T(8,128)(2,1)}, u32[]{:S(2)}, u32[]{:S(2)}) collective-permute-start(bf16[1536,128]{1,0:T(8,128)(2,1)} %get-tuple-element.109), channel_id=1, source_target_pairs={{1,0},{2,1},{3,2},{5,4},{6,5},{7,6},{9,8},{10,9},{11,10},{13,12},{... | collective-permute-start | bytes 1179656 | tf_op jit(solution)/shard_map/ppermute | solution.py:378
  588.8 9.4 collective-permute-start.33
  592.4 26.0 %all-to-all-start.5 = ((bf16[8,256,384]{2,1,0:T(8,128)(2,1)}), bf16[8,256,384]{2,1,0:T(8,128)(2,1)}, u32[]{:S(2)}, u32[]{:S(2)}) async-start(bf16[8,256,384]{2,1,0:T(8,128)(2,1)} %bitcast.241), calls=%async_computation.7 | async-start | bytes 3145728 | tf_op jit(solution)/shard_map/all_to_all | solution.py:428
  596.8 28.8 %collective-permute-start.24 = (bf16[1536,128]{1,0:T(8,128)(2,1)}, bf16[1536,128]{1,0:T(8,128)(2,1)}, u32[]{:S(2)}, u32[]{:S(2)}) collective-permute-start(bf16[1536,128]{1,0:T(8,128)(2,1)} %get-tuple-element.110), channel_id=1, source_target_pairs={{1,0},{2,1},{3,2},{5,4},{6,5},{7,6},{9,8},{10,9},{11,10},{13,12},{... | collective-permute-start | bytes 1179656 | tf_op jit(solution)/shard_map/ppermute | solution.py:378
  598.1 24.6 %collective-permute-start.34 = (f32[168,128]{1,0:T(8,128)S(1)}, f32[168,128]{1,0:T(8,128)}, u32[]{:S(2)}, u32[]{:S(2)}) collective-permute-start(f32[168,128]{1,0:T(8,128)S(1)} %fusion.90), channel_id=1, source_target_pairs={{0,8},{4,12},{8,0},{12,4},{16,24},{20,28},{24,16},{28,20},{1,9},{5... | collective-permute-start | bytes 258056 | tf_op jit(solution)/shard_map/ppermute | solution.py:406
  602.1 23.5 %collective-permute-start.22 = (bf16[1536,128]{1,0:T(8,128)(2,1)}, bf16[1536,128]{1,0:T(8,128)(2,1)}, u32[]{:S(2)}, u32[]{:S(2)}) collective-permute-start(bf16[1536,128]{1,0:T(8,128)(2,1)} %add_convert_fusion.3), channel_id=1, source_target_pairs={{1,0},{2,1},{3,2},{5,4},{6,5},{7,6},{9,8},{10,9},{11,10},{13,12},{... | collective-permute-start | bytes 1179656 | tf_op jit(solution)/shard_map/ppermute | solution.py:378
  618.4 25.4 %all-to-all-start.4 = ((bf16[8,256,384]{2,1,0:T(8,128)(2,1)}), bf16[8,256,384]{2,1,0:T(8,128)(2,1)}, u32[]{:S(2)}, u32[]{:S(2)}) async-start(bf16[8,256,384]{2,1,0:T(8,128)(2,1)} %bitcast.240), calls=%async_computation.6 | async-start | bytes 3145728 | tf_op jit(solution)/shard_map/all_to_all | solution.py:428
  622.7 265.8 %reduce-scatter.9.cloned.1.call-start = ((), (), s32[]{:S(2)}) async-start(), calls=%async_computation.18 | async-start | bytes 2949120 | tf_op jit(solution)/shard_map/reduce_scatter | solution.py:442
  623.7 39.1 %collective-permute-start.35 = (f32[168,128]{1,0:T(8,128)S(1)}, f32[168,128]{1,0:T(8,128)S(1)}, u32[]{:S(2)}, u32[]{:S(2)}) collective-permute-start(f32[168,128]{1,0:T(8,128)S(1)} %fusion.130), channel_id=1, source_target_pairs={{0,16},{4,20},{8,24},{12,28},{16,0},{20,4},{24,8},{28,12},{1,17},{... | collective-permute-start | bytes 258056 | tf_op jit(solution)/shard_map/ppermute | solution.py:406
  628.1 60.2 %collective-permute-start.25 = (bf16[1536,128]{1,0:T(8,128)(2,1)}, bf16[1536,128]{1,0:T(8,128)(2,1)}, u32[]{:S(2)}, u32[]{:S(2)}) collective-permute-start(bf16[1536,128]{1,0:T(8,128)(2,1)} %get-tuple-element.108), channel_id=1, source_target_pairs={{1,0},{2,1},{3,2},{5,4},{6,5},{7,6},{9,8},{10,9},{11,10},{13,12},{... | collective-permute-start | bytes 1179656 | tf_op jit(solution)/shard_map/ppermute | solution.py:378
  663.4 9.6 %collective-permute-start.36 = (f32[168,128]{1,0:T(8,128)}, f32[168,128]{1,0:T(8,128)}, u32[]{:S(2)}, u32[]{:S(2)}) collective-permute-start(f32[168,128]{1,0:T(8,128)} %add.256), channel_id=1, source_target_pairs={{0,1},{1,0},{2,3},{3,2},{4,5},{5,4},{6,7},{7,6},{8,9},{9,8},{10,11... | collective-permute-start | bytes 258056 | tf_op jit(solution)/shard_map/ppermute | solution.py:406
  673.9 13.0 %collective-permute-start.37 = (f32[168,128]{1,0:T(8,128)S(1)}, f32[168,128]{1,0:T(8,128)S(1)}, u32[]{:S(2)}, u32[]{:S(2)}) collective-permute-start(f32[168,128]{1,0:T(8,128)S(1)} %add.257), channel_id=1, source_target_pairs={{0,2},{1,3},{2,0},{3,1},{4,6},{5,7},{6,4},{7,5},{8,10},{9,11},{10,... | collective-permute-start | bytes 258056 | tf_op jit(solution)/shard_map/ppermute | solution.py:406
  678.2 77.6 %all-to-all-start.6 = ((bf16[8,256,512]{2,1,0:T(8,128)(2,1)}), bf16[8,256,512]{2,1,0:T(8,128)(2,1)}, u32[]{:S(2)}, u32[]{:S(2)}) async-start(bf16[8,256,512]{2,1,0:T(8,128)(2,1)} %fusion.50), calls=%async_computation.9 | async-start | bytes 4194304 | tf_op jit(solution)/shard_map/all_to_all | solution.py:428
  687.0 24.6 %collective-permute-start.23 = (bf16[1536,128]{1,0:T(8,128)(2,1)S(1)}, bf16[1536,128]{1,0:T(8,128)(2,1)S(1)}, u32[]{:S(2)}, u32[]{:S(2)}) collective-permute-start(bf16[1536,128]{1,0:T(8,128)(2,1)S(1)} %copy-done.32), channel_id=1, source_target_pairs={{1,0},{2,1},{3,2},{5,4},{6,5},{7,6},{9,8},{10,9},{11,10},{13,12},{... | collective-permute-start | bytes 1179656 | tf_op jit(solution)/shard_map/ppermute | solution.py:378
  689.5 32.0 %collective-permute-start.26 = (bf16[1536,128]{1,0:T(8,128)(2,1)S(1)}, bf16[1536,128]{1,0:T(8,128)(2,1)S(1)}, u32[]{:S(2)}, u32[]{:S(2)}) collective-permute-start(bf16[1536,128]{1,0:T(8,128)(2,1)S(1)} %add_convert_fusion), channel_id=1, source_target_pairs={{1,0},{2,1},{3,2},{5,4},{6,5},{7,6},{9,8},{10,9},{11,10},{13,12},{... | collective-permute-start | bytes 1179656 | tf_op jit(solution)/shard_map/ppermute | solution.py:378
  753.6 33.2 %collective-permute-start.27 = (f32[3,3328]{1,0:T(4,128)}, f32[3,3328]{1,0:T(4,128)}, u32[]{:S(2)}, u32[]{:S(2)}) collective-permute-start(f32[3,3328]{1,0:T(4,128)} %pad_maximum_fusion.15), channel_id=1, source_target_pairs={{1,0},{2,1},{3,2},{5,4},{6,5},{7,6},{9,8},{10,9},{11,10},{13,12},{... | collective-permute-start | bytes 119816 | tf_op jit(solution)/shard_map/ppermute | solution.py:378
  755.8 25.3 %all-to-all-start.1 = ((bf16[8,256,384]{2,1,0:T(8,128)(2,1)}), bf16[8,256,384]{2,1,0:T(8,128)(2,1)}, u32[]{:S(2)}, u32[]{:S(2)}) async-start(bf16[8,256,384]{2,1,0:T(8,128)(2,1)} %bitcast.227), calls=%async_computation.1 | async-start | bytes 3145728 | tf_op jit(solution)/shard_map/all_to_all | solution.py:428
  760.2 129.4 %reduce-scatter.11.cloned.1.call-start = ((), (), s32[]{:S(2)}) async-start(), calls=%async_computation.19 | async-start | bytes 1966080 | tf_op jit(solution)/shard_map/reduce_scatter | solution.py:442
  781.2 25.3 %all-to-all-start = ((bf16[8,256,384]{2,1,0:T(8,128)(2,1)}), bf16[8,256,384]{2,1,0:T(8,128)(2,1)}, u32[]{:S(2)}, u32[]{:S(2)}) async-start(bf16[8,256,384]{2,1,0:T(8,128)(2,1)} %bitcast.229), calls=%async_computation | async-start | bytes 3145728 | tf_op jit(solution)/shard_map/all_to_all | solution.py:428
  785.5 110.2 %reduce-scatter.5.cloned.1.call-start = ((), (), s32[]{:S(2)}) async-start(), calls=%async_computation.16 | async-start | bytes 2949120 | tf_op jit(solution)/shard_map/reduce_scatter | solution.py:442
  828.4 2.8 collective-permute-start.28
  831.2 5.0 collective-permute-start.29
  836.9 4.8 collective-permute-start.30
  842.7 9.8 %collective-permute-start.31 = (f32[168,128]{1,0:T(8,128)S(1)}, f32[168,128]{1,0:T(8,128)S(1)}, u32[]{:S(2)}, u32[]{:S(2)}) collective-permute-start(f32[168,128]{1,0:T(8,128)S(1)} %add.251), channel_id=1, source_target_pairs={{0,1},{1,0},{2,3},{3,2},{4,5},{5,4},{6,7},{7,6},{8,9},{9,8},{10,11... | collective-permute-start | bytes 258056 | tf_op jit(solution)/shard_map/ppermute | solution.py:406
  847.0 31.1 %all-to-all-start.2 = ((bf16[8,256,512]{2,1,0:T(8,128)(2,1)}), bf16[8,256,512]{2,1,0:T(8,128)(2,1)}, u32[]{:S(2)}, u32[]{:S(2)}) async-start(bf16[8,256,512]{2,1,0:T(8,128)(2,1)} %fusion.48), calls=%async_computation.3 | async-start | bytes 4194304 | tf_op jit(solution)/shard_map/all_to_all | solution.py:428
  851.5 70.2 %reduce-scatter.7.cloned.1.call-start = ((), (), s32[]{:S(2)}) async-start(), calls=%async_computation.17 | async-start | bytes 1966080 | tf_op jit(solution)/shard_map/reduce_scatter | solution.py:442
  852.5 12.8 %collective-permute-start.32 = (f32[168,128]{1,0:T(8,128)S(1)}, f32[168,128]{1,0:T(8,128)S(1)}, u32[]{:S(2)}, u32[]{:S(2)}) collective-permute-start(f32[168,128]{1,0:T(8,128)S(1)} %add.252), channel_id=1, source_target_pairs={{0,2},{1,3},{2,0},{3,1},{4,6},{5,7},{6,4},{7,5},{8,10},{9,11},{10,... | collective-permute-start | bytes 258056 | tf_op jit(solution)/shard_map/ppermute | solution.py:406
  891.5 32.0 %all-to-all-start.7 = ((bf16[8,48,806]{2,1,0:T(8,128)(2,1)}), bf16[8,48,806]{2,1,0:T(8,128)(2,1)S(1)}, u32[]{:S(2)}, u32[]{:S(2)}) async-start(bf16[8,48,806]{2,1,0:T(8,128)(2,1)} %bitcast.64), calls=%async_computation.11 | async-start | bytes 1376256 | tf_op jit(solution)/shard_map/all_to_all | solution.py:473
  895.1 32.1 %copy-start.79 = (f32[1,48]{1,0:T(1,128)S(1)}, f32[1,48]{1,0:T(1,128)}, u32[]{:S(2)}) copy-start(f32[1,48]{1,0:T(1,128)} %get-tuple-element.142) | copy-start | bytes 580
  923.5 15.1 %all-to-all-start.3 = ((bf16[8,48,806]{2,1,0:T(8,128)(2,1)}), bf16[8,48,806]{2,1,0:T(8,128)(2,1)S(1)}, u32[]{:S(2)}, u32[]{:S(2)}) async-start(bf16[8,48,806]{2,1,0:T(8,128)(2,1)} %bitcast.47), calls=%async_computation.5 | async-start | bytes 1376256 | tf_op jit(solution)/shard_map/all_to_all | solution.py:473
  (79 other events, 395.5 us)
Sparse Core Ops, SparseCore 0:
  10.7 106.2 all-gather.14
  118.9 103.5 all-gather.6
  224.4 98.5 all-gather.8
  325.4 98.5 all-gather.10
  552.8 44.1 all-gather.12
  653.6 65.1 reduce-scatter.8
  770.3 38.5 reduce-scatter.10
  816.4 52.2 reduce-scatter.4
  887.2 34.3 reduce-scatter.6

commit v3 on v2

--- a/solution.py
+++ b/solution.py
@@ -442,33 +442,40 @@
     return lax.psum_scatter(flat, "ctx", scatter_dimension=0, tiled=True)
 
 
-def early_gradients(normed_all, grad_all, d_gate, gnormed):
-    fsdp_count, ctx_count = lax.axis_size("fsdp"), lax.axis_size("ctx")
-    rows = d_gate.shape[0]
-    width = DI // fsdp_count
-    gate_cols = to_owners(d_gate.reshape(rows, fsdp_count, width))
-    norm_cols = to_owners(gnormed.reshape(rows, fsdp_count, width))
-    part_gate = by_run(rows_product(normed_all, gate_cols))
-    part_out = rows_product(norm_cols, grad_all).astype(BF)
-    tile = width // ctx_count
-    model = part_out.shape[1]
-    part_out = jnp.transpose(part_out.reshape(ctx_count, tile, model // width, width), (0, 2, 1, 3))
-    part_out = part_out.reshape(ctx_count, -1, width)
+def gate_parts(normed_all, d_gate):
+    fsdp_count = lax.axis_size("fsdp")
+    return by_run(rows_product(normed_all, to_owners(d_gate.reshape(d_gate.shape[0], fsdp_count, -1))))
+
+
+def out_parts(norm_cols, grad_all):
+    ctx_count = lax.axis_size("ctx")
+    width, model = norm_cols.shape[1], grad_all.shape[1]
+    part = rows_product(norm_cols, grad_all).astype(BF)
+    part = part.reshape(ctx_count, width // ctx_count, model // width, width)
+    return jnp.transpose(part, (0, 2, 1, 3)).reshape(ctx_count, -1, width)
+
+
+def early_sum(part_gate, part_out, model):
     summed = run_sum(jnp.concatenate([part_gate, part_out], 1))
-    in_rows = part_gate.shape[1]
-    owned_out = jnp.transpose(summed[in_rows:].reshape(model // width, tile, width), (1, 0, 2))
-    return summed[:in_rows], owned_out.reshape(tile, model).astype(F32)
-
-
-def late_gradients(normed_all, d_x, d_small, gate_sum):
+    in_rows, width = part_gate.shape[1:]
+    owned_out = jnp.transpose(summed[in_rows:].reshape(model // width, -1, width), (1, 0, 2))
+    return summed[:in_rows], owned_out.reshape(-1, model).astype(F32)
+
+
+def rest_parts(normed_all, d_rest):
     fsdp_count = lax.axis_size("fsdp")
-    rows = d_x.shape[0]
-    width, extra = DI // fsdp_count, d_small.shape[1] // fsdp_count
-    split = jnp.concatenate([d_x.reshape(rows, fsdp_count, width), d_small.reshape(rows, fsdp_count, extra)], 2)
-    split = jnp.pad(split, ((0, 0), (0, 0), (0, -(width + extra) % 128)))
-    part = rows_product(normed_all, to_owners(split))[:, : width + extra]
-    rest_sum = run_sum(by_run(part))
-    both = jnp.concatenate([gate_sum, rest_sum], 1)
+    rows = d_rest.shape[0]
+    wide = d_rest[:, :DI].reshape(rows, fsdp_count, -1)
+    narrow = d_rest[:, DI:].reshape(rows, fsdp_count, -1)
+    width = wide.shape[2] + narrow.shape[2]
+    split = jnp.concatenate([wide, narrow, jnp.zeros((rows, fsdp_count, -width % 128), BF)], 2)
+    return by_run(rows_product(normed_all, to_owners(split))[:, :width])
+
+
+def late_sum(part_rest, gate_sum):
+    fsdp_count = lax.axis_size("fsdp")
+    width = gate_sum.shape[1]
+    both = jnp.concatenate([gate_sum, run_sum(part_rest)], 1)
     both = both.reshape(fsdp_count, -1, both.shape[1])
     both = lax.all_to_all(both, "fsdp", split_axis=0, concat_axis=0, tiled=True)
     both = jnp.transpose(both, (1, 0, 2))
@@ -500,23 +507,11 @@
     edge_count = CONV - 1
     order = jnp.arange(rows)
     lower = (order[:, None] >= order[None, :]).astype(F32)
-    in_rows = in_weight.shape[1]
     model = out_weight.shape[2]
-
-    def side_by_side(k):
-        return jnp.concatenate([out_weight[k, :in_rows], out_weight[k, in_rows:]], 1)
-
-    def stacked_rows(full):
-        blocks = jnp.transpose(full.reshape(-1, in_rows, 2, model), (0, 2, 1, 3))
-        return blocks.reshape(DI, model)
-
     first = gathered(in_weight[0])
-    middle = gathered(jnp.concatenate([side_by_side(0), in_weight[1, :, DI:]], 1))
-    last = gathered(jnp.concatenate([in_weight[1, :, :DI], side_by_side(1)], 1))
-    weights = [
-        (first[:, DI:], first[:, :DI], stacked_rows(middle[:, :DI])),
-        (middle[:, DI:], last[:, :DI], stacked_rows(last[:, DI:])),
-    ]
+    weights = [(first[:, DI:], first[:, :DI], gathered(out_weight[0]))]
+    for k in range(1, LAYERS):
+        weights.append((gathered(in_weight[k][:, DI:]), gathered(in_weight[k][:, :DI]), gathered(out_weight[k])))
     stream = activations
     kept = []
     for k in range(LAYERS):
@@ -542,7 +537,10 @@
         stream = stream + jnp.dot(gnormed, w_out, preferred_element_type=F32)
     grad_stream = cotangent
     token_rows = gathered(jnp.concatenate([kept[0][1], kept[1][1], cotangent.astype(BF)], 1))
-    collected = []
+    width = DI // lax.axis_size("fsdp")
+    norm_cols = to_owners(jnp.concatenate([kept[k][-1].reshape(rows, -1, width) for k in range(LAYERS)], 2))
+    norm_cols = [norm_cols[:, k * width : (k + 1) * width] for k in range(LAYERS)]
+    collected, owned_ins, waiting = [], [], None
     for k in reversed(range(LAYERS)):
         w_conv, w_gate, w_out = weights[k]
         (stream_in, normed, gate_in, conv_in, halo, raw_steps, steps, col, row, totals, skip, bias, bc,
@@ -553,7 +551,16 @@
         outgoing = carry(totals, local_grad, -1)
         normed_all = token_rows[:, k * model : (k + 1) * model]
         grad_all = token_rows[:, LAYERS * model :] if k == LAYERS - 1 else gathered(grad_bf)
-        gate_sum, owned_out = early_gradients(normed_all, grad_all, d_gate, gnormed)
+        part_gate = gate_parts(normed_all, d_gate)
+        part_out = out_parts(norm_cols[k], grad_all)
+        if waiting is None:
+            outgoing, part_gate, part_out, norm_cols = lax.optimization_barrier(
+                (outgoing, part_gate, part_out, norm_cols))
+        else:
+            outgoing, part_gate, part_out, part_rest = lax.optimization_barrier(
+                (outgoing, part_gate, part_out, waiting[0]))
+            owned_ins.append(late_sum(part_rest, waiting[1]))
+        gate_sum, owned_out = early_sum(part_gate, part_out, model)
         d_x, edge_x, gt_x, d_bc, edge_bc, gt_bc, colo, rowo, misc = scan_bwd(
             conv_in, halo, conv_weight[k], bias, col, row, skip, bc, d_ssm, incoming, outgoing)
         edges = jnp.concatenate([edge_x[:edge_count], edge_bc[:edge_count]], 1)
@@ -579,7 +586,7 @@
         _, pullback = jax.vjp(rms_norm, stream_in, norm_gain[k])
         d_stream, g_norm = pullback(d_normed)
         grad_stream = grad_stream + d_stream
-        owned_in = late_gradients(normed_all, d_rest[:, :DI], d_rest[:, DI:], gate_sum)
+        waiting = (rest_parts(normed_all, d_rest), gate_sum)
         small = [g_norm, taps_grad[:CONV].reshape(-1), taps_grad[CONV], g_bias, g_log, g_skip, g_gate.reshape(-1)]
         sizes = [part.shape[0] for part in small]
         flat = jnp.concatenate(small)
@@ -589,8 +596,9 @@
             parts.append(flat[at : at + size])
             at += size
         parts[1] = parts[1].reshape(CONV, CC)
-        collected.append((owned_in, owned_out, *parts))
-    collected = collected[::-1]
+        collected.append((owned_out, *parts))
+    owned_ins.append(late_sum(*waiting))
+    collected = [(owned_in, *entry) for owned_in, entry in zip(owned_ins, collected)][::-1]
     stacked = [jnp.stack([entry[member] for entry in collected], 0) for member in range(9)]
     return (stream, grad_stream, *stacked)
 

time: 960 us -> 930 us (0.969)
  local copies, waits for them, and re-layouts: 171 us -> 109 us
  waiting for transfers between devices: 288 us -> 311 us
    reshape x16 -> x13, local copies, waits for them, and re-layouts: 61.9 us -> 20.3 us  [the longest x4 7.37 us: out_parts(): part = part.reshape(ctx_count, width // ctx_count, model // width, width)]
    all_gather x5 -> x7, waiting for transfers between devices: 107 us -> 128 us  [gathered(): return lax.all_gather(value, 'fsdp', axis=0, tiled=True)]
    all_to_all x6 -> x5, waiting for transfers between devices: 33.6 us -> 14.2 us  [to_owners(): lax.all_to_all(jnp.transpose(split, (1, 0, 2)), 'fsdp', split_axis=0, con...]
    transpose x2 -> x0, local copies, waits for them, and re-layouts: 19.4 us -> none  [stacked_rows(): blocks = jnp.transpose(full.reshape(-1, in_rows, 2, model), (0, 2, 1, 3))]
    ppermute x28, waiting for transfers between devices: 93.6 us -> 108 us  [passed_along(): lax.ppermute(value, axis, [(source, source + steps) for source in range(i...]
    slice x23 -> x24, local copies, waits for them, and re-layouts: 26.8 us -> 22.5 us  [the longest x4 3.65 us: rest_parts(): return by_run(rows_product(normed_all, to_owners(split))[:, :width])]
    all_to_all x6 -> x5, starting transfers between devices: 26.3 us -> 22.2 us  [to_owners(): lax.all_to_all(jnp.transpose(split, (1, 0, 2)), 'fsdp', split_axis=0, con...]
  transfers between devices with their start and end apart: 55 -> 56, of which waited for: 28 -> 30; matrix products, arithmetic and copies ran while one was open for 37% -> 29% of each run, Pallas kernels for 16% -> 14%
where the time goes in v3:
time: 930 us; the launch traced here: 919 us
  waiting for transfers between devices  311 us (33%)
  Pallas kernels  153 us (16%)
  matrix products  137 us (15%)
  starting transfers between devices  126 us (14%)
  local copies, waits for them, and re-layouts  109 us (12%)
  other arithmetic  67.4 us (7%)
  between operations  16.2 us (2%)
    all_gather x7, waiting for transfers between devices, gathered(): return lax.all_gather(value, 'fsdp', axis=0, tiled=True)  128 us
    ppermute x28, waiting for transfers between devices, passed_along(): lax.ppermute(value, axis, [(source, source + steps) for source in range(i...  108 us
    ppermute x28, starting transfers between devices, passed_along(): lax.ppermute(value, axis, [(source, source + steps) for source in range(i...  76.4 us
    pallas_call x2, Pallas kernels, scan_bwd(): pl.pallas_call(scan_bwd_kernel, grid=(G,), in_specs=conv_specs(rows) + [f...  53.8 us
    dot_general x6, matrix products, right_transposed(): lax.dot_general(left, right, (((1,), (1,)), ((), ())), preferred_element_...  48.4 us
    pallas_call x2, Pallas kernels, gate_bwd(): pl.pallas_call(gate_bwd_kernel, grid=(2, G), in_specs=[block, block, bloc...  47.2 us
    dot_general x6, matrix products, rows_product(): lax.dot_general(left, right, (((0,), (0,)), ((), ())), preferred_element_...  41 us
    pallas_call x2, Pallas kernels, scan_fwd(): pl.pallas_call(scan_fwd_kernel, grid=(G,), in_specs=conv_specs(rows), out...  28.9 us
  transfers between devices with their start and end apart: 56, of which 30 were waited for; matrix products, arithmetic and copies ran while one was open for 29% of the time, Pallas kernels for 14%

profile of v3, /device:TPU:0, one launch (start us, length us, event | category | flops | bytes accessed | tf_op | source)
XLA Modules:
  0.0 919.5 jit_solution(5849134112618575282)
XLA Ops:
  7.2 5.1 slice_bitcast_fusion
  26.3 92.5 %all-gather.19.cloned.1.call-done = bf16[1,1536,6448]{2,1,0:T(8,128)(2,1)} async-done(((bf16[1,192,6448]{2,1,0:T(8,128)(2,1)}), bf16[1,1536,6448]{2,1,0:T(8,128)(2,1)}) %all-gather.19.cloned.1.call-update) | async-done | bytes 19808272 | tf_op jit(solution)/shard_map/all_gather | solution.py:424
  118.8 5.9 fusion.102
  135.1 14.4 %scan_fwd.2 = (f32[256,3072]{1,0:T(8,128)}, f32[3072,128]{1,0:T(8,128)}, f32[256,256]{1,0:T(8,128)}) custom-call(bf16[256,3328]{1,0:T(8,128)(2,1)} %slice.450.conv_ref.conv_bc_ref, bf16[256,3328]{1,0:T(8,128)(2,1)} %slice.450.conv_ref.conv_bc_ref, f32[8,3328]{1,0:T(8,128)} %pad_convert_fusion.1.halo_ref.halo_bc_ref, ...), custom_call_target="tpu_custom_call" | custom-call | tf_op jit(solution)/shard_map/scan_fwd/pallas_call | solution.py:317
  152.5 4.3 collective-permute-start.4
  160.7 5.2 collective-permute-done.4
  167.9 5.1 collective-permute-start.5
  175.4 6.3 collective-permute-done.5
  183.2 4.4 collective-permute-start.2
  191.6 5.4 collective-permute-done.2
  197.3 4.9 collective-permute-start.3
  202.2 8.0 fusion.14.gate_ref
  213.0 11.8 %gate_fwd.2 = (f32[256,3072]{1,0:T(8,128)}, bf16[256,3072]{1,0:T(8,128)(2,1)}) custom-call(f32[256,3072]{1,0:T(8,128)} %get-tuple-element.55.y_ref, f32[256,3072]{1,0:T(8,128)} %fusion.14.gate_ref, bf16[3072,128]{1,0:T(8,128)(2,1)} %copy-done.10, f32[256,256]{1,0:T(8,128)} %get-tuple-element.57.bc_ref, f32[12,256,8]{2,1,0:T(8,128)} %copy.205.col_ref, ...), custom_call_target="tpu_custom_call" | custom-call | tf_op jit(solution)/shard_map/gate_fwd/pallas_call | solution.py:330
  224.9 5.9 multiply_reduce_fusion.4
  235.8 9.3 %all-gather.11.cloned.1.call-done = bf16[1536,3376]{1,0:T(8,128)(2,1)} async-done(((bf16[192,3376]{1,0:T(8,128)(2,1)}), bf16[1536,3376]{1,0:T(8,128)(2,1)}) %all-gather.11.cloned.1.call-update) | async-done | bytes 10371088 | tf_op jit(solution)/shard_map/all_gather | solution.py:424
  245.0 5.9 fusion.103
  261.4 14.5 %scan_fwd.3 = (f32[256,3072]{1,0:T(8,128)}, f32[3072,128]{1,0:T(8,128)}, f32[256,256]{1,0:T(8,128)}) custom-call(bf16[256,3328]{1,0:T(8,128)(2,1)} %slice.458.conv_ref.conv_bc_ref, bf16[256,3328]{1,0:T(8,128)(2,1)} %slice.458.conv_ref.conv_bc_ref, f32[8,3328]{1,0:T(8,128)} %pad_convert_fusion.halo_ref.halo_bc_ref, ...), custom_call_target="tpu_custom_call" | custom-call | tf_op jit(solution)/shard_map/scan_fwd/pallas_call | solution.py:317
  278.9 4.3 collective-permute-start.11
  287.0 5.2 collective-permute-done.11
  294.3 5.1 collective-permute-start.12
  300.7 7.5 collective-permute-done.12
  310.5 4.4 collective-permute-start.9
  314.9 4.1 collective-permute-start.13
  319.0 5.3 collective-permute-done.9
  325.4 4.6 collective-permute-start.10
  330.0 8.6 fusion.104.gate_ref
  341.5 11.4 %gate_fwd.3 = (f32[256,3072]{1,0:T(8,128)}, bf16[256,3072]{1,0:T(8,128)(2,1)}) custom-call(f32[256,3072]{1,0:T(8,128)} %get-tuple-element.59.y_ref, f32[256,3072]{1,0:T(8,128)} %fusion.104.gate_ref, bf16[3072,128]{1,0:T(8,128)(2,1)} %copy-done.11, f32[256,256]{1,0:T(8,128)} %get-tuple-element.61.bc_ref, f32[12,256,8]{2,1,0:T(8,128)} %copy.212.col_ref, ...), custom_call_target="tpu_custom_call" | custom-call | tf_op jit(solution)/shard_map/gate_fwd/pallas_call | solution.py:330
  357.2 4.6 all-to-all-start.1
  361.8 4.7 all-gather.23.cloned.1.call-done
  366.5 8.0 fusion.dn_ref
  374.5 24.0 %gate_bwd.2 = (f32[256,3072]{1,0:T(8,128)}, bf16[256,3072]{1,0:T(8,128)(2,1)}, f32[1,3072]{1,0:T(1,128)}, f32[3072,128]{1,0:T(8,128)}) custom-call(f32[256,3072]{1,0:T(8,128)} %get-tuple-element.63.ssm_ref, f32[256,3072]{1,0:T(8,128)} %fusion.104.gate_ref, f32[256,3072]{1,0:T(8,128)} %fusion.dn_ref, f32[1,3072]{1,0:T(1,128)} %get-tuple-element.167.gain_ref, ...), custom_call_target="tpu_custom_call" | custom-call | tf_op jit(solution)/shard_map/gate_bwd/pallas_call | solution.py:345
  402.7 11.3 %collective-permute-done.14 = bf16[1536,128]{1,0:T(8,128)(2,1)S(1)} collective-permute-done((bf16[1536,128]{1,0:T(8,128)(2,1)S(1)}, bf16[1536,128]{1,0:T(8,128)(2,1)S(1)}, u32[]{:S(2)}, u32[]{:S(2)}) %collective-permute-start.14) | collective-permute-done | bytes 393248 | tf_op jit(solution)/shard_map/ppermute | solution.py:378
  415.6 6.8 collective-permute-done.17
  422.4 7.7 collective-permute-done.15
  437.2 4.3 all-to-all-start
  441.6 4.2 collective-permute-done.18
  448.5 8.0 fusion.105
  456.5 4.4 collective-permute-done.19
  465.6 14.2 %all-to-all-done = bf16[8,256,384]{2,1,0:T(8,128)(2,1)} async-done(((bf16[8,256,384]{2,1,0:T(8,128)(2,1)}), bf16[8,256,384]{2,1,0:T(8,128)(2,1)}, u32[]{:S(2)}, u32[]{:S(2)}) %all-to-all-start) | async-done | bytes 1572896 | tf_op jit(solution)/shard_map/all_to_all | solution.py:428
  479.7 22.0 %all-gather.15.cloned.1.call-done = bf16[2048,4608]{1,0:T(8,128)(2,1)} async-done(((bf16[256,4608]{1,0:T(8,128)(2,1)}), bf16[2048,4608]{1,0:T(8,128)(2,1)}) %all-gather.15.cloned.1.call-update) | async-done | bytes 18874384 | tf_op jit(solution)/shard_map/all_gather | solution.py:424
  501.7 6.7 fusion.28
  509.6 6.9 fusion.34
  520.2 26.9 %scan_bwd.2 = (f32[256,3072]{1,0:T(8,128)}, f32[8,3072]{1,0:T(8,128)}, f32[8,3072]{1,0:T(8,128)}, f32[256,256]{1,0:T(8,128)}, f32[8,256]{1,0:T(8,128)}, /*index=...) custom-call(bf16[256,3328]{1,0:T(8,128)(2,1)} %slice.458.conv_ref.conv_bc_ref, ...), custom_call_target="tpu_custom_call" | custom-call | tf_op jit(solution)/shard_map/scan_bwd/pallas_call | solution.py:362
  561.5 6.8 multiply_reduce_fusion
  577.6 8.2 fusion.4.dn_ref
  585.8 23.1 %gate_bwd.3 = (f32[256,3072]{1,0:T(8,128)}, bf16[256,3072]{1,0:T(8,128)(2,1)}, f32[1,3072]{1,0:T(1,128)}, f32[3072,128]{1,0:T(8,128)}) custom-call(f32[256,3072]{1,0:T(8,128)} %get-tuple-element.75.ssm_ref, f32[256,3072]{1,0:T(8,128)} %fusion.14.gate_ref, f32[256,3072]{1,0:T(8,128)} %fusion.4.dn_ref, f32[1,3072]{1,0:T(1,128)} %get-tuple-element.168.gain_ref, ...), custom_call_target="tpu_custom_call" | custom-call | tf_op jit(solution)/shard_map/gate_bwd/pallas_call | solution.py:345
  615.4 4.4 all-to-all-start.2
  630.2 11.5 %collective-permute-done.34 = f32[168,128]{1,0:T(8,128)S(1)} collective-permute-done((f32[168,128]{1,0:T(8,128)S(1)}, f32[168,128]{1,0:T(8,128)S(1)}, u32[]{:S(2)}, u32[]{:S(2)}) %collective-permute-start.34) | collective-permute-done | bytes 86048 | tf_op jit(solution)/shard_map/ppermute | solution.py:406
  650.2 23.0 %collective-permute-done.22 = bf16[1536,128]{1,0:T(8,128)(2,1)S(1)} collective-permute-done((bf16[1536,128]{1,0:T(8,128)(2,1)S(1)}, bf16[1536,128]{1,0:T(8,128)(2,1)S(1)}, u32[]{:S(2)}, u32[]{:S(2)}) %collective-permute-start.22) | collective-permute-done | bytes 393248 | tf_op jit(solution)/shard_map/ppermute | solution.py:378
  676.7 4.4 all-to-all-start.3
  681.1 8.3 fusion.43
  697.8 6.7 fusion.31
  707.6 7.5 collective-permute-done.26
  716.1 6.9 fusion.22
  727.3 6.9 convolution_convert_fusion
  738.2 8.0 fusion.12
  748.4 26.9 %scan_bwd.3 = (f32[256,3072]{1,0:T(8,128)}, f32[8,3072]{1,0:T(8,128)}, f32[8,3072]{1,0:T(8,128)}, f32[256,256]{1,0:T(8,128)}, f32[8,256]{1,0:T(8,128)}, /*index=...) custom-call(bf16[256,3328]{1,0:T(8,128)(2,1)} %slice.450.conv_ref.conv_bc_ref, ...), custom_call_target="tpu_custom_call" | custom-call | tf_op jit(solution)/shard_map/scan_bwd/pallas_call | solution.py:362
  798.6 4.5 all-to-all-start.4
  803.5 9.4 %multiply_reduce_fusion.1 = (f32[1536]{0:T(1024)S(1)}, f32[256]{0:T(256)}, f32[256,1536]{1,0:T(8,128)}) fusion(f32[256,1536]{1,0:T(8,128)S(1)} %copy-done, f32[256]{0:T(256)S(1)} %copy-done.59, f32[1536]{0:T(1024)S(1)} %copy-done.39, f32[256,1536]{1,0:T(8,128)} %fusion.12, bf16[1536,6448]{1,0:T(8,128)(2,1)} %bitcast.280, ...), kind=kOutput, calls=%fused_computation.64 | convolution fusion | flops 2661202176 | bytes 17078272 | tf_op jit(solution)/shard_map/dot_general | solution.py:420
  820.1 10.5 %collective-permute-done.29 = f32[168,128]{1,0:T(8,128)} collective-permute-done((f32[168,128]{1,0:T(8,128)}, f32[168,128]{1,0:T(8,128)}, u32[]{:S(2)}, u32[]{:S(2)}) %collective-permute-start.29) | collective-permute-done | bytes 86048 | tf_op jit(solution)/shard_map/ppermute | solution.py:406
  849.0 6.9 fusion.18
  868.6 24.8 %reduce-scatter.7.cloned.1.call-done = bf16[384,422]{1,0:T(8,128)(2,1)} async-done(((bf16[1536,422]{1,0:T(8,128)(2,1)}), bf16[384,422]{1,0:T(8,128)(2,1)}) %reduce-scatter.7.cloned.1.call-update) | async-done | bytes 324112 | tf_op jit(solution)/shard_map/reduce_scatter | solution.py:442
  895.2 3.7 all-to-all-start.5
  901.5 8.8 all-to-all-done.5
  (516 shorter events, 247.9 us)
Async XLA Ops:
  7.2 111.6 %all-gather.19.cloned.1.call-start = ((), (), s32[]{:S(2)}) async-start(), calls=%async_computation.19 | async-start | bytes 22560768 | tf_op jit(solution)/shard_map/all_gather | solution.py:424
  12.3 212.5 %all-gather.21.cloned.1.call-start = ((), (), s32[]{:S(2)}) async-start(), calls=%async_computation.20 | async-start | bytes 10616832 | tf_op jit(solution)/shard_map/all_gather | solution.py:424
  15.6 229.4 %all-gather.11.cloned.1.call-start = ((), (), s32[]{:S(2)}) async-start(), calls=%async_computation.11 | async-start | bytes 11943936 | tf_op jit(solution)/shard_map/all_gather | solution.py:424
  18.2 311.8 %all-gather.13.cloned.1.call-start = ((), (), s32[]{:S(2)}) async-start(), calls=%async_computation.12 | async-start | bytes 10616832 | tf_op jit(solution)/shard_map/all_gather | solution.py:424
  20.7 345.8 %all-gather.23.cloned.1.call-start = ((), (), s32[]{:S(2)}) async-start(), calls=%async_computation.21 | async-start | bytes 10616832 | tf_op jit(solution)/shard_map/all_gather | solution.py:424
  21.3 480.4 %all-gather.15.cloned.1.call-start = ((), (), s32[]{:S(2)}) async-start(), calls=%async_computation.13 | async-start | bytes 21233664 | tf_op jit(solution)/shard_map/all_gather | solution.py:424
  24.1 105.2 %copy-start.70 = (f32[48]{0:T(128)}, f32[48]{0:T(128)S(1)}, u32[]{:S(2)}) copy-start(f32[48]{0:T(128)S(1)} %get-tuple-element.174) | copy-start | bytes 580
  24.7 104.8 %copy-start.72 = (f32[48]{0:T(128)}, f32[48]{0:T(128)S(1)}, u32[]{:S(2)}) copy-start(f32[48]{0:T(128)S(1)} %get-tuple-element.172) | copy-start | bytes 580
  24.9 99.8 %copy-start.16 = (bf16[256,1536]{1,0:T(8,128)(2,1)}, bf16[256,1536]{1,0:T(8,128)(2,1)S(1)}, u32[]{:S(2)}) copy-start(bf16[256,1536]{1,0:T(8,128)(2,1)S(1)} %multiply_convert_fusion.1) | copy-start | bytes 2359300
  125.9 8.6 collective-permute-start
  152.5 13.3 %collective-permute-start.4 = (bf16[1536,128]{1,0:T(8,128)(2,1)}, bf16[1536,128]{1,0:T(8,128)(2,1)}, u32[]{:S(2)}, u32[]{:S(2)}) collective-permute-start(bf16[1536,128]{1,0:T(8,128)(2,1)} %get-tuple-element.137), channel_id=1, source_target_pairs={{0,1},{1,2},{2,3},{4,5},{5,6},{6,7},{8,9},{9,10},{10,11},{12,13},{... | collective-permute-start | bytes 1179656 | tf_op jit(solution)/shard_map/ppermute | solution.py:378
  157.9 17.6 %collective-permute-start.1 = (bf16[1536,128]{1,0:T(8,128)(2,1)}, bf16[1536,128]{1,0:T(8,128)(2,1)S(1)}, u32[]{:S(2)}, u32[]{:S(2)}) collective-permute-start(bf16[1536,128]{1,0:T(8,128)(2,1)} %get-tuple-element.138), channel_id=1, source_target_pairs={{0,1},{1,2},{2,3},{4,5},{5,6},{6,7},{8,9},{9,10},{10,11},{12,13},{... | collective-permute-start | bytes 1179656 | tf_op jit(solution)/shard_map/ppermute | solution.py:378
  167.9 13.8 %collective-permute-start.5 = (bf16[1536,128]{1,0:T(8,128)(2,1)}, bf16[1536,128]{1,0:T(8,128)(2,1)}, u32[]{:S(2)}, u32[]{:S(2)}) collective-permute-start(bf16[1536,128]{1,0:T(8,128)(2,1)} %add_convert_fusion.13), channel_id=1, source_target_pairs={{0,1},{1,2},{2,3},{4,5},{5,6},{6,7},{8,9},{9,10},{10,11},{12,13},{... | collective-permute-start | bytes 1179656 | tf_op jit(solution)/shard_map/ppermute | solution.py:378
  175.4 26.8 %copy-start.17 = (bf16[256,1536]{1,0:T(8,128)(2,1)S(1)}, bf16[256,1536]{1,0:T(8,128)(2,1)}, u32[]{:S(2)}) copy-start(bf16[256,1536]{1,0:T(8,128)(2,1)} %copy-done.16) | copy-start | bytes 2359300
  183.2 13.9 %collective-permute-start.2 = (bf16[1536,128]{1,0:T(8,128)(2,1)S(1)}, bf16[1536,128]{1,0:T(8,128)(2,1)S(1)}, u32[]{:S(2)}, u32[]{:S(2)}) collective-permute-start(bf16[1536,128]{1,0:T(8,128)(2,1)S(1)} %get-tuple-element.136), channel_id=1, source_target_pairs={{0,1},{1,2},{2,3},{4,5},{5,6},{6,7},{8,9},{9,10},{10,11},{12,13},{... | collective-permute-start | bytes 1179656 | tf_op jit(solution)/shard_map/ppermute | solution.py:378
  188.2 23.8 %collective-permute-start.6 = (bf16[1536,128]{1,0:T(8,128)(2,1)S(1)}, bf16[1536,128]{1,0:T(8,128)(2,1)S(1)}, u32[]{:S(2)}, u32[]{:S(2)}) collective-permute-start(bf16[1536,128]{1,0:T(8,128)(2,1)S(1)} %get-tuple-element.135), channel_id=1, source_target_pairs={{0,1},{1,2},{2,3},{4,5},{5,6},{6,7},{8,9},{9,10},{10,11},{12,13},{... | collective-permute-start | bytes 1179656 | tf_op jit(solution)/shard_map/ppermute | solution.py:378
  197.3 14.7 %collective-permute-start.3 = (bf16[1536,128]{1,0:T(8,128)(2,1)S(1)}, bf16[1536,128]{1,0:T(8,128)(2,1)S(1)}, u32[]{:S(2)}, u32[]{:S(2)}) collective-permute-start(bf16[1536,128]{1,0:T(8,128)(2,1)S(1)} %add_convert_fusion.14), channel_id=1, source_target_pairs={{0,1},{1,2},{2,3},{4,5},{5,6},{6,7},{8,9},{9,10},{10,11},{12,13},{... | collective-permute-start | bytes 1179656 | tf_op jit(solution)/shard_map/ppermute | solution.py:378
  252.1 8.6 collective-permute-start.7
  278.9 13.4 %collective-permute-start.11 = (bf16[1536,128]{1,0:T(8,128)(2,1)}, bf16[1536,128]{1,0:T(8,128)(2,1)}, u32[]{:S(2)}, u32[]{:S(2)}) collective-permute-start(bf16[1536,128]{1,0:T(8,128)(2,1)} %get-tuple-element.133), channel_id=1, source_target_pairs={{0,1},{1,2},{2,3},{4,5},{5,6},{6,7},{8,9},{9,10},{10,11},{12,13},{... | collective-permute-start | bytes 1179656 | tf_op jit(solution)/shard_map/ppermute | solution.py:378
  283.7 17.0 %collective-permute-start.8 = (bf16[1536,128]{1,0:T(8,128)(2,1)}, bf16[1536,128]{1,0:T(8,128)(2,1)}, u32[]{:S(2)}, u32[]{:S(2)}) collective-permute-start(bf16[1536,128]{1,0:T(8,128)(2,1)} %get-tuple-element.134), channel_id=1, source_target_pairs={{0,1},{1,2},{2,3},{4,5},{5,6},{6,7},{8,9},{9,10},{10,11},{12,13},{... | collective-permute-start | bytes 1179656 | tf_op jit(solution)/shard_map/ppermute | solution.py:378
  294.3 13.9 %collective-permute-start.12 = (bf16[1536,128]{1,0:T(8,128)(2,1)}, bf16[1536,128]{1,0:T(8,128)(2,1)}, u32[]{:S(2)}, u32[]{:S(2)}) collective-permute-start(bf16[1536,128]{1,0:T(8,128)(2,1)} %add_convert_fusion.9), channel_id=1, source_target_pairs={{0,1},{1,2},{2,3},{4,5},{5,6},{6,7},{8,9},{9,10},{10,11},{12,13},{... | collective-permute-start | bytes 1179656 | tf_op jit(solution)/shard_map/ppermute | solution.py:378
  310.5 13.9 %collective-permute-start.9 = (bf16[1536,128]{1,0:T(8,128)(2,1)S(1)}, bf16[1536,128]{1,0:T(8,128)(2,1)S(1)}, u32[]{:S(2)}, u32[]{:S(2)}) collective-permute-start(bf16[1536,128]{1,0:T(8,128)(2,1)S(1)} %get-tuple-element.132), channel_id=1, source_target_pairs={{0,1},{1,2},{2,3},{4,5},{5,6},{6,7},{8,9},{9,10},{10,11},{12,13},{... | collective-permute-start | bytes 1179656 | tf_op jit(solution)/shard_map/ppermute | solution.py:378
  314.9 24.7 %collective-permute-start.13 = (bf16[1536,128]{1,0:T(8,128)(2,1)}, bf16[1536,128]{1,0:T(8,128)(2,1)}, u32[]{:S(2)}, u32[]{:S(2)}) collective-permute-start(bf16[1536,128]{1,0:T(8,128)(2,1)} %get-tuple-element.131), channel_id=1, source_target_pairs={{0,1},{1,2},{2,3},{4,5},{5,6},{6,7},{8,9},{9,10},{10,11},{12,13},{... | collective-permute-start | bytes 1179656 | tf_op jit(solution)/shard_map/ppermute | solution.py:378
  325.4 14.1 %collective-permute-start.10 = (bf16[1536,128]{1,0:T(8,128)(2,1)}, bf16[1536,128]{1,0:T(8,128)(2,1)S(1)}, u32[]{:S(2)}, u32[]{:S(2)}) collective-permute-start(bf16[1536,128]{1,0:T(8,128)(2,1)} %add_convert_fusion.10), channel_id=1, source_target_pairs={{0,1},{1,2},{2,3},{4,5},{5,6},{6,7},{8,9},{9,10},{10,11},{12,13},{... | collective-permute-start | bytes 1179656 | tf_op jit(solution)/shard_map/ppermute | solution.py:378
  357.2 80.0 %all-to-all-start.1 = ((bf16[8,256,768]{2,1,0:T(8,128)(2,1)}), bf16[8,256,768]{2,1,0:T(8,128)(2,1)}, u32[]{:S(2)}, u32[]{:S(2)}) async-start(bf16[8,256,768]{2,1,0:T(8,128)(2,1)} %maximum_bitcast_fusion), calls=%async_computation.1 | async-start | bytes 6291456 | tf_op jit(solution)/shard_map/all_to_all | solution.py:428
  400.1 13.9 %collective-permute-start.14 = (bf16[1536,128]{1,0:T(8,128)(2,1)S(1)}, bf16[1536,128]{1,0:T(8,128)(2,1)S(1)}, u32[]{:S(2)}, u32[]{:S(2)}) collective-permute-start(bf16[1536,128]{1,0:T(8,128)(2,1)S(1)} %get-tuple-element.129), channel_id=1, source_target_pairs={{1,0},{2,1},{3,2},{5,4},{6,5},{7,6},{9,8},{10,9},{11,10},{13,12},{... | collective-permute-start | bytes 1179656 | tf_op jit(solution)/shard_map/ppermute | solution.py:378
  401.4 21.0 %collective-permute-start.17 = (bf16[1536,128]{1,0:T(8,128)(2,1)S(1)}, bf16[1536,128]{1,0:T(8,128)(2,1)S(1)}, u32[]{:S(2)}, u32[]{:S(2)}) collective-permute-start(bf16[1536,128]{1,0:T(8,128)(2,1)S(1)} %get-tuple-element.130), channel_id=1, source_target_pairs={{1,0},{2,1},{3,2},{5,4},{6,5},{7,6},{9,8},{10,9},{11,10},{13,12},{... | collective-permute-start | bytes 1179656 | tf_op jit(solution)/shard_map/ppermute | solution.py:378
  414.3 15.9 %collective-permute-start.15 = (bf16[1536,128]{1,0:T(8,128)(2,1)S(1)}, bf16[1536,128]{1,0:T(8,128)(2,1)S(1)}, u32[]{:S(2)}, u32[]{:S(2)}) collective-permute-start(bf16[1536,128]{1,0:T(8,128)(2,1)S(1)} %add_convert_fusion.7), channel_id=1, source_target_pairs={{1,0},{2,1},{3,2},{5,4},{6,5},{7,6},{9,8},{10,9},{11,10},{13,12},{... | collective-permute-start | bytes 1179656 | tf_op jit(solution)/shard_map/ppermute | solution.py:378
  431.5 14.2 %collective-permute-start.18 = (bf16[1536,128]{1,0:T(8,128)(2,1)}, bf16[1536,128]{1,0:T(8,128)(2,1)}, u32[]{:S(2)}, u32[]{:S(2)}) collective-permute-start(bf16[1536,128]{1,0:T(8,128)(2,1)} %get-tuple-element.128), channel_id=1, source_target_pairs={{1,0},{2,1},{3,2},{5,4},{6,5},{7,6},{9,8},{10,9},{11,10},{13,12},{... | collective-permute-start | bytes 1179656 | tf_op jit(solution)/shard_map/ppermute | solution.py:378
  432.8 121.4 %copy-start.90 = (pred[256]{0:T(512)(128)(4,1)}, pred[256]{0:T(512)(128)(4,1)S(1)}, u32[]{:S(2)}) copy-start(pred[256]{0:T(512)(128)(4,1)S(1)} %iota_compare_fusion.5) | copy-start | bytes 772
  435.9 20.6 %collective-permute-start.16 = (bf16[1536,128]{1,0:T(8,128)(2,1)}, bf16[1536,128]{1,0:T(8,128)(2,1)}, u32[]{:S(2)}, u32[]{:S(2)}) collective-permute-start(bf16[1536,128]{1,0:T(8,128)(2,1)} %get-tuple-element.127), channel_id=1, source_target_pairs={{1,0},{2,1},{3,2},{5,4},{6,5},{7,6},{9,8},{10,9},{11,10},{13,12},{... | collective-permute-start | bytes 1179656 | tf_op jit(solution)/shard_map/ppermute | solution.py:378
  437.2 42.5 %all-to-all-start = ((bf16[8,256,384]{2,1,0:T(8,128)(2,1)}), bf16[8,256,384]{2,1,0:T(8,128)(2,1)}, u32[]{:S(2)}, u32[]{:S(2)}) async-start(bf16[8,256,384]{2,1,0:T(8,128)(2,1)} %bitcast.233), calls=%async_computation | async-start | bytes 3145728 | tf_op jit(solution)/shard_map/all_to_all | solution.py:428
  441.5 285.7 %all-gather.17.cloned.1.call-start = ((), (), s32[]{:S(2)}) async-start(), calls=%async_computation.14 | async-start | bytes 7077888 | tf_op jit(solution)/shard_map/all_gather | solution.py:424
  447.0 13.9 %collective-permute-start.19 = (bf16[1536,128]{1,0:T(8,128)(2,1)S(1)}, bf16[1536,128]{1,0:T(8,128)(2,1)S(1)}, u32[]{:S(2)}, u32[]{:S(2)}) collective-permute-start(bf16[1536,128]{1,0:T(8,128)(2,1)S(1)} %add_convert_fusion.4), channel_id=1, source_target_pairs={{1,0},{2,1},{3,2},{5,4},{6,5},{7,6},{9,8},{10,9},{11,10},{13,12},{... | collective-permute-start | bytes 1179656 | tf_op jit(solution)/shard_map/ppermute | solution.py:378
  552.5 6.0 collective-permute-start.20
  570.2 262.9 %reduce-scatter.9.cloned.1.call-start = ((), (), s32[]{:S(2)}) async-start(), calls=%async_computation.17 | async-start | bytes 2949120 | tf_op jit(solution)/shard_map/reduce_scatter | solution.py:442
  570.3 72.9 %copy-start.60 = (bf16[512]{0:T(512)(128)(2,1)}, bf16[512]{0:T(512)(128)(2,1)S(1)}, u32[]{:S(2)}) copy-start(bf16[512]{0:T(512)(128)(2,1)S(1)} %pad.63.clone) | copy-start | bytes 3076
  611.5 16.1 %collective-permute-start.21 = (bf16[1536,128]{1,0:T(8,128)(2,1)}, bf16[1536,128]{1,0:T(8,128)(2,1)}, u32[]{:S(2)}, u32[]{:S(2)}) collective-permute-start(bf16[1536,128]{1,0:T(8,128)(2,1)} %get-tuple-element.125), channel_id=1, source_target_pairs={{1,0},{2,1},{3,2},{5,4},{6,5},{7,6},{9,8},{10,9},{11,10},{13,12},{... | collective-permute-start | bytes 1179656 | tf_op jit(solution)/shard_map/ppermute | solution.py:378
  612.7 37.4 %collective-permute-start.24 = (bf16[1536,128]{1,0:T(8,128)(2,1)}, bf16[1536,128]{1,0:T(8,128)(2,1)}, u32[]{:S(2)}, u32[]{:S(2)}) collective-permute-start(bf16[1536,128]{1,0:T(8,128)(2,1)} %get-tuple-element.126), channel_id=1, source_target_pairs={{1,0},{2,1},{3,2},{5,4},{6,5},{7,6},{9,8},{10,9},{11,10},{13,12},{... | collective-permute-start | bytes 1179656 | tf_op jit(solution)/shard_map/ppermute | solution.py:378
  615.4 61.2 %all-to-all-start.2 = ((bf16[8,256,384]{2,1,0:T(8,128)(2,1)}), bf16[8,256,384]{2,1,0:T(8,128)(2,1)}, u32[]{:S(2)}, u32[]{:S(2)}) async-start(bf16[8,256,384]{2,1,0:T(8,128)(2,1)} %bitcast.230), calls=%async_computation.2 | async-start | bytes 3145728 | tf_op jit(solution)/shard_map/all_to_all | solution.py:428
  620.0 5.8 collective-permute-start.33
  625.9 15.8 %collective-permute-start.34 = (f32[168,128]{1,0:T(8,128)S(1)}, f32[168,128]{1,0:T(8,128)S(1)}, u32[]{:S(2)}, u32[]{:S(2)}) collective-permute-start(f32[168,128]{1,0:T(8,128)S(1)} %fusion.85), channel_id=1, source_target_pairs={{0,8},{4,12},{8,0},{12,4},{16,24},{20,28},{24,16},{28,20},{1,9},{5... | collective-permute-start | bytes 258056 | tf_op jit(solution)/shard_map/ppermute | solution.py:406
  628.9 44.3 %collective-permute-start.22 = (bf16[1536,128]{1,0:T(8,128)(2,1)S(1)}, bf16[1536,128]{1,0:T(8,128)(2,1)S(1)}, u32[]{:S(2)}, u32[]{:S(2)}) collective-permute-start(bf16[1536,128]{1,0:T(8,128)(2,1)S(1)} %add_convert_fusion.3), channel_id=1, source_target_pairs={{1,0},{2,1},{3,2},{5,4},{6,5},{7,6},{9,8},{10,9},{11,10},{13,12},{... | collective-permute-start | bytes 1179656 | tf_op jit(solution)/shard_map/ppermute | solution.py:378
  641.7 4.6 collective-permute-start.35
  646.9 42.6 %collective-permute-start.36 = (f32[168,128]{1,0:T(8,128)}, f32[168,128]{1,0:T(8,128)}, u32[]{:S(2)}, u32[]{:S(2)}) collective-permute-start(f32[168,128]{1,0:T(8,128)} %add.252), channel_id=1, source_target_pairs={{0,1},{1,0},{2,3},{3,2},{4,5},{5,4},{6,7},{7,6},{8,9},{9,8},{10,11... | collective-permute-start | bytes 258056 | tf_op jit(solution)/shard_map/ppermute | solution.py:406
  675.4 19.7 %collective-permute-start.25 = (bf16[1536,128]{1,0:T(8,128)(2,1)}, bf16[1536,128]{1,0:T(8,128)(2,1)}, u32[]{:S(2)}, u32[]{:S(2)}) collective-permute-start(bf16[1536,128]{1,0:T(8,128)(2,1)} %get-tuple-element.124), channel_id=1, source_target_pairs={{1,0},{2,1},{3,2},{5,4},{6,5},{7,6},{9,8},{10,9},{11,10},{13,12},{... | collective-permute-start | bytes 1179656 | tf_op jit(solution)/shard_map/ppermute | solution.py:378
  676.7 39.4 %all-to-all-start.3 = ((bf16[8,256,512]{2,1,0:T(8,128)(2,1)}), bf16[8,256,512]{2,1,0:T(8,128)(2,1)}, u32[]{:S(2)}, u32[]{:S(2)}) async-start(bf16[8,256,512]{2,1,0:T(8,128)(2,1)} %maximum_bitcast_fusion.1), calls=%async_computation.3 | async-start | bytes 4194304 | tf_op jit(solution)/shard_map/all_to_all | solution.py:428
  681.1 179.7 %reduce-scatter.11.cloned.1.call-start = ((), (), s32[]{:S(2)}) async-start(), calls=%async_computation.18 | async-start | bytes 1966080 | tf_op jit(solution)/shard_map/reduce_scatter | solution.py:442
  691.0 55.1 %collective-permute-start.37 = (f32[168,128]{1,0:T(8,128)}, f32[168,128]{1,0:T(8,128)}, u32[]{:S(2)}, u32[]{:S(2)}) collective-permute-start(f32[168,128]{1,0:T(8,128)} %add.253), channel_id=1, source_target_pairs={{0,2},{1,3},{2,0},{3,1},{4,6},{5,7},{6,4},{7,5},{8,10},{9,11},{10,... | collective-permute-start | bytes 258056 | tf_op jit(solution)/shard_map/ppermute | solution.py:406
  693.8 13.9 %collective-permute-start.23 = (bf16[1536,128]{1,0:T(8,128)(2,1)S(1)}, bf16[1536,128]{1,0:T(8,128)(2,1)S(1)}, u32[]{:S(2)}, u32[]{:S(2)}) collective-permute-start(bf16[1536,128]{1,0:T(8,128)(2,1)S(1)} %get-tuple-element.123), channel_id=1, source_target_pairs={{1,0},{2,1},{3,2},{5,4},{6,5},{7,6},{9,8},{10,9},{11,10},{13,12},{... | collective-permute-start | bytes 1179656 | tf_op jit(solution)/shard_map/ppermute | solution.py:378
  696.3 18.8 %collective-permute-start.26 = (bf16[1536,128]{1,0:T(8,128)(2,1)S(1)}, bf16[1536,128]{1,0:T(8,128)(2,1)S(1)}, u32[]{:S(2)}, u32[]{:S(2)}) collective-permute-start(bf16[1536,128]{1,0:T(8,128)(2,1)S(1)} %add_convert_fusion), channel_id=1, source_target_pairs={{1,0},{2,1},{3,2},{5,4},{6,5},{7,6},{9,8},{10,9},{11,10},{13,12},{... | collective-permute-start | bytes 1179656 | tf_op jit(solution)/shard_map/ppermute | solution.py:378
  737.9 129.6 %reduce-scatter.5.cloned.1.call-start = ((), (), s32[]{:S(2)}) async-start(), calls=%async_computation.15 | async-start | bytes 2949120 | tf_op jit(solution)/shard_map/reduce_scatter | solution.py:442
  779.8 9.0 collective-permute-start.27
  798.6 50.4 %all-to-all-start.4 = ((bf16[8,256,512]{2,1,0:T(8,128)(2,1)}), bf16[8,256,512]{2,1,0:T(8,128)(2,1)}, u32[]{:S(2)}, u32[]{:S(2)}) async-start(bf16[8,256,512]{2,1,0:T(8,128)(2,1)} %maximum_bitcast_fusion.2), calls=%async_computation.5 | async-start | bytes 4194304 | tf_op jit(solution)/shard_map/all_to_all | solution.py:428
  803.1 90.2 %reduce-scatter.7.cloned.1.call-start = ((), (), s32[]{:S(2)}) async-start(), calls=%async_computation.16 | async-start | bytes 1966080 | tf_op jit(solution)/shard_map/reduce_scatter | solution.py:442
  813.6 1.3 collective-permute-start.28
  815.6 30.4 %copy-start.9 = (f32[256,1536]{1,0:T(8,128)S(1)}, f32[256,1536]{1,0:T(8,128)}, u32[]{:S(2)}) copy-start(f32[256,1536]{1,0:T(8,128)} %get-tuple-element.118) | copy-start | bytes 4718596
  815.6 14.9 %collective-permute-start.29 = (f32[168,128]{1,0:T(8,128)}, f32[168,128]{1,0:T(8,128)}, u32[]{:S(2)}, u32[]{:S(2)}) collective-permute-start(f32[168,128]{1,0:T(8,128)} %fusion.84), channel_id=1, source_target_pairs={{0,8},{4,12},{8,0},{12,4},{16,24},{20,28},{24,16},{28,20},{1,9},{5... | collective-permute-start | bytes 258056 | tf_op jit(solution)/shard_map/ppermute | solution.py:406
  831.5 5.3 collective-permute-start.30
  837.7 5.4 collective-permute-start.31
  843.2 5.8 collective-permute-start.32
  862.7 32.5 %all-to-all-start.6 = ((bf16[8,48,806]{2,1,0:T(8,128)(2,1)}), bf16[8,48,806]{2,1,0:T(8,128)(2,1)S(1)}, u32[]{:S(2)}, u32[]{:S(2)}) async-start(bf16[8,48,806]{2,1,0:T(8,128)(2,1)} %bitcast.55), calls=%async_computation.10 | async-start | bytes 1376256 | tf_op jit(solution)/shard_map/all_to_all | solution.py:480
  867.4 31.5 %copy-start.81 = (f32[1,48]{1,0:T(1,128)S(1)}, f32[1,48]{1,0:T(1,128)}, u32[]{:S(2)}) copy-start(f32[1,48]{1,0:T(1,128)} %get-tuple-element.158) | copy-start | bytes 580
  895.2 15.1 %all-to-all-start.5 = ((bf16[8,48,806]{2,1,0:T(8,128)(2,1)}), bf16[8,48,806]{2,1,0:T(8,128)(2,1)S(1)}, u32[]{:S(2)}, u32[]{:S(2)}) async-start(bf16[8,48,806]{2,1,0:T(8,128)(2,1)} %bitcast.51), calls=%async_computation.7 | async-start | bytes 1376256 | tf_op jit(solution)/shard_map/all_to_all | solution.py:480
  (85 other events, 458.8 us)
Sparse Core Ops, SparseCore 0:
  12.5 106.2 all-gather.18
  120.7 58.6 all-gather.20
  181.3 63.6 all-gather.10
  246.8 58.6 all-gather.12
  307.8 58.6 all-gather.22
  368.8 132.8 all-gather.14
  570.3 44.4 all-gather.16
  617.7 71.3 reduce-scatter.8
  738.0 34.4 reduce-scatter.10
  788.9 49.3 reduce-scatter.4
  858.1 35.1 reduce-scatter.6

commit v4 on v3

--- a/solution.py
+++ b/solution.py
@@ -462,14 +462,18 @@
     return summed[:in_rows], owned_out.reshape(-1, model).astype(F32)
 
 
-def rest_parts(normed_all, d_rest):
+def rest_owners(d_rest):
     fsdp_count = lax.axis_size("fsdp")
     rows = d_rest.shape[0]
     wide = d_rest[:, :DI].reshape(rows, fsdp_count, -1)
     narrow = d_rest[:, DI:].reshape(rows, fsdp_count, -1)
     width = wide.shape[2] + narrow.shape[2]
-    split = jnp.concatenate([wide, narrow, jnp.zeros((rows, fsdp_count, -width % 128), BF)], 2)
-    return by_run(rows_product(normed_all, to_owners(split))[:, :width])
+    return to_owners(jnp.concatenate([wide, narrow, jnp.zeros((rows, fsdp_count, -width % 128), BF)], 2))
+
+
+def rest_parts(normed_all, rest_cols):
+    width = (CC - DI + H + DI) // lax.axis_size("fsdp")
+    return by_run(rows_product(normed_all, rest_cols)[:, :width])
 
 
 def late_sum(part_rest, gate_sum):
@@ -536,10 +540,7 @@
                      incoming, ssm, gnormed))
         stream = stream + jnp.dot(gnormed, w_out, preferred_element_type=F32)
     grad_stream = cotangent
-    token_rows = gathered(jnp.concatenate([kept[0][1], kept[1][1], cotangent.astype(BF)], 1))
-    width = DI // lax.axis_size("fsdp")
-    norm_cols = to_owners(jnp.concatenate([kept[k][-1].reshape(rows, -1, width) for k in range(LAYERS)], 2))
-    norm_cols = [norm_cols[:, k * width : (k + 1) * width] for k in range(LAYERS)]
+    gnormed_cols = to_owners(kept[-1][-1].reshape(rows, lax.axis_size("fsdp"), -1))
     collected, owned_ins, waiting = [], [], None
     for k in reversed(range(LAYERS)):
         w_conv, w_gate, w_out = weights[k]
@@ -548,21 +549,30 @@
         grad_bf = grad_stream.astype(BF)
         d_gnormed = right_transposed(grad_bf, w_out)
         d_ssm, d_gate, g_gate, local_grad = gate_bwd(ssm, gate_in, d_gnormed, gate_gain[k][None, :], col, bc)
+        tokens = jnp.concatenate([normed, grad_bf], 1)
+        if waiting is not None:
+            local_grad, rest_cols = lax.optimization_barrier((local_grad, waiting[1]))
+            tokens, gate_sum = lax.optimization_barrier((tokens, waiting[2]))
+        tokens = gathered(tokens)
         outgoing = carry(totals, local_grad, -1)
-        normed_all = token_rows[:, k * model : (k + 1) * model]
-        grad_all = token_rows[:, LAYERS * model :] if k == LAYERS - 1 else gathered(grad_bf)
+        normed_all, grad_all = tokens[:, :model], tokens[:, model:]
         part_gate = gate_parts(normed_all, d_gate)
-        part_out = out_parts(norm_cols[k], grad_all)
+        part_out = out_parts(gnormed_cols, grad_all)
         if waiting is None:
-            outgoing, part_gate, part_out, norm_cols = lax.optimization_barrier(
-                (outgoing, part_gate, part_out, norm_cols))
+            outgoing, part_gate, part_out = lax.optimization_barrier((outgoing, part_gate, part_out))
         else:
+            part_rest = rest_parts(waiting[0], rest_cols)
             outgoing, part_gate, part_out, part_rest = lax.optimization_barrier(
-                (outgoing, part_gate, part_out, waiting[0]))
-            owned_ins.append(late_sum(part_rest, waiting[1]))
+                (outgoing, part_gate, part_out, part_rest))
+            owned_ins.append(late_sum(part_rest, gate_sum))
+        if k:
+            outgoing, next_gnormed = lax.optimization_barrier((outgoing, kept[k - 1][-1]))
+            gnormed_cols = to_owners(next_gnormed.reshape(rows, lax.axis_size("fsdp"), -1))
         gate_sum, owned_out = early_sum(part_gate, part_out, model)
         d_x, edge_x, gt_x, d_bc, edge_bc, gt_bc, colo, rowo, misc = scan_bwd(
             conv_in, halo, conv_weight[k], bias, col, row, skip, bc, d_ssm, incoming, outgoing)
+        if k:
+            d_x, gnormed_cols = lax.optimization_barrier((d_x, gnormed_cols))
         edges = jnp.concatenate([edge_x[:edge_count], edge_bc[:edge_count]], 1)
         edge_back = passed_along(edges, "ctx", -1)
         taps_grad = jnp.concatenate([gt_x, gt_bc], 1)
@@ -586,20 +596,21 @@
         _, pullback = jax.vjp(rms_norm, stream_in, norm_gain[k])
         d_stream, g_norm = pullback(d_normed)
         grad_stream = grad_stream + d_stream
-        waiting = (rest_parts(normed_all, d_rest), gate_sum)
+        waiting = (normed_all, rest_owners(d_rest), gate_sum)
         small = [g_norm, taps_grad[:CONV].reshape(-1), taps_grad[CONV], g_bias, g_log, g_skip, g_gate.reshape(-1)]
-        sizes = [part.shape[0] for part in small]
-        flat = jnp.concatenate(small)
-        flat = all_sum(jnp.pad(flat, (0, -flat.shape[0] % 1024)).reshape(-1, 128)).reshape(-1)
-        parts, at = [], 0
-        for size in sizes:
-            parts.append(flat[at : at + size])
-            at += size
-        parts[1] = parts[1].reshape(CONV, CC)
-        collected.append((owned_out, *parts))
-    owned_ins.append(late_sum(*waiting))
-    collected = [(owned_in, *entry) for owned_in, entry in zip(owned_ins, collected)][::-1]
-    stacked = [jnp.stack([entry[member] for entry in collected], 0) for member in range(9)]
+        collected.append((owned_out, small))
+    sizes = [part.shape[0] for part in collected[0][1]]
+    flat = jnp.concatenate([part for entry in collected[::-1] for part in entry[1]])
+    flat = jnp.pad(flat, (0, -flat.shape[0] % 1024)).reshape(-1, 128)
+    flat, part_rest = lax.optimization_barrier((flat, rest_parts(waiting[0], waiting[1])))
+    owned_ins.append(late_sum(part_rest, waiting[2]))
+    flat = all_sum(flat).reshape(-1)[: LAYERS * sum(sizes)].reshape(LAYERS, -1)
+    stacked = [jnp.stack(owned_ins[::-1], 0), jnp.stack([entry[0] for entry in collected[::-1]], 0)]
+    at = 0
+    for size in sizes:
+        stacked.append(flat[:, at : at + size])
+        at += size
+    stacked[3] = stacked[3].reshape(LAYERS, CONV, CC)
     return (stream, grad_stream, *stacked)
 
 

time: 930 us -> 901 us (0.969)
  starting transfers between devices: 126 us -> 114 us
    reduce_scatter x4, waiting for transfers between devices: 24.8 us -> 10.3 us  [run_sum(): return lax.psum_scatter(flat, 'ctx', scatter_dimension=0, tiled=True)]
    all_to_all x5 -> x6, waiting for transfers between devices: 14.2 us -> 28.2 us  [to_owners(): lax.all_to_all(jnp.transpose(split, (1, 0, 2)), 'fsdp', split_axis=0, con...]
    ppermute x10 -> x5, starting transfers between devices: 19.3 us -> 7.01 us  [all_sum(): lax.ppermute(value, axis, [(i, i ^ bit) for i in range(count)])]
    all_gather x7, waiting for transfers between devices: 128 us -> 138 us  [gathered(): return lax.all_gather(value, 'fsdp', axis=0, tiled=True)]
    ppermute x10 -> x5, waiting for transfers between devices: 26 us -> 20.3 us  [all_sum(): lax.ppermute(value, axis, [(i, i ^ bit) for i in range(count)])]
    all_to_all x5 -> x6, starting transfers between devices: 22.2 us -> 25.9 us  [to_owners(): lax.all_to_all(jnp.transpose(split, (1, 0, 2)), 'fsdp', split_axis=0, con...]
  transfers between devices with their start and end apart: 56 -> 52, of which waited for: 30 -> 31; matrix products, arithmetic and copies ran while one was open for 29% -> 28% of each run, Pallas kernels for 14% -> 17%
where the time goes in v4:
time: 901 us; the launch traced here: 890 us
  waiting for transfers between devices  311 us (35%)
  Pallas kernels  153 us (17%)
  matrix products  132 us (15%)
  starting transfers between devices  114 us (13%)
  local copies, waits for them, and re-layouts  107 us (12%)
  other arithmetic  58.3 us (6%)
  between operations  16.1 us (2%)
    all_gather x7, waiting for transfers between devices, gathered(): return lax.all_gather(value, 'fsdp', axis=0, tiled=True)  138 us
    ppermute x28, waiting for transfers between devices, passed_along(): lax.ppermute(value, axis, [(source, source + steps) for source in range(i...  107 us
    ppermute x28, starting transfers between devices, passed_along(): lax.ppermute(value, axis, [(source, source + steps) for source in range(i...  72.4 us
    pallas_call x2, Pallas kernels, scan_bwd(): pl.pallas_call(scan_bwd_kernel, grid=(G,), in_specs=conv_specs(rows) + [f...  54.1 us
    dot_general x6, matrix products, right_transposed(): lax.dot_general(left, right, (((1,), (1,)), ((), ())), preferred_element_...  47.7 us
    pallas_call x2, Pallas kernels, gate_bwd(): pl.pallas_call(gate_bwd_kernel, grid=(2, G), in_specs=[block, block, bloc...  46.2 us
    dot_general x6, matrix products, rows_product(): lax.dot_general(left, right, (((0,), (0,)), ((), ())), preferred_element_...  38.7 us
    pallas_call x2, Pallas kernels, scan_fwd(): pl.pallas_call(scan_fwd_kernel, grid=(G,), in_specs=conv_specs(rows), out...  29 us
  transfers between devices with their start and end apart: 52, of which 31 were waited for; matrix products, arithmetic and copies ran while one was open for 28% of the time, Pallas kernels for 17%

profile of v4, /device:TPU:0, one launch (start us, length us, event | category | flops | bytes accessed | tf_op | source)
XLA Modules:
  0.0 889.9 jit_solution(12026914945932879671)
XLA Ops:
  7.2 5.1 slice_bitcast_fusion
  26.3 92.5 %all-gather.19.cloned.1.call-done = bf16[1,1536,6448]{2,1,0:T(8,128)(2,1)} async-done(((bf16[1,192,6448]{2,1,0:T(8,128)(2,1)}), bf16[1,1536,6448]{2,1,0:T(8,128)(2,1)}) %all-gather.19.cloned.1.call-update) | async-done | bytes 19808272 | tf_op jit(solution)/shard_map/all_gather | solution.py:424
  118.8 5.9 fusion.105
  135.1 14.5 %scan_fwd.2 = (f32[256,3072]{1,0:T(8,128)}, f32[3072,128]{1,0:T(8,128)}, f32[256,256]{1,0:T(8,128)}) custom-call(bf16[256,3328]{1,0:T(8,128)(2,1)} %slice.416.conv_ref.conv_bc_ref, bf16[256,3328]{1,0:T(8,128)(2,1)} %slice.416.conv_ref.conv_bc_ref, f32[8,3328]{1,0:T(8,128)} %pad_convert_fusion.1.halo_ref.halo_bc_ref, ...), custom_call_target="tpu_custom_call" | custom-call | tf_op jit(solution)/shard_map/scan_fwd/pallas_call | solution.py:317
  152.6 4.3 collective-permute-start.4
  160.7 5.2 collective-permute-done.4
  167.9 5.1 collective-permute-start.5
  175.5 6.2 collective-permute-done.5
  183.2 4.4 collective-permute-start.2
  191.7 5.4 collective-permute-done.2
  197.4 4.6 collective-permute-start.3
  202.0 8.0 fusion.14.gate_ref
  213.1 11.8 %gate_fwd.2 = (f32[256,3072]{1,0:T(8,128)}, bf16[256,3072]{1,0:T(8,128)(2,1)}) custom-call(f32[256,3072]{1,0:T(8,128)} %get-tuple-element.64.y_ref, f32[256,3072]{1,0:T(8,128)} %fusion.14.gate_ref, bf16[3072,128]{1,0:T(8,128)(2,1)} %copy-done.11, f32[256,256]{1,0:T(8,128)} %get-tuple-element.66.bc_ref, f32[12,256,8]{2,1,0:T(8,128)} %copy.205.col_ref, ...), custom_call_target="tpu_custom_call" | custom-call | tf_op jit(solution)/shard_map/gate_fwd/pallas_call | solution.py:330
  224.9 5.9 multiply_reduce_fusion.4
  234.7 10.3 %all-gather.11.cloned.1.call-done = bf16[1536,3376]{1,0:T(8,128)(2,1)} async-done(((bf16[192,3376]{1,0:T(8,128)(2,1)}), bf16[1536,3376]{1,0:T(8,128)(2,1)}) %all-gather.11.cloned.1.call-update) | async-done | bytes 10371088 | tf_op jit(solution)/shard_map/all_gather | solution.py:424
  245.0 5.9 fusion.106
  261.5 14.5 %scan_fwd.3 = (f32[256,3072]{1,0:T(8,128)}, f32[3072,128]{1,0:T(8,128)}, f32[256,256]{1,0:T(8,128)}) custom-call(bf16[256,3328]{1,0:T(8,128)(2,1)} %slice.424.conv_ref.conv_bc_ref, bf16[256,3328]{1,0:T(8,128)(2,1)} %slice.424.conv_ref.conv_bc_ref, f32[8,3328]{1,0:T(8,128)} %pad_convert_fusion.halo_ref.halo_bc_ref, ...), custom_call_target="tpu_custom_call" | custom-call | tf_op jit(solution)/shard_map/scan_fwd/pallas_call | solution.py:317
  279.0 3.6 collective-permute-start.11
  286.5 5.2 collective-permute-done.11
  293.7 5.2 collective-permute-start.12
  300.1 7.2 collective-permute-done.12
  309.8 5.2 collective-permute-start.9
  314.9 8.9 %fusion.dn_ref = f32[256,3072]{1,0:T(8,128)} fusion(bf16[256,1536]{1,0:T(8,128)(2,1)} %convert_element_type.230, bf16[1,3072,1536]{2,1,0:T(8,128)(2,1)} %all-gather.23.cloned.1.call-done), kind=kOutput, calls=%fused_computation | convolution fusion | flops 2415919104 | bytes 13369344 | tf_op jit(solution)/shard_map/dot_general | solution.py:420
  323.9 3.7 collective-permute-start.13
  331.3 35.2 %all-gather.13.cloned.1.call-done = bf16[1536,3072]{1,0:T(8,128)(2,1)} async-done(((bf16[192,3072]{1,0:T(8,128)(2,1)}), bf16[1536,3072]{1,0:T(8,128)(2,1)}) %all-gather.13.cloned.1.call-update) | async-done | bytes 9437200 | tf_op jit(solution)/shard_map/all_gather | solution.py:424
  366.5 8.3 fusion.107.gate_ref
  376.9 11.5 %gate_fwd.3 = (f32[256,3072]{1,0:T(8,128)}, bf16[256,3072]{1,0:T(8,128)(2,1)}) custom-call(f32[256,3072]{1,0:T(8,128)} %get-tuple-element.68.y_ref, f32[256,3072]{1,0:T(8,128)} %fusion.107.gate_ref, bf16[3072,128]{1,0:T(8,128)(2,1)} %copy-done.12, f32[256,256]{1,0:T(8,128)} %get-tuple-element.70.bc_ref, f32[12,256,8]{2,1,0:T(8,128)} %copy.212.col_ref, ...), custom_call_target="tpu_custom_call" | custom-call | tf_op jit(solution)/shard_map/gate_fwd/pallas_call | solution.py:330
  388.4 23.3 %gate_bwd.2 = (f32[256,3072]{1,0:T(8,128)}, bf16[256,3072]{1,0:T(8,128)(2,1)}, f32[1,3072]{1,0:T(1,128)}, f32[3072,128]{1,0:T(8,128)}) custom-call(f32[256,3072]{1,0:T(8,128)} %get-tuple-element.72.ssm_ref, f32[256,3072]{1,0:T(8,128)} %fusion.107.gate_ref, f32[256,3072]{1,0:T(8,128)} %fusion.dn_ref, f32[1,3072]{1,0:T(1,128)} %get-tuple-element.182.gain_ref, ...), custom_call_target="tpu_custom_call" | custom-call | tf_op jit(solution)/shard_map/gate_bwd/pallas_call | solution.py:345
  416.6 11.3 %collective-permute-done.14 = bf16[1536,128]{1,0:T(8,128)(2,1)S(1)} collective-permute-done((bf16[1536,128]{1,0:T(8,128)(2,1)S(1)}, bf16[1536,128]{1,0:T(8,128)(2,1)S(1)}, u32[]{:S(2)}, u32[]{:S(2)}) %collective-permute-start.14) | collective-permute-done | bytes 393248 | tf_op jit(solution)/shard_map/ppermute | solution.py:378
  431.5 4.3 all-to-all-start
  436.4 7.8 collective-permute-done.15
  449.1 11.3 %collective-permute-done.18 = bf16[1536,128]{1,0:T(8,128)(2,1)S(1)} collective-permute-done((bf16[1536,128]{1,0:T(8,128)(2,1)S(1)}, bf16[1536,128]{1,0:T(8,128)(2,1)S(1)}, u32[]{:S(2)}, u32[]{:S(2)}) %collective-permute-start.18) | collective-permute-done | bytes 393248 | tf_op jit(solution)/shard_map/ppermute | solution.py:378
  464.0 3.6 all-to-all-start.1
  468.9 6.9 collective-permute-done.19
  477.8 6.7 fusion.30
  488.6 6.4 fusion.36
  500.7 4.4 all-to-all-start.2
  509.7 7.5 fusion.108
  517.1 27.2 %scan_bwd.2 = (f32[256,3072]{1,0:T(8,128)}, f32[8,3072]{1,0:T(8,128)}, f32[8,3072]{1,0:T(8,128)}, f32[256,256]{1,0:T(8,128)}, f32[8,256]{1,0:T(8,128)}, /*index=...) custom-call(bf16[256,3328]{1,0:T(8,128)(2,1)} %slice.424.conv_ref.conv_bc_ref, ...), custom_call_target="tpu_custom_call" | custom-call | tf_op jit(solution)/shard_map/scan_bwd/pallas_call | solution.py:362
  551.2 6.2 collective-permute-done.20
  561.0 6.8 multiply_reduce_fusion
  579.5 4.7 all-to-all-start.3
  584.3 8.0 fusion.4.dn_ref
  592.2 23.0 %gate_bwd.3 = (f32[256,3072]{1,0:T(8,128)}, bf16[256,3072]{1,0:T(8,128)(2,1)}, f32[1,3072]{1,0:T(1,128)}, f32[3072,128]{1,0:T(8,128)}) custom-call(f32[256,3072]{1,0:T(8,128)} %get-tuple-element.87.ssm_ref, f32[256,3072]{1,0:T(8,128)} %fusion.14.gate_ref, f32[256,3072]{1,0:T(8,128)} %fusion.4.dn_ref, f32[1,3072]{1,0:T(1,128)} %get-tuple-element.183.gain_ref, ...), custom_call_target="tpu_custom_call" | custom-call | tf_op jit(solution)/shard_map/gate_bwd/pallas_call | solution.py:345
  615.2 9.4 %all-to-all-done.3 = bf16[8,256,512]{2,1,0:T(8,128)(2,1)} async-done(((bf16[8,256,512]{2,1,0:T(8,128)(2,1)}), bf16[8,256,512]{2,1,0:T(8,128)(2,1)}, u32[]{:S(2)}, u32[]{:S(2)}) %all-to-all-start.3) | async-done | bytes 2097184 | tf_op jit(solution)/shard_map/all_to_all | solution.py:428
  628.7 11.3 %collective-permute-done.21 = bf16[1536,128]{1,0:T(8,128)(2,1)S(1)} collective-permute-done((bf16[1536,128]{1,0:T(8,128)(2,1)S(1)}, bf16[1536,128]{1,0:T(8,128)(2,1)S(1)}, u32[]{:S(2)}, u32[]{:S(2)}) %collective-permute-start.21) | collective-permute-done | bytes 393248 | tf_op jit(solution)/shard_map/ppermute | solution.py:378
  641.7 6.7 collective-permute-done.24
  648.4 4.5 collective-permute-done.22
  656.7 4.3 all-to-all-start.4
  667.4 6.9 fusion.24
  678.3 5.4 collective-permute-done.26
  685.8 6.8 fusion.33
  693.8 5.1 fusion.39
  706.4 7.7 fusion.12
  714.1 26.9 %scan_bwd.3 = (f32[256,3072]{1,0:T(8,128)}, f32[8,3072]{1,0:T(8,128)}, f32[8,3072]{1,0:T(8,128)}, f32[256,256]{1,0:T(8,128)}, f32[8,256]{1,0:T(8,128)}, /*index=...) custom-call(bf16[256,3328]{1,0:T(8,128)(2,1)} %slice.416.conv_ref.conv_bc_ref, ...), custom_call_target="tpu_custom_call" | custom-call | tf_op jit(solution)/shard_map/scan_bwd/pallas_call | solution.py:362
  761.5 4.5 all-to-all-start.5
  767.6 8.9 multiply_reduce_fusion.1
  776.7 15.9 %all-to-all-done.5 = bf16[8,256,512]{2,1,0:T(8,128)(2,1)} async-done(((bf16[8,256,512]{2,1,0:T(8,128)(2,1)}), bf16[8,256,512]{2,1,0:T(8,128)(2,1)}, u32[]{:S(2)}, u32[]{:S(2)}) %all-to-all-start.5) | async-done | bytes 2097184 | tf_op jit(solution)/shard_map/all_to_all | solution.py:428
  792.7 6.9 fusion.20
  805.7 5.9 collective-permute-done.29
  812.8 7.4 fusion.48
  841.9 9.5 %collective-permute-done.32 = f32[336,128]{1,0:T(8,128)} collective-permute-done((f32[336,128]{1,0:T(8,128)}, f32[336,128]{1,0:T(8,128)}, u32[]{:S(2)}, u32[]{:S(2)}) %collective-permute-start.32) | collective-permute-done | bytes 172064 | tf_op jit(solution)/shard_map/ppermute | solution.py:406
  853.7 10.3 %reduce-scatter.9.cloned.1.call-done = bf16[384,422]{1,0:T(8,128)(2,1)} async-done(((bf16[1536,422]{1,0:T(8,128)(2,1)}), bf16[384,422]{1,0:T(8,128)(2,1)}) %reduce-scatter.9.cloned.1.call-update) | async-done | bytes 324112 | tf_op jit(solution)/shard_map/reduce_scatter | solution.py:442
  874.8 6.0 all-to-all-done.6
  (502 shorter events, 230.8 us)
Async XLA Ops:
  7.2 111.6 %all-gather.19.cloned.1.call-start = ((), (), s32[]{:S(2)}) async-start(), calls=%async_computation.20 | async-start | bytes 22560768 | tf_op jit(solution)/shard_map/all_gather | solution.py:424
  12.3 212.5 %all-gather.21.cloned.1.call-start = ((), (), s32[]{:S(2)}) async-start(), calls=%async_computation.21 | async-start | bytes 10616832 | tf_op jit(solution)/shard_map/all_gather | solution.py:424
  15.6 229.4 %all-gather.11.cloned.1.call-start = ((), (), s32[]{:S(2)}) async-start(), calls=%async_computation.12 | async-start | bytes 11943936 | tf_op jit(solution)/shard_map/all_gather | solution.py:424
  18.1 296.8 %all-gather.23.cloned.1.call-start = ((), (), s32[]{:S(2)}) async-start(), calls=%async_computation.22 | async-start | bytes 10616832 | tf_op jit(solution)/shard_map/all_gather | solution.py:424
  18.8 347.8 %all-gather.13.cloned.1.call-start = ((), (), s32[]{:S(2)}) async-start(), calls=%async_computation.13 | async-start | bytes 10616832 | tf_op jit(solution)/shard_map/all_gather | solution.py:424
  21.3 456.5 %all-gather.15.cloned.1.call-start = ((), (), s32[]{:S(2)}) async-start(), calls=%async_computation.14 | async-start | bytes 14155776 | tf_op jit(solution)/shard_map/all_gather | solution.py:424
  24.1 105.2 %copy-start.78 = (f32[48]{0:T(128)}, f32[48]{0:T(128)S(1)}, u32[]{:S(2)}) copy-start(f32[48]{0:T(128)S(1)} %get-tuple-element.189) | copy-start | bytes 580
  24.7 104.9 %copy-start.80 = (f32[48]{0:T(128)}, f32[48]{0:T(128)S(1)}, u32[]{:S(2)}) copy-start(f32[48]{0:T(128)S(1)} %get-tuple-element.187) | copy-start | bytes 580
  24.9 99.8 %copy-start.17 = (bf16[256,1536]{1,0:T(8,128)(2,1)}, bf16[256,1536]{1,0:T(8,128)(2,1)S(1)}, u32[]{:S(2)}) copy-start(bf16[256,1536]{1,0:T(8,128)(2,1)S(1)} %multiply_convert_fusion.1) | copy-start | bytes 2359300
  125.9 8.5 collective-permute-start
  149.6 16.3 %copy-start.2 = (f32[3072,128]{1,0:T(8,128)S(1)}, f32[3072,128]{1,0:T(8,128)}, u32[]{:S(2)}) copy-start(f32[3072,128]{1,0:T(8,128)} %get-tuple-element.65) | copy-start | bytes 4718596
  152.6 13.3 %collective-permute-start.4 = (bf16[1536,128]{1,0:T(8,128)(2,1)}, bf16[1536,128]{1,0:T(8,128)(2,1)}, u32[]{:S(2)}, u32[]{:S(2)}) collective-permute-start(bf16[1536,128]{1,0:T(8,128)(2,1)} %get-tuple-element.155), channel_id=1, source_target_pairs={{0,1},{1,2},{2,3},{4,5},{5,6},{6,7},{8,9},{9,10},{10,11},{12,13},{... | collective-permute-start | bytes 1179656 | tf_op jit(solution)/shard_map/ppermute | solution.py:378
  157.9 17.6 %collective-permute-start.1 = (bf16[1536,128]{1,0:T(8,128)(2,1)}, bf16[1536,128]{1,0:T(8,128)(2,1)S(1)}, u32[]{:S(2)}, u32[]{:S(2)}) collective-permute-start(bf16[1536,128]{1,0:T(8,128)(2,1)} %get-tuple-element.156), channel_id=1, source_target_pairs={{0,1},{1,2},{2,3},{4,5},{5,6},{6,7},{8,9},{9,10},{10,11},{12,13},{... | collective-permute-start | bytes 1179656 | tf_op jit(solution)/shard_map/ppermute | solution.py:378
  167.9 13.8 %collective-permute-start.5 = (bf16[1536,128]{1,0:T(8,128)(2,1)}, bf16[1536,128]{1,0:T(8,128)(2,1)}, u32[]{:S(2)}, u32[]{:S(2)}) collective-permute-start(bf16[1536,128]{1,0:T(8,128)(2,1)} %add_convert_fusion.13), channel_id=1, source_target_pairs={{0,1},{1,2},{2,3},{4,5},{5,6},{6,7},{8,9},{9,10},{10,11},{12,13},{... | collective-permute-start | bytes 1179656 | tf_op jit(solution)/shard_map/ppermute | solution.py:378
  175.5 26.5 %copy-start.18 = (bf16[256,1536]{1,0:T(8,128)(2,1)S(1)}, bf16[256,1536]{1,0:T(8,128)(2,1)}, u32[]{:S(2)}) copy-start(bf16[256,1536]{1,0:T(8,128)(2,1)} %copy-done.17) | copy-start | bytes 2359300
  183.2 13.9 %collective-permute-start.2 = (bf16[1536,128]{1,0:T(8,128)(2,1)S(1)}, bf16[1536,128]{1,0:T(8,128)(2,1)S(1)}, u32[]{:S(2)}, u32[]{:S(2)}) collective-permute-start(bf16[1536,128]{1,0:T(8,128)(2,1)S(1)} %get-tuple-element.154), channel_id=1, source_target_pairs={{0,1},{1,2},{2,3},{4,5},{5,6},{6,7},{8,9},{9,10},{10,11},{12,13},{... | collective-permute-start | bytes 1179656 | tf_op jit(solution)/shard_map/ppermute | solution.py:378
  188.3 23.8 %collective-permute-start.6 = (bf16[1536,128]{1,0:T(8,128)(2,1)S(1)}, bf16[1536,128]{1,0:T(8,128)(2,1)S(1)}, u32[]{:S(2)}, u32[]{:S(2)}) collective-permute-start(bf16[1536,128]{1,0:T(8,128)(2,1)S(1)} %get-tuple-element.153), channel_id=1, source_target_pairs={{0,1},{1,2},{2,3},{4,5},{5,6},{6,7},{8,9},{9,10},{10,11},{12,13},{... | collective-permute-start | bytes 1179656 | tf_op jit(solution)/shard_map/ppermute | solution.py:378
  197.4 14.7 %collective-permute-start.3 = (bf16[1536,128]{1,0:T(8,128)(2,1)S(1)}, bf16[1536,128]{1,0:T(8,128)(2,1)S(1)}, u32[]{:S(2)}, u32[]{:S(2)}) collective-permute-start(bf16[1536,128]{1,0:T(8,128)(2,1)S(1)} %add_convert_fusion.14), channel_id=1, source_target_pairs={{0,1},{1,2},{2,3},{4,5},{5,6},{6,7},{8,9},{9,10},{10,11},{12,13},{... | collective-permute-start | bytes 1179656 | tf_op jit(solution)/shard_map/ppermute | solution.py:378
  234.7 20.8 %copy-start.82 = (f32[48]{0:T(128)S(1)}, f32[48]{0:T(128)}, u32[]{:S(2)}) copy-start(f32[48]{0:T(128)} %get-tuple-element.188) | copy-start | bytes 580
  234.7 21.0 %copy-start.84 = (f32[48]{0:T(128)S(1)}, f32[48]{0:T(128)}, u32[]{:S(2)}) copy-start(f32[48]{0:T(128)} %get-tuple-element.186) | copy-start | bytes 580
  252.1 8.7 collective-permute-start.7
  279.0 12.7 %collective-permute-start.11 = (bf16[1536,128]{1,0:T(8,128)(2,1)}, bf16[1536,128]{1,0:T(8,128)(2,1)}, u32[]{:S(2)}, u32[]{:S(2)}) collective-permute-start(bf16[1536,128]{1,0:T(8,128)(2,1)} %get-tuple-element.151), channel_id=1, source_target_pairs={{0,1},{1,2},{2,3},{4,5},{5,6},{6,7},{8,9},{9,10},{10,11},{12,13},{... | collective-permute-start | bytes 1179656 | tf_op jit(solution)/shard_map/ppermute | solution.py:378
  283.0 17.0 %collective-permute-start.8 = (bf16[1536,128]{1,0:T(8,128)(2,1)}, bf16[1536,128]{1,0:T(8,128)(2,1)}, u32[]{:S(2)}, u32[]{:S(2)}) collective-permute-start(bf16[1536,128]{1,0:T(8,128)(2,1)} %get-tuple-element.152), channel_id=1, source_target_pairs={{0,1},{1,2},{2,3},{4,5},{5,6},{6,7},{8,9},{9,10},{10,11},{12,13},{... | collective-permute-start | bytes 1179656 | tf_op jit(solution)/shard_map/ppermute | solution.py:378
  293.7 13.6 %collective-permute-start.12 = (bf16[1536,128]{1,0:T(8,128)(2,1)}, bf16[1536,128]{1,0:T(8,128)(2,1)}, u32[]{:S(2)}, u32[]{:S(2)}) collective-permute-start(bf16[1536,128]{1,0:T(8,128)(2,1)} %add_convert_fusion.9), channel_id=1, source_target_pairs={{0,1},{1,2},{2,3},{4,5},{5,6},{6,7},{8,9},{9,10},{10,11},{12,13},{... | collective-permute-start | bytes 1179656 | tf_op jit(solution)/shard_map/ppermute | solution.py:378
  309.8 17.8 %collective-permute-start.9 = (bf16[1536,128]{1,0:T(8,128)(2,1)}, bf16[1536,128]{1,0:T(8,128)(2,1)}, u32[]{:S(2)}, u32[]{:S(2)}) collective-permute-start(bf16[1536,128]{1,0:T(8,128)(2,1)} %get-tuple-element.150), channel_id=1, source_target_pairs={{0,1},{1,2},{2,3},{4,5},{5,6},{6,7},{8,9},{9,10},{10,11},{12,13},{... | collective-permute-start | bytes 1179656 | tf_op jit(solution)/shard_map/ppermute | solution.py:378
  323.9 51.0 %collective-permute-start.13 = (bf16[1536,128]{1,0:T(8,128)(2,1)}, bf16[1536,128]{1,0:T(8,128)(2,1)}, u32[]{:S(2)}, u32[]{:S(2)}) collective-permute-start(bf16[1536,128]{1,0:T(8,128)(2,1)} %get-tuple-element.149), channel_id=1, source_target_pairs={{0,1},{1,2},{2,3},{4,5},{5,6},{6,7},{8,9},{9,10},{10,11},{12,13},{... | collective-permute-start | bytes 1179656 | tf_op jit(solution)/shard_map/ppermute | solution.py:378
  329.6 45.2 %collective-permute-start.10 = (bf16[1536,128]{1,0:T(8,128)(2,1)}, bf16[1536,128]{1,0:T(8,128)(2,1)S(1)}, u32[]{:S(2)}, u32[]{:S(2)}) collective-permute-start(bf16[1536,128]{1,0:T(8,128)(2,1)} %add_convert_fusion.10), channel_id=1, source_target_pairs={{0,1},{1,2},{2,3},{4,5},{5,6},{6,7},{8,9},{9,10},{10,11},{12,13},{... | collective-permute-start | bytes 1179656 | tf_op jit(solution)/shard_map/ppermute | solution.py:378
  411.6 16.3 %copy-start.4 = (f32[3072,128]{1,0:T(8,128)S(1)}, f32[3072,128]{1,0:T(8,128)}, u32[]{:S(2)}) copy-start(f32[3072,128]{1,0:T(8,128)} %get-tuple-element.75) | copy-start | bytes 4718596
  411.6 18.6 %copy-start.32 = (bf16[256,3072]{1,0:T(8,128)(2,1)S(1)}, bf16[256,3072]{1,0:T(8,128)(2,1)}, u32[]{:S(2)}) copy-start(bf16[256,3072]{1,0:T(8,128)(2,1)} %get-tuple-element.73) | copy-start | bytes 4718596
  414.0 13.9 %collective-permute-start.14 = (bf16[1536,128]{1,0:T(8,128)(2,1)S(1)}, bf16[1536,128]{1,0:T(8,128)(2,1)S(1)}, u32[]{:S(2)}, u32[]{:S(2)}) collective-permute-start(bf16[1536,128]{1,0:T(8,128)(2,1)S(1)} %get-tuple-element.147), channel_id=1, source_target_pairs={{1,0},{2,1},{3,2},{5,4},{6,5},{7,6},{9,8},{10,9},{11,10},{13,12},{... | collective-permute-start | bytes 1179656 | tf_op jit(solution)/shard_map/ppermute | solution.py:378
  415.3 21.1 %collective-permute-start.17 = (bf16[1536,128]{1,0:T(8,128)(2,1)}, bf16[1536,128]{1,0:T(8,128)(2,1)}, u32[]{:S(2)}, u32[]{:S(2)}) collective-permute-start(bf16[1536,128]{1,0:T(8,128)(2,1)} %get-tuple-element.148), channel_id=1, source_target_pairs={{1,0},{2,1},{3,2},{5,4},{6,5},{7,6},{9,8},{10,9},{11,10},{13,12},{... | collective-permute-start | bytes 1179656 | tf_op jit(solution)/shard_map/ppermute | solution.py:378
  428.9 15.3 %collective-permute-start.15 = (bf16[1536,128]{1,0:T(8,128)(2,1)}, bf16[1536,128]{1,0:T(8,128)(2,1)}, u32[]{:S(2)}, u32[]{:S(2)}) collective-permute-start(bf16[1536,128]{1,0:T(8,128)(2,1)} %add_convert_fusion.7), channel_id=1, source_target_pairs={{1,0},{2,1},{3,2},{5,4},{6,5},{7,6},{9,8},{10,9},{11,10},{13,12},{... | collective-permute-start | bytes 1179656 | tf_op jit(solution)/shard_map/ppermute | solution.py:378
  431.5 32.5 %all-to-all-start = ((bf16[8,256,384]{2,1,0:T(8,128)(2,1)}), bf16[8,256,384]{2,1,0:T(8,128)(2,1)}, u32[]{:S(2)}, u32[]{:S(2)}) async-start(bf16[8,256,384]{2,1,0:T(8,128)(2,1)} %bitcast.193), calls=%async_computation | async-start | bytes 3145728 | tf_op jit(solution)/shard_map/all_to_all | solution.py:428
  435.9 26.9 %copy-start.27 = (bf16[256,3072]{1,0:T(8,128)(2,1)S(1)}, bf16[256,3072]{1,0:T(8,128)(2,1)}, u32[]{:S(2)}) copy-start(bf16[256,3072]{1,0:T(8,128)(2,1)} %get-tuple-element.71) | copy-start | bytes 4718596
  446.5 13.9 %collective-permute-start.18 = (bf16[1536,128]{1,0:T(8,128)(2,1)S(1)}, bf16[1536,128]{1,0:T(8,128)(2,1)S(1)}, u32[]{:S(2)}, u32[]{:S(2)}) collective-permute-start(bf16[1536,128]{1,0:T(8,128)(2,1)S(1)} %get-tuple-element.146), channel_id=1, source_target_pairs={{1,0},{2,1},{3,2},{5,4},{6,5},{7,6},{9,8},{10,9},{11,10},{13,12},{... | collective-permute-start | bytes 1179656 | tf_op jit(solution)/shard_map/ppermute | solution.py:378
  447.8 21.1 %collective-permute-start.16 = (bf16[1536,128]{1,0:T(8,128)(2,1)}, bf16[1536,128]{1,0:T(8,128)(2,1)}, u32[]{:S(2)}, u32[]{:S(2)}) collective-permute-start(bf16[1536,128]{1,0:T(8,128)(2,1)} %get-tuple-element.145), channel_id=1, source_target_pairs={{1,0},{2,1},{3,2},{5,4},{6,5},{7,6},{9,8},{10,9},{11,10},{13,12},{... | collective-permute-start | bytes 1179656 | tf_op jit(solution)/shard_map/ppermute | solution.py:378
  461.4 14.4 %collective-permute-start.19 = (bf16[1536,128]{1,0:T(8,128)(2,1)}, bf16[1536,128]{1,0:T(8,128)(2,1)}, u32[]{:S(2)}, u32[]{:S(2)}) collective-permute-start(bf16[1536,128]{1,0:T(8,128)(2,1)} %add_convert_fusion.4), channel_id=1, source_target_pairs={{1,0},{2,1},{3,2},{5,4},{6,5},{7,6},{9,8},{10,9},{11,10},{13,12},{... | collective-permute-start | bytes 1179656 | tf_op jit(solution)/shard_map/ppermute | solution.py:378
  464.0 24.5 %all-to-all-start.1 = ((bf16[8,256,384]{2,1,0:T(8,128)(2,1)}), bf16[8,256,384]{2,1,0:T(8,128)(2,1)S(1)}, u32[]{:S(2)}, u32[]{:S(2)}) async-start(bf16[8,256,384]{2,1,0:T(8,128)(2,1)} %bitcast.184), calls=%async_computation.1 | async-start | bytes 3145728 | tf_op jit(solution)/shard_map/all_to_all | solution.py:428
  467.6 81.6 %copy-start.99 = (pred[256]{0:T(512)(128)(4,1)}, pred[256]{0:T(512)(128)(4,1)S(1)}, u32[]{:S(2)}) copy-start(pred[256]{0:T(512)(128)(4,1)S(1)} %iota_compare_fusion.5) | copy-start | bytes 772
  500.7 50.6 %all-to-all-start.2 = ((bf16[8,256,384]{2,1,0:T(8,128)(2,1)}), bf16[8,256,384]{2,1,0:T(8,128)(2,1)}, u32[]{:S(2)}, u32[]{:S(2)}) async-start(bf16[8,256,384]{2,1,0:T(8,128)(2,1)} %bitcast.182), calls=%async_computation.2 | async-start | bytes 3145728 | tf_op jit(solution)/shard_map/all_to_all | solution.py:428
  505.1 66.6 %reduce-scatter.5.cloned.1.call-start = ((), (), s32[]{:S(2)}) async-start(), calls=%async_computation.15 | async-start | bytes 2949120 | tf_op jit(solution)/shard_map/reduce_scatter | solution.py:442
  508.3 177.5 %all-gather.17.cloned.1.call-start = ((), (), s32[]{:S(2)}) async-start(), calls=%async_computation.16 | async-start | bytes 14155776 | tf_op jit(solution)/shard_map/all_gather | solution.py:424
  548.0 9.5 %collective-permute-start.20 = (f32[3,3328]{1,0:T(4,128)S(1)}, f32[3,3328]{1,0:T(4,128)S(1)}, u32[]{:S(2)}, u32[]{:S(2)}) collective-permute-start(f32[3,3328]{1,0:T(4,128)S(1)} %pad_maximum_fusion.12), channel_id=1, source_target_pairs={{1,0},{2,1},{3,2},{5,4},{6,5},{7,6},{9,8},{10,9},{11,10},{13,12},{... | collective-permute-start | bytes 119816 | tf_op jit(solution)/shard_map/ppermute | solution.py:378
  579.5 45.0 %all-to-all-start.3 = ((bf16[8,256,512]{2,1,0:T(8,128)(2,1)}), bf16[8,256,512]{2,1,0:T(8,128)(2,1)}, u32[]{:S(2)}, u32[]{:S(2)}) async-start(bf16[8,256,512]{2,1,0:T(8,128)(2,1)} %maximum_bitcast_fusion), calls=%async_computation.3 | async-start | bytes 4194304 | tf_op jit(solution)/shard_map/all_to_all | solution.py:428
  615.2 24.7 %copy-start.3 = (f32[3072,128]{1,0:T(8,128)S(1)}, f32[3072,128]{1,0:T(8,128)}, u32[]{:S(2)}) copy-start(f32[3072,128]{1,0:T(8,128)} %get-tuple-element.91) | copy-start | bytes 4718596
  626.1 13.9 %collective-permute-start.21 = (bf16[1536,128]{1,0:T(8,128)(2,1)S(1)}, bf16[1536,128]{1,0:T(8,128)(2,1)S(1)}, u32[]{:S(2)}, u32[]{:S(2)}) collective-permute-start(bf16[1536,128]{1,0:T(8,128)(2,1)S(1)} %get-tuple-element.143), channel_id=1, source_target_pairs={{1,0},{2,1},{3,2},{5,4},{6,5},{7,6},{9,8},{10,9},{11,10},{13,12},{... | collective-permute-start | bytes 1179656 | tf_op jit(solution)/shard_map/ppermute | solution.py:378
  627.4 21.0 %collective-permute-start.24 = (bf16[1536,128]{1,0:T(8,128)(2,1)S(1)}, bf16[1536,128]{1,0:T(8,128)(2,1)S(1)}, u32[]{:S(2)}, u32[]{:S(2)}) collective-permute-start(bf16[1536,128]{1,0:T(8,128)(2,1)S(1)} %get-tuple-element.144), channel_id=1, source_target_pairs={{1,0},{2,1},{3,2},{5,4},{6,5},{7,6},{9,8},{10,9},{11,10},{13,12},{... | collective-permute-start | bytes 1179656 | tf_op jit(solution)/shard_map/ppermute | solution.py:378
  640.2 12.6 %collective-permute-start.22 = (bf16[1536,128]{1,0:T(8,128)(2,1)S(1)}, bf16[1536,128]{1,0:T(8,128)(2,1)S(1)}, u32[]{:S(2)}, u32[]{:S(2)}) collective-permute-start(bf16[1536,128]{1,0:T(8,128)(2,1)S(1)} %add_convert_fusion.3), channel_id=1, source_target_pairs={{1,0},{2,1},{3,2},{5,4},{6,5},{7,6},{9,8},{10,9},{11,10},{13,12},{... | collective-permute-start | bytes 1179656 | tf_op jit(solution)/shard_map/ppermute | solution.py:378
  654.1 10.0 %collective-permute-start.25 = (bf16[1536,128]{1,0:T(8,128)(2,1)}, bf16[1536,128]{1,0:T(8,128)(2,1)}, u32[]{:S(2)}, u32[]{:S(2)}) collective-permute-start(bf16[1536,128]{1,0:T(8,128)(2,1)} %get-tuple-element.142), channel_id=1, source_target_pairs={{1,0},{2,1},{3,2},{5,4},{6,5},{7,6},{9,8},{10,9},{11,10},{13,12},{... | collective-permute-start | bytes 1179656 | tf_op jit(solution)/shard_map/ppermute | solution.py:378
  656.7 29.1 %all-to-all-start.4 = ((bf16[8,256,384]{2,1,0:T(8,128)(2,1)}), bf16[8,256,384]{2,1,0:T(8,128)(2,1)}, u32[]{:S(2)}, u32[]{:S(2)}) async-start(bf16[8,256,384]{2,1,0:T(8,128)(2,1)} %bitcast.192), calls=%async_computation.5 | async-start | bytes 3145728 | tf_op jit(solution)/shard_map/all_to_all | solution.py:428
  661.0 175.3 %reduce-scatter.11.cloned.1.call-start = ((), (), s32[]{:S(2)}) async-start(), calls=%async_computation.19 | async-start | bytes 1966080 | tf_op jit(solution)/shard_map/reduce_scatter | solution.py:442
  661.0 17.3 %collective-permute-start.23 = (bf16[1536,128]{1,0:T(8,128)(2,1)S(1)}, bf16[1536,128]{1,0:T(8,128)(2,1)}, u32[]{:S(2)}, u32[]{:S(2)}) collective-permute-start(bf16[1536,128]{1,0:T(8,128)(2,1)S(1)} %get-tuple-element.141), channel_id=1, source_target_pairs={{1,0},{2,1},{3,2},{5,4},{6,5},{7,6},{9,8},{10,9},{11,10},{13,12},{... | collective-permute-start | bytes 1179656 | tf_op jit(solution)/shard_map/ppermute | solution.py:378
  666.1 17.7 %collective-permute-start.26 = (bf16[1536,128]{1,0:T(8,128)(2,1)}, bf16[1536,128]{1,0:T(8,128)(2,1)}, u32[]{:S(2)}, u32[]{:S(2)}) collective-permute-start(bf16[1536,128]{1,0:T(8,128)(2,1)} %add_convert_fusion), channel_id=1, source_target_pairs={{1,0},{2,1},{3,2},{5,4},{6,5},{7,6},{9,8},{10,9},{11,10},{13,12},{... | collective-permute-start | bytes 1179656 | tf_op jit(solution)/shard_map/ppermute | solution.py:378
  702.6 150.0 %reduce-scatter.7.cloned.1.call-start = ((), (), s32[]{:S(2)}) async-start(), calls=%async_computation.17 | async-start | bytes 2949120 | tf_op jit(solution)/shard_map/reduce_scatter | solution.py:442
  744.1 7.0 collective-permute-start.27
  761.5 31.2 %all-to-all-start.5 = ((bf16[8,256,512]{2,1,0:T(8,128)(2,1)}), bf16[8,256,512]{2,1,0:T(8,128)(2,1)}, u32[]{:S(2)}, u32[]{:S(2)}) async-start(bf16[8,256,512]{2,1,0:T(8,128)(2,1)} %maximum_bitcast_fusion.1), calls=%async_computation.7 | async-start | bytes 4194304 | tf_op jit(solution)/shard_map/all_to_all | solution.py:428
  766.0 98.0 %reduce-scatter.9.cloned.1.call-start = ((), (), s32[]{:S(2)}) async-start(), calls=%async_computation.18 | async-start | bytes 1966080 | tf_op jit(solution)/shard_map/reduce_scatter | solution.py:442
  803.6 1.4 collective-permute-start.28
  805.1 6.5 collective-permute-start.29
  812.2 10.1 %collective-permute-start.30 = (f32[336,128]{1,0:T(8,128)}, f32[336,128]{1,0:T(8,128)}, u32[]{:S(2)}, u32[]{:S(2)}) collective-permute-start(f32[336,128]{1,0:T(8,128)} %add.229), channel_id=1, source_target_pairs={{0,16},{4,20},{8,24},{12,28},{16,0},{20,4},{24,8},{28,12},{1,17},{... | collective-permute-start | bytes 516104 | tf_op jit(solution)/shard_map/ppermute | solution.py:406
  823.4 6.3 collective-permute-start.31
  830.4 21.0 %collective-permute-start.32 = (f32[336,128]{1,0:T(8,128)}, f32[336,128]{1,0:T(8,128)}, u32[]{:S(2)}, u32[]{:S(2)}) collective-permute-start(f32[336,128]{1,0:T(8,128)} %add.231), channel_id=1, source_target_pairs={{0,2},{1,3},{2,0},{3,1},{4,6},{5,7},{6,4},{7,5},{8,10},{9,11},{10,... | collective-permute-start | bytes 516104 | tf_op jit(solution)/shard_map/ppermute | solution.py:406
  838.3 27.6 %all-to-all-start.7 = ((bf16[8,48,806]{2,1,0:T(8,128)(2,1)}), bf16[8,48,806]{2,1,0:T(8,128)(2,1)S(1)}, u32[]{:S(2)}, u32[]{:S(2)}) async-start(bf16[8,48,806]{2,1,0:T(8,128)(2,1)} %bitcast.61), calls=%async_computation.11 | async-start | bytes 1376256 | tf_op jit(solution)/shard_map/all_to_all | solution.py:484
  865.9 15.0 %all-to-all-start.6 = ((bf16[8,48,806]{2,1,0:T(8,128)(2,1)}), bf16[8,48,806]{2,1,0:T(8,128)(2,1)S(1)}, u32[]{:S(2)}, u32[]{:S(2)}) async-start(bf16[8,48,806]{2,1,0:T(8,128)(2,1)} %bitcast.58), calls=%async_computation.9 | async-start | bytes 1376256 | tf_op jit(solution)/shard_map/all_to_all | solution.py:484
  (90 other events, 403.7 us)
Sparse Core Ops, SparseCore 0:
  12.5 106.2 all-gather.18
  120.7 58.6 all-gather.20
  181.3 63.6 all-gather.10
  247.3 58.6 all-gather.22
  307.8 58.6 all-gather.12
  368.3 72.0 all-gather.14
  508.8 52.1 reduce-scatter.4
  573.8 94.5 all-gather.16
  702.7 36.0 reduce-scatter.10
  748.5 50.4 reduce-scatter.6
  822.5 41.4 reduce-scatter.8

commit v5 on v4

--- a/solution.py
+++ b/solution.py
@@ -4,6 +4,7 @@
 import jax.numpy as jnp
 from jax import lax
 from jax.experimental import pallas as pl
+from jax.experimental.layout import Layout, with_layout_constraint
 from jax.experimental.pallas import tpu as pltpu
 from jax.sharding import PartitionSpec as P
 
@@ -381,7 +382,7 @@
 CHUNKS = 2
 
 
-def carry(totals, local_state, steps):
+def carry(totals, local_state, steps, side=None):
     hops = lax.axis_size("ctx") - 1
     size = DI // CHUNKS
     parts = []
@@ -389,10 +390,12 @@
         rows = slice(chunk * size, chunk * size + size)
         own, factor = local_state[rows], totals[rows]
         incoming = passed_along(own.astype(BF), "ctx", steps)
-        for _ in range(hops - 1):
+        for hop in range(hops - 1):
+            if side is not None and chunk == 0 and hop == hops - 2:
+                incoming, side = lax.optimization_barrier((incoming, side))
             incoming = passed_along((factor * incoming.astype(F32) + own).astype(BF), "ctx", steps)
         parts.append(incoming)
-    return jnp.concatenate(parts, 0)
+    return jnp.concatenate(parts, 0), side
 
 
 def all_sum(value):
@@ -429,22 +432,18 @@
     return moved.reshape(-1, split.shape[2])
 
 
-def by_run(part):
-    fsdp_count, ctx_count = lax.axis_size("fsdp"), lax.axis_size("ctx")
-    rows, width = part.shape
-    own = rows // (fsdp_count * ctx_count)
-    blocks = part.astype(BF).reshape(fsdp_count, ctx_count, own, width)
-    return jnp.transpose(blocks, (1, 0, 2, 3)).reshape(ctx_count, fsdp_count * own, width)
-
-
-def run_sum(blocks):
-    flat = blocks.reshape(-1, blocks.shape[2])
+def by_run(normed):
+    rows, model = normed.shape
+    blocks = normed.reshape(rows, lax.axis_size("fsdp"), lax.axis_size("ctx"), -1)
+    return jnp.transpose(blocks, (0, 2, 1, 3)).reshape(rows, model)
+
+
+def run_sum(flat):
     return lax.psum_scatter(flat, "ctx", scatter_dimension=0, tiled=True)
 
 
-def gate_parts(normed_all, d_gate):
-    fsdp_count = lax.axis_size("fsdp")
-    return by_run(rows_product(normed_all, to_owners(d_gate.reshape(d_gate.shape[0], fsdp_count, -1))))
+def gate_owners(d_gate):
+    return to_owners(d_gate.reshape(d_gate.shape[0], lax.axis_size("fsdp"), -1))
 
 
 def out_parts(norm_cols, grad_all):
@@ -456,8 +455,10 @@
 
 
 def early_sum(part_gate, part_out, model):
-    summed = run_sum(jnp.concatenate([part_gate, part_out], 1))
-    in_rows, width = part_gate.shape[1:]
+    ctx_count = lax.axis_size("ctx")
+    in_rows, width = part_gate.shape[0] // ctx_count, part_gate.shape[1]
+    part_gate = part_gate.reshape(ctx_count, in_rows, width)
+    summed = run_sum(jnp.concatenate([part_gate, part_out], 1).reshape(-1, width))
     owned_out = jnp.transpose(summed[in_rows:].reshape(model // width, -1, width), (1, 0, 2))
     return summed[:in_rows], owned_out.reshape(-1, model).astype(F32)
 
@@ -473,7 +474,8 @@
 
 def rest_parts(normed_all, rest_cols):
     width = (CC - DI + H + DI) // lax.axis_size("fsdp")
-    return by_run(rows_product(normed_all, rest_cols)[:, :width])
+    part = rows_product(normed_all, rest_cols)[:, :width].astype(BF)
+    return with_layout_constraint(part, Layout(major_to_minor=(0, 1)))
 
 
 def late_sum(part_rest, gate_sum):
@@ -515,7 +517,9 @@
     first = gathered(in_weight[0])
     weights = [(first[:, DI:], first[:, :DI], gathered(out_weight[0]))]
     for k in range(1, LAYERS):
-        weights.append((gathered(in_weight[k][:, DI:]), gathered(in_weight[k][:, :DI]), gathered(out_weight[k])))
+        w_conv = gathered(in_weight[k][:, DI:])
+        own_out, w_conv = lax.optimization_barrier((out_weight[k], w_conv))
+        weights.append((w_conv, gathered(in_weight[k][:, :DI]), gathered(own_out)))
     stream = activations
     kept = []
     for k in range(LAYERS):
@@ -534,7 +538,7 @@
         bias = conv_bias[k][None, :]
         y, state, bc = scan_fwd(conv_in, halo, conv_weight[k], bias, col, row, skip)
         gate_in = jnp.dot(normed, w_gate, preferred_element_type=F32)
-        incoming = carry(totals, state, 1)
+        incoming, _ = carry(totals, state, 1)
         ssm, gnormed = gate_fwd(y, gate_in, incoming, bc, col, gate_gain[k][None, :])
         kept.append((stream, normed, gate_in, conv_in, halo, raw_steps, steps, col, row, totals, skip, bias, bc,
                      incoming, ssm, gnormed))
@@ -549,14 +553,25 @@
         grad_bf = grad_stream.astype(BF)
         d_gnormed = right_transposed(grad_bf, w_out)
         d_ssm, d_gate, g_gate, local_grad = gate_bwd(ssm, gate_in, d_gnormed, gate_gain[k][None, :], col, bc)
-        tokens = jnp.concatenate([normed, grad_bf], 1)
-        if waiting is not None:
+        local_grad, gnormed_cols = lax.optimization_barrier((local_grad, gnormed_cols))
+        if waiting is None:
+            tokens = gathered(jnp.concatenate([by_run(normed), grad_bf], 1))
+            normed_all, grad_all = tokens[:, :model], tokens[:, model:]
+        else:
             local_grad, rest_cols = lax.optimization_barrier((local_grad, waiting[1]))
-            tokens, gate_sum = lax.optimization_barrier((tokens, waiting[2]))
-        tokens = gathered(tokens)
-        outgoing = carry(totals, local_grad, -1)
-        normed_all, grad_all = tokens[:, :model], tokens[:, model:]
-        part_gate = gate_parts(normed_all, d_gate)
+            own_grad, gate_sum = lax.optimization_barrier((grad_bf, waiting[2]))
+            normed_all, grad_all = next_normed, gathered(own_grad)
+        side = [right_transposed(d_gate, w_gate), gate_owners(d_gate)]
+        if waiting is None:
+            side.append(stream)
+        outgoing, side = carry(totals, local_grad, -1, side)
+        d_normed, gate_cols = side[:2]
+        if waiting is None:
+            stream = side[2]
+        if k:
+            own_normed, grad_all = lax.optimization_barrier((by_run(kept[k - 1][1]), grad_all))
+            next_normed = gathered(own_normed)
+        part_gate = rows_product(normed_all, gate_cols).astype(BF)
         part_out = out_parts(gnormed_cols, grad_all)
         if waiting is None:
             outgoing, part_gate, part_out = lax.optimization_barrier((outgoing, part_gate, part_out))
@@ -592,7 +607,7 @@
         d_conv = jnp.concatenate([d_x, d_bc], 1)
         d_conv = d_conv + jnp.pad(edge_back, ((rows - edge_count, 0), (0, 0)))
         d_rest = jnp.concatenate([d_conv, d_raw], 1).astype(BF)
-        d_normed = right_transposed(d_gate, w_gate) + right_transposed(d_rest, w_conv)
+        d_normed = d_normed + right_transposed(d_rest, w_conv)
         _, pullback = jax.vjp(rms_norm, stream_in, norm_gain[k])
         d_stream, g_norm = pullback(d_normed)
         grad_stream = grad_stream + d_stream

time: 901 us -> 934 us (1.037)
  waiting for transfers between devices: 311 us -> 345 us
    all_gather x7 -> x8, waiting for transfers between devices: 138 us -> 164 us  [gathered(): return lax.all_gather(value, 'fsdp', axis=0, tiled=True)]
    all_to_all x6, waiting for transfers between devices: 28.2 us -> 45.8 us  [to_owners(): lax.all_to_all(jnp.transpose(split, (1, 0, 2)), 'fsdp', split_axis=0, con...]
    ppermute x28, waiting for transfers between devices: 107 us -> 95.8 us  [passed_along(): lax.ppermute(value, axis, [(source, source + steps) for source in range(i...]
  transfers between devices with their start and end apart: 52 -> 53, of which waited for: 31 -> 32; matrix products, arithmetic and copies ran while one was open for 28% -> 26% of each run, Pallas kernels for 17% -> 16%
where the time goes in v5:
time: 934 us; the launch traced here: 924 us
  waiting for transfers between devices  345 us (37%)
  Pallas kernels  152 us (16%)
  matrix products  135 us (14%)
  starting transfers between devices  116 us (12%)
  local copies, waits for them, and re-layouts  105 us (11%)
  other arithmetic  54.9 us (6%)
  between operations  16.6 us (2%)
    all_gather x8, waiting for transfers between devices, gathered(): return lax.all_gather(value, 'fsdp', axis=0, tiled=True)  164 us
    ppermute x28, waiting for transfers between devices, passed_along(): lax.ppermute(value, axis, [(source, source + steps) for source in range(i...  95.8 us
    ppermute x28, starting transfers between devices, passed_along(): lax.ppermute(value, axis, [(source, source + steps) for source in range(i...  76.8 us
    pallas_call x2, Pallas kernels, scan_bwd(): pl.pallas_call(scan_bwd_kernel, grid=(G,), in_specs=conv_specs(rows) + [f...  53.8 us
    pallas_call x2, Pallas kernels, gate_bwd(): pl.pallas_call(gate_bwd_kernel, grid=(2, G), in_specs=[block, block, bloc...  46.1 us
    all_to_all x6, waiting for transfers between devices, to_owners(): lax.all_to_all(jnp.transpose(split, (1, 0, 2)), 'fsdp', split_axis=0, con...  45.8 us
    dot_general x6, matrix products, right_transposed(): lax.dot_general(left, right, (((1,), (1,)), ((), ())), preferred_element_...  44.1 us
    dot_general x6, matrix products, rows_product(): lax.dot_general(left, right, (((0,), (0,)), ((), ())), preferred_element_...  43.9 us
  transfers between devices with their start and end apart: 53, of which 32 were waited for; matrix products, arithmetic and copies ran while one was open for 26% of the time, Pallas kernels for 16%

profile of v5, /device:TPU:0, one launch (start us, length us, event | category | flops | bytes accessed | tf_op | source)
XLA Modules:
  0.0 923.9 jit_solution(10934465365312752504)
XLA Ops:
  7.2 4.3 slice_bitcast_fusion
  18.0 61.2 %all-gather.11.cloned.1.call-done = bf16[1536,3376]{1,0:T(8,128)(2,1)} async-done(((bf16[192,3376]{1,0:T(8,128)(2,1)}), bf16[1536,3376]{1,0:T(8,128)(2,1)}) %all-gather.11.cloned.1.call-update) | async-done | bytes 10371088 | tf_op jit(solution)/shard_map/all_gather | solution.py:427
  82.2 103.1 %all-gather.23.cloned.1.call-done = bf16[1,1536,6448]{2,1,0:T(8,128)(2,1)} async-done(((bf16[1,192,6448]{2,1,0:T(8,128)(2,1)}), bf16[1,1536,6448]{2,1,0:T(8,128)(2,1)}) %all-gather.23.cloned.1.call-update) | async-done | bytes 19808272 | tf_op jit(solution)/shard_map/all_gather | solution.py:427
  185.3 5.9 fusion.78
  201.6 14.5 %scan_fwd.2 = (f32[256,3072]{1,0:T(8,128)}, f32[3072,128]{1,0:T(8,128)}, f32[256,256]{1,0:T(8,128)}) custom-call(bf16[256,3328]{1,0:T(8,128)(2,1)} %slice.408.conv_ref.conv_bc_ref, bf16[256,3328]{1,0:T(8,128)(2,1)} %slice.408.conv_ref.conv_bc_ref, f32[8,3328]{1,0:T(8,128)} %pad_convert_fusion.1.halo_ref.halo_bc_ref, ...), custom_call_target="tpu_custom_call" | custom-call | tf_op jit(solution)/shard_map/scan_fwd/pallas_call | solution.py:318
  219.1 4.3 collective-permute-start.4
  227.8 4.6 collective-permute-done.4
  234.5 5.1 collective-permute-start.5
  242.3 6.0 collective-permute-done.5
  249.9 4.4 collective-permute-start.2
  258.3 5.4 collective-permute-done.2
  264.0 4.6 collective-permute-start.3
  268.6 7.9 fusion.10.gate_ref
  279.7 11.4 %gate_fwd.2 = (f32[256,3072]{1,0:T(8,128)}, bf16[256,3072]{1,0:T(8,128)(2,1)}) custom-call(f32[256,3072]{1,0:T(8,128)} %get-tuple-element.79.y_ref, f32[256,3072]{1,0:T(8,128)} %fusion.10.gate_ref, bf16[3072,128]{1,0:T(8,128)(2,1)} %copy-done.9, f32[256,256]{1,0:T(8,128)} %get-tuple-element.81.bc_ref, f32[12,256,8]{2,1,0:T(8,128)} %copy.225.col_ref, ...), custom_call_target="tpu_custom_call" | custom-call | tf_op jit(solution)/shard_map/gate_fwd/pallas_call | solution.py:331
  291.2 6.0 multiply_reduce_fusion.4
  302.1 5.9 fusion.79
  309.2 4.3 collective-permute-start.7
  319.4 14.5 %scan_fwd.3 = (f32[256,3072]{1,0:T(8,128)}, f32[3072,128]{1,0:T(8,128)}, f32[256,256]{1,0:T(8,128)}) custom-call(bf16[256,3328]{1,0:T(8,128)(2,1)} %slice.419.conv_ref.conv_bc_ref, bf16[256,3328]{1,0:T(8,128)(2,1)} %slice.419.conv_ref.conv_bc_ref, f32[8,3328]{1,0:T(8,128)} %pad_convert_fusion.halo_ref.halo_bc_ref, ...), custom_call_target="tpu_custom_call" | custom-call | tf_op jit(solution)/shard_map/scan_fwd/pallas_call | solution.py:318
  336.3 4.0 collective-permute-start.11
  343.4 6.0 collective-permute-done.11
  351.4 5.2 collective-permute-start.12
  357.8 5.5 collective-permute-done.12
  365.6 4.4 collective-permute-start.9
  373.7 5.7 collective-permute-done.9
  380.5 4.6 collective-permute-start.10
  385.1 8.2 fusion.80.gate_ref
  395.3 11.6 %gate_fwd.3 = (f32[256,3072]{1,0:T(8,128)}, bf16[256,3072]{1,0:T(8,128)(2,1)}) custom-call(f32[256,3072]{1,0:T(8,128)} %get-tuple-element.84.y_ref, f32[256,3072]{1,0:T(8,128)} %fusion.80.gate_ref, bf16[3072,128]{1,0:T(8,128)(2,1)} %copy-done.10, f32[256,256]{1,0:T(8,128)} %get-tuple-element.86.bc_ref, f32[12,256,8]{2,1,0:T(8,128)} %copy.232.col_ref, ...), custom_call_target="tpu_custom_call" | custom-call | tf_op jit(solution)/shard_map/gate_fwd/pallas_call | solution.py:331
  409.7 4.4 all-to-all-start
  414.2 8.1 convolution_bitcast_fusion.dn_ref
  422.2 23.1 %gate_bwd.2 = (f32[256,3072]{1,0:T(8,128)}, bf16[256,3072]{1,0:T(8,128)(2,1)}, f32[1,3072]{1,0:T(1,128)}, f32[3072,128]{1,0:T(8,128)}) custom-call(f32[256,3072]{1,0:T(8,128)} %get-tuple-element.87.ssm_ref, f32[256,3072]{1,0:T(8,128)} %fusion.80.gate_ref, f32[256,3072]{1,0:T(8,128)} %convolution_bitcast_fusion.dn_ref, ...), custom_call_target="tpu_custom_call" | custom-call | tf_op jit(solution)/shard_map/gate_bwd/pallas_call | solution.py:346
  448.1 4.3 all-to-all-done
  452.4 4.3 all-to-all-start.1
  459.1 9.0 convolution_add_fusion
  473.6 3.8 fusion.81
  477.7 13.2 %collective-permute-done.15 = bf16[1536,128]{1,0:T(8,128)(2,1)} collective-permute-done((bf16[1536,128]{1,0:T(8,128)(2,1)}, bf16[1536,128]{1,0:T(8,128)(2,1)}, u32[]{:S(2)}, u32[]{:S(2)}) %collective-permute-start.15) | collective-permute-done | bytes 393248 | tf_op jit(solution)/shard_map/ppermute | solution.py:379
  496.2 10.9 %collective-permute-done.18 = bf16[1536,128]{1,0:T(8,128)(2,1)S(1)} collective-permute-done((bf16[1536,128]{1,0:T(8,128)(2,1)S(1)}, bf16[1536,128]{1,0:T(8,128)(2,1)S(1)}, u32[]{:S(2)}, u32[]{:S(2)}) %collective-permute-start.18) | collective-permute-done | bytes 393248 | tf_op jit(solution)/shard_map/ppermute | solution.py:379
  511.7 3.9 collective-permute-done.16
  515.6 7.1 collective-permute-done.19
  524.7 6.5 slice.424
  531.2 6.9 convolution_convert_fusion.2
  540.8 6.7 fusion.18
  556.5 26.9 %scan_bwd.2 = (f32[256,3072]{1,0:T(8,128)}, f32[8,3072]{1,0:T(8,128)}, f32[8,3072]{1,0:T(8,128)}, f32[256,256]{1,0:T(8,128)}, f32[8,256]{1,0:T(8,128)}, /*index=...) custom-call(bf16[256,3328]{1,0:T(8,128)(2,1)} %slice.419.conv_ref.conv_bc_ref, ...), custom_call_target="tpu_custom_call" | custom-call | tf_op jit(solution)/shard_map/scan_bwd/pallas_call | solution.py:363
  602.5 7.2 multiply_reduce_fusion
  619.4 4.5 all-to-all-start.3
  623.9 8.3 fusion.dn_ref
  632.2 23.0 %gate_bwd.3 = (f32[256,3072]{1,0:T(8,128)}, bf16[256,3072]{1,0:T(8,128)(2,1)}, f32[1,3072]{1,0:T(1,128)}, f32[3072,128]{1,0:T(8,128)}) custom-call(f32[256,3072]{1,0:T(8,128)} %get-tuple-element.111.ssm_ref, f32[256,3072]{1,0:T(8,128)} %fusion.10.gate_ref, f32[256,3072]{1,0:T(8,128)} %fusion.dn_ref, f32[1,3072]{1,0:T(1,128)} %get-tuple-element.213.gain_ref, ...), custom_call_target="tpu_custom_call" | custom-call | tf_op jit(solution)/shard_map/gate_bwd/pallas_call | solution.py:346
  655.2 10.1 %all-to-all-done.3 = bf16[8,256,512]{2,1,0:T(8,128)(2,1)} async-done(((bf16[8,256,512]{2,1,0:T(8,128)(2,1)}), bf16[8,256,512]{2,1,0:T(8,128)(2,1)}, u32[]{:S(2)}, u32[]{:S(2)}) %all-to-all-start.3) | async-done | bytes 2097184 | tf_op jit(solution)/shard_map/all_to_all | solution.py:431
  670.2 4.4 all-to-all-start.4
  681.2 8.0 fusion.8
  689.2 14.9 %all-to-all-done.4 = bf16[8,256,384]{2,1,0:T(8,128)(2,1)} async-done(((bf16[8,256,384]{2,1,0:T(8,128)(2,1)}), bf16[8,256,384]{2,1,0:T(8,128)(2,1)}, u32[]{:S(2)}, u32[]{:S(2)}) %all-to-all-start.4) | async-done | bytes 1572896 | tf_op jit(solution)/shard_map/all_to_all | solution.py:431
  708.3 11.9 %collective-permute-done.25 = bf16[1536,128]{1,0:T(8,128)(2,1)S(1)} collective-permute-done((bf16[1536,128]{1,0:T(8,128)(2,1)S(1)}, bf16[1536,128]{1,0:T(8,128)(2,1)S(1)}, u32[]{:S(2)}, u32[]{:S(2)}) %collective-permute-start.25) | collective-permute-done | bytes 393248 | tf_op jit(solution)/shard_map/ppermute | solution.py:379
  722.0 8.1 fusion.12
  734.2 7.8 convolution_convert_fusion.1
  742.0 6.4 convolution_convert_fusion
  755.7 26.9 %scan_bwd.3 = (f32[256,3072]{1,0:T(8,128)}, f32[8,3072]{1,0:T(8,128)}, f32[8,3072]{1,0:T(8,128)}, f32[256,256]{1,0:T(8,128)}, f32[8,256]{1,0:T(8,128)}, /*index=...) custom-call(bf16[256,3328]{1,0:T(8,128)(2,1)} %slice.408.conv_ref.conv_bc_ref, ...), custom_call_target="tpu_custom_call" | custom-call | tf_op jit(solution)/shard_map/scan_bwd/pallas_call | solution.py:363
  806.5 4.8 all-to-all-start.5
  812.7 8.8 multiply_reduce_fusion.1
  821.8 16.3 %all-to-all-done.5 = bf16[8,256,512]{2,1,0:T(8,128)(2,1)} async-done(((bf16[8,256,512]{2,1,0:T(8,128)(2,1)}), bf16[8,256,512]{2,1,0:T(8,128)(2,1)}, u32[]{:S(2)}, u32[]{:S(2)}) %all-to-all-start.5) | async-done | bytes 2097184 | tf_op jit(solution)/shard_map/all_to_all | solution.py:431
  838.0 8.0 fusion.82
  848.1 5.9 collective-permute-done.29
  862.5 8.0 collective-permute-done.31
  881.7 7.1 collective-permute-done.32
  891.0 6.5 reduce-scatter.9.cloned.1.call-done
  908.5 5.8 all-to-all-done.6
  (470 shorter events, 227.2 us)
Async XLA Ops:
  7.2 72.0 %all-gather.11.cloned.1.call-start = ((), (), s32[]{:S(2)}) async-start(), calls=%async_computation.12 | async-start | bytes 11943936 | tf_op jit(solution)/shard_map/all_gather | solution.py:427
  12.7 172.6 %all-gather.23.cloned.1.call-start = ((), (), s32[]{:S(2)}) async-start(), calls=%async_computation.22 | async-start | bytes 22560768 | tf_op jit(solution)/shard_map/all_gather | solution.py:427
  13.4 277.8 %all-gather.25.cloned.1.call-start = ((), (), s32[]{:S(2)}) async-start(), calls=%async_computation.23 | async-start | bytes 10616832 | tf_op jit(solution)/shard_map/all_gather | solution.py:427
  16.7 368.4 %all-gather.13.cloned.1.call-start = ((), (), s32[]{:S(2)}) async-start(), calls=%async_computation.13 | async-start | bytes 10616832 | tf_op jit(solution)/shard_map/all_gather | solution.py:427
  17.9 62.2 %copy-start.49 = (f32[2,1536]{1,0:T(2,128)S(1)}, f32[2,1536]{1,0:T(2,128)}, u32[]{:S(2)}) copy-start(f32[2,1536]{1,0:T(2,128)} %param.14) | copy-start | bytes 36868
  17.9 62.2 %copy-start = (f32[256,1536]{1,0:T(8,128)S(1)}, f32[256,1536]{1,0:T(8,128)}, u32[]{:S(2)}) copy-start(f32[256,1536]{1,0:T(8,128)} %param.11) | copy-start | bytes 4718596
  17.9 62.4 %copy-start.74 = (f32[2,48]{1,0:T(2,128)S(1)}, f32[2,48]{1,0:T(2,128)}, u32[]{:S(2)}) copy-start(f32[2,48]{1,0:T(2,128)} %param.17) | copy-start | bytes 1156
  17.9 62.5 %copy-start.75 = (f32[2,48]{1,0:T(2,128)S(1)}, f32[2,48]{1,0:T(2,128)}, u32[]{:S(2)}) copy-start(f32[2,48]{1,0:T(2,128)} %param.18) | copy-start | bytes 1156
  17.9 396.2 %all-gather.15.cloned.1.call-start = ((), (), s32[]{:S(2)}) async-start(), calls=%async_computation.14 | async-start | bytes 10616832 | tf_op jit(solution)/shard_map/all_gather | solution.py:427
  79.2 445.4 %all-gather.17.cloned.1.call-start = ((), (), s32[]{:S(2)}) async-start(), calls=%async_computation.15 | async-start | bytes 14155776 | tf_op jit(solution)/shard_map/all_gather | solution.py:427
  80.3 110.8 %copy-start.54 = (f32[256]{0:T(256)}, f32[256]{0:T(256)S(1)}, u32[]{:S(2)}) copy-start(f32[256]{0:T(256)S(1)} %multiply_reduce_fusion.5) | copy-start | bytes 3076
  80.4 110.8 %copy-start.50 = (f32[256]{0:T(256)}, f32[256]{0:T(256)S(1)}, u32[]{:S(2)}) copy-start(f32[256]{0:T(256)S(1)} %fusion.53) | copy-start | bytes 3076
  80.4 115.4 %copy-start.65 = (f32[48]{0:T(128)}, f32[48]{0:T(128)S(1)}, u32[]{:S(2)}) copy-start(f32[48]{0:T(128)S(1)} %get-tuple-element.219) | copy-start | bytes 580
  80.4 233.1 %copy-start.69 = (f32[48]{0:T(128)}, f32[48]{0:T(128)S(1)}, u32[]{:S(2)}) copy-start(f32[48]{0:T(128)S(1)} %get-tuple-element.218) | copy-start | bytes 580
  80.4 115.6 %copy-start.67 = (f32[48]{0:T(128)}, f32[48]{0:T(128)S(1)}, u32[]{:S(2)}) copy-start(f32[48]{0:T(128)S(1)} %get-tuple-element.217) | copy-start | bytes 580
  80.4 233.3 %copy-start.70 = (f32[48]{0:T(128)}, f32[48]{0:T(128)S(1)}, u32[]{:S(2)}) copy-start(f32[48]{0:T(128)S(1)} %get-tuple-element.216) | copy-start | bytes 580
  80.9 110.3 %copy-start.12 = (bf16[256,1536]{1,0:T(8,128)(2,1)}, bf16[256,1536]{1,0:T(8,128)(2,1)S(1)}, u32[]{:S(2)}) copy-start(bf16[256,1536]{1,0:T(8,128)(2,1)S(1)} %multiply_convert_fusion.1) | copy-start | bytes 2359300
  192.4 8.6 collective-permute-start
  219.1 13.4 %collective-permute-start.4 = (bf16[1536,128]{1,0:T(8,128)(2,1)}, bf16[1536,128]{1,0:T(8,128)(2,1)}, u32[]{:S(2)}, u32[]{:S(2)}) collective-permute-start(bf16[1536,128]{1,0:T(8,128)(2,1)} %get-tuple-element.185), channel_id=1, source_target_pairs={{0,1},{1,2},{2,3},{4,5},{5,6},{6,7},{8,9},{9,10},{10,11},{12,13},{... | collective-permute-start | bytes 1179656 | tf_op jit(solution)/shard_map/ppermute | solution.py:379
  224.4 17.9 %collective-permute-start.1 = (bf16[1536,128]{1,0:T(8,128)(2,1)}, bf16[1536,128]{1,0:T(8,128)(2,1)}, u32[]{:S(2)}, u32[]{:S(2)}) collective-permute-start(bf16[1536,128]{1,0:T(8,128)(2,1)} %get-tuple-element.186), channel_id=1, source_target_pairs={{0,1},{1,2},{2,3},{4,5},{5,6},{6,7},{8,9},{9,10},{10,11},{12,13},{... | collective-permute-start | bytes 1179656 | tf_op jit(solution)/shard_map/ppermute | solution.py:379
  234.5 13.8 %collective-permute-start.5 = (bf16[1536,128]{1,0:T(8,128)(2,1)}, bf16[1536,128]{1,0:T(8,128)(2,1)}, u32[]{:S(2)}, u32[]{:S(2)}) collective-permute-start(bf16[1536,128]{1,0:T(8,128)(2,1)} %add_convert_fusion.13), channel_id=1, source_target_pairs={{0,1},{1,2},{2,3},{4,5},{5,6},{6,7},{8,9},{9,10},{10,11},{12,13},{... | collective-permute-start | bytes 1179656 | tf_op jit(solution)/shard_map/ppermute | solution.py:379
  249.9 13.9 %collective-permute-start.2 = (bf16[1536,128]{1,0:T(8,128)(2,1)S(1)}, bf16[1536,128]{1,0:T(8,128)(2,1)S(1)}, u32[]{:S(2)}, u32[]{:S(2)}) collective-permute-start(bf16[1536,128]{1,0:T(8,128)(2,1)S(1)} %get-tuple-element.184), channel_id=1, source_target_pairs={{0,1},{1,2},{2,3},{4,5},{5,6},{6,7},{8,9},{9,10},{10,11},{12,13},{... | collective-permute-start | bytes 1179656 | tf_op jit(solution)/shard_map/ppermute | solution.py:379
  254.9 23.8 %collective-permute-start.6 = (bf16[1536,128]{1,0:T(8,128)(2,1)S(1)}, bf16[1536,128]{1,0:T(8,128)(2,1)S(1)}, u32[]{:S(2)}, u32[]{:S(2)}) collective-permute-start(bf16[1536,128]{1,0:T(8,128)(2,1)S(1)} %get-tuple-element.183), channel_id=1, source_target_pairs={{0,1},{1,2},{2,3},{4,5},{5,6},{6,7},{8,9},{9,10},{10,11},{12,13},{... | collective-permute-start | bytes 1179656 | tf_op jit(solution)/shard_map/ppermute | solution.py:379
  264.0 14.7 %collective-permute-start.3 = (bf16[1536,128]{1,0:T(8,128)(2,1)S(1)}, bf16[1536,128]{1,0:T(8,128)(2,1)S(1)}, u32[]{:S(2)}, u32[]{:S(2)}) collective-permute-start(bf16[1536,128]{1,0:T(8,128)(2,1)S(1)} %add_convert_fusion.14), channel_id=1, source_target_pairs={{0,1},{1,2},{2,3},{4,5},{5,6},{6,7},{8,9},{9,10},{10,11},{12,13},{... | collective-permute-start | bytes 1179656 | tf_op jit(solution)/shard_map/ppermute | solution.py:379
  309.2 9.5 %collective-permute-start.7 = (bf16[3,3328]{1,0:T(4,128)(2,1)S(1)}, bf16[3,3328]{1,0:T(4,128)(2,1)S(1)}, u32[]{:S(2)}, u32[]{:S(2)}) collective-permute-start(bf16[3,3328]{1,0:T(4,128)(2,1)S(1)} %slice.420), channel_id=1, source_target_pairs={{0,1},{1,2},{2,3},{4,5},{5,6},{6,7},{8,9},{9,10},{10,11},{12,13},{... | collective-permute-start | bytes 59912 | tf_op jit(solution)/shard_map/ppermute | solution.py:379
  336.3 13.0 %collective-permute-start.11 = (bf16[1536,128]{1,0:T(8,128)(2,1)}, bf16[1536,128]{1,0:T(8,128)(2,1)}, u32[]{:S(2)}, u32[]{:S(2)}) collective-permute-start(bf16[1536,128]{1,0:T(8,128)(2,1)} %get-tuple-element.181), channel_id=1, source_target_pairs={{0,1},{1,2},{2,3},{4,5},{5,6},{6,7},{8,9},{9,10},{10,11},{12,13},{... | collective-permute-start | bytes 1179656 | tf_op jit(solution)/shard_map/ppermute | solution.py:379
  340.8 17.0 %collective-permute-start.8 = (bf16[1536,128]{1,0:T(8,128)(2,1)}, bf16[1536,128]{1,0:T(8,128)(2,1)}, u32[]{:S(2)}, u32[]{:S(2)}) collective-permute-start(bf16[1536,128]{1,0:T(8,128)(2,1)} %get-tuple-element.182), channel_id=1, source_target_pairs={{0,1},{1,2},{2,3},{4,5},{5,6},{6,7},{8,9},{9,10},{10,11},{12,13},{... | collective-permute-start | bytes 1179656 | tf_op jit(solution)/shard_map/ppermute | solution.py:379
  351.4 11.9 %collective-permute-start.12 = (bf16[1536,128]{1,0:T(8,128)(2,1)}, bf16[1536,128]{1,0:T(8,128)(2,1)}, u32[]{:S(2)}, u32[]{:S(2)}) collective-permute-start(bf16[1536,128]{1,0:T(8,128)(2,1)} %add_convert_fusion.9), channel_id=1, source_target_pairs={{0,1},{1,2},{2,3},{4,5},{5,6},{6,7},{8,9},{9,10},{10,11},{12,13},{... | collective-permute-start | bytes 1179656 | tf_op jit(solution)/shard_map/ppermute | solution.py:379
  365.6 13.9 %collective-permute-start.9 = (bf16[1536,128]{1,0:T(8,128)(2,1)S(1)}, bf16[1536,128]{1,0:T(8,128)(2,1)S(1)}, u32[]{:S(2)}, u32[]{:S(2)}) collective-permute-start(bf16[1536,128]{1,0:T(8,128)(2,1)S(1)} %get-tuple-element.180), channel_id=1, source_target_pairs={{0,1},{1,2},{2,3},{4,5},{5,6},{6,7},{8,9},{9,10},{10,11},{12,13},{... | collective-permute-start | bytes 1179656 | tf_op jit(solution)/shard_map/ppermute | solution.py:379
  370.0 23.4 %collective-permute-start.13 = (bf16[1536,128]{1,0:T(8,128)(2,1)}, bf16[1536,128]{1,0:T(8,128)(2,1)}, u32[]{:S(2)}, u32[]{:S(2)}) collective-permute-start(bf16[1536,128]{1,0:T(8,128)(2,1)} %get-tuple-element.179), channel_id=1, source_target_pairs={{0,1},{1,2},{2,3},{4,5},{5,6},{6,7},{8,9},{9,10},{10,11},{12,13},{... | collective-permute-start | bytes 1179656 | tf_op jit(solution)/shard_map/ppermute | solution.py:379
  380.5 12.9 %collective-permute-start.10 = (bf16[1536,128]{1,0:T(8,128)(2,1)}, bf16[1536,128]{1,0:T(8,128)(2,1)S(1)}, u32[]{:S(2)}, u32[]{:S(2)}) collective-permute-start(bf16[1536,128]{1,0:T(8,128)(2,1)} %add_convert_fusion.10), channel_id=1, source_target_pairs={{0,1},{1,2},{2,3},{4,5},{5,6},{6,7},{8,9},{9,10},{10,11},{12,13},{... | collective-permute-start | bytes 1179656 | tf_op jit(solution)/shard_map/ppermute | solution.py:379
  409.7 42.7 %all-to-all-start = ((bf16[8,256,384]{2,1,0:T(8,128)(2,1)}), bf16[8,256,384]{2,1,0:T(8,128)(2,1)}, u32[]{:S(2)}, u32[]{:S(2)}) async-start(bf16[8,256,384]{2,1,0:T(8,128)(2,1)} %bitcast.179), calls=%async_computation | async-start | bytes 3145728 | tf_op jit(solution)/shard_map/all_to_all | solution.py:431
  452.4 25.3 %all-to-all-start.1 = ((bf16[8,256,384]{2,1,0:T(8,128)(2,1)}), bf16[8,256,384]{2,1,0:T(8,128)(2,1)}, u32[]{:S(2)}, u32[]{:S(2)}) async-start(bf16[8,256,384]{2,1,0:T(8,128)(2,1)} %bitcast.185), calls=%async_computation.1 | async-start | bytes 3145728 | tf_op jit(solution)/shard_map/all_to_all | solution.py:431
  456.6 154.9 %reduce-scatter.5.cloned.1.call-start = ((), (), s32[]{:S(2)}) async-start(), calls=%async_computation.17 | async-start | bytes 2949120 | tf_op jit(solution)/shard_map/reduce_scatter | solution.py:442
  457.6 13.6 %collective-permute-start.14 = (bf16[1536,128]{1,0:T(8,128)(2,1)S(1)}, bf16[1536,128]{1,0:T(8,128)(2,1)S(1)}, u32[]{:S(2)}, u32[]{:S(2)}) collective-permute-start(bf16[1536,128]{1,0:T(8,128)(2,1)S(1)} %get-tuple-element.178), channel_id=1, source_target_pairs={{1,0},{2,1},{3,2},{5,4},{6,5},{7,6},{9,8},{10,9},{11,10},{13,12},{... | collective-permute-start | bytes 1179656 | tf_op jit(solution)/shard_map/ppermute | solution.py:379
  468.1 22.8 %collective-permute-start.17 = (bf16[1536,128]{1,0:T(8,128)(2,1)}, bf16[1536,128]{1,0:T(8,128)(2,1)}, u32[]{:S(2)}, u32[]{:S(2)}) collective-permute-start(bf16[1536,128]{1,0:T(8,128)(2,1)} %get-tuple-element.177), channel_id=1, source_target_pairs={{1,0},{2,1},{3,2},{5,4},{6,5},{7,6},{9,8},{10,9},{11,10},{13,12},{... | collective-permute-start | bytes 1179656 | tf_op jit(solution)/shard_map/ppermute | solution.py:379
  472.2 18.7 %collective-permute-start.15 = (bf16[1536,128]{1,0:T(8,128)(2,1)}, bf16[1536,128]{1,0:T(8,128)(2,1)}, u32[]{:S(2)}, u32[]{:S(2)}) collective-permute-start(bf16[1536,128]{1,0:T(8,128)(2,1)} %add_convert_fusion.7), channel_id=1, source_target_pairs={{1,0},{2,1},{3,2},{5,4},{6,5},{7,6},{9,8},{10,9},{11,10},{13,12},{... | collective-permute-start | bytes 1179656 | tf_op jit(solution)/shard_map/ppermute | solution.py:379
  493.2 13.9 %collective-permute-start.18 = (bf16[1536,128]{1,0:T(8,128)(2,1)S(1)}, bf16[1536,128]{1,0:T(8,128)(2,1)S(1)}, u32[]{:S(2)}, u32[]{:S(2)}) collective-permute-start(bf16[1536,128]{1,0:T(8,128)(2,1)S(1)} %get-tuple-element.176), channel_id=1, source_target_pairs={{1,0},{2,1},{3,2},{5,4},{6,5},{7,6},{9,8},{10,9},{11,10},{13,12},{... | collective-permute-start | bytes 1179656 | tf_op jit(solution)/shard_map/ppermute | solution.py:379
  494.9 20.7 %collective-permute-start.16 = (bf16[1536,128]{1,0:T(8,128)(2,1)}, bf16[1536,128]{1,0:T(8,128)(2,1)}, u32[]{:S(2)}, u32[]{:S(2)}) collective-permute-start(bf16[1536,128]{1,0:T(8,128)(2,1)} %get-tuple-element.175), channel_id=1, source_target_pairs={{1,0},{2,1},{3,2},{5,4},{6,5},{7,6},{9,8},{10,9},{11,10},{13,12},{... | collective-permute-start | bytes 1179656 | tf_op jit(solution)/shard_map/ppermute | solution.py:379
  508.1 14.6 %collective-permute-start.19 = (bf16[1536,128]{1,0:T(8,128)(2,1)}, bf16[1536,128]{1,0:T(8,128)(2,1)S(1)}, u32[]{:S(2)}, u32[]{:S(2)}) collective-permute-start(bf16[1536,128]{1,0:T(8,128)(2,1)} %add_convert_fusion.4), channel_id=1, source_target_pairs={{1,0},{2,1},{3,2},{5,4},{6,5},{7,6},{9,8},{10,9},{11,10},{13,12},{... | collective-permute-start | bytes 1179656 | tf_op jit(solution)/shard_map/ppermute | solution.py:379
  549.2 185.0 %all-gather.19.cloned.1.call-start = ((), (), s32[]{:S(2)}) async-start(), calls=%async_computation.16 | async-start | bytes 7077888 | tf_op jit(solution)/shard_map/all_gather | solution.py:427
  551.9 44.7 %all-to-all-start.2 = ((bf16[8,256,384]{2,1,0:T(8,128)(2,1)}), bf16[8,256,384]{2,1,0:T(8,128)(2,1)S(1)}, u32[]{:S(2)}, u32[]{:S(2)}) async-start(bf16[8,256,384]{2,1,0:T(8,128)(2,1)} %bitcast.175), calls=%async_computation.2 | async-start | bytes 3145728 | tf_op jit(solution)/shard_map/all_to_all | solution.py:431
  555.5 186.5 %all-gather.21.cloned.1.call-start = ((), (), s32[]{:S(2)}) async-start(), calls=%async_computation.18 | async-start | bytes 7077888 | tf_op jit(solution)/shard_map/all_gather | solution.py:427
  593.2 6.4 collective-permute-start.20
  619.4 45.9 %all-to-all-start.3 = ((bf16[8,256,512]{2,1,0:T(8,128)(2,1)}), bf16[8,256,512]{2,1,0:T(8,128)(2,1)}, u32[]{:S(2)}, u32[]{:S(2)}) async-start(bf16[8,256,512]{2,1,0:T(8,128)(2,1)} %maximum_bitcast_fusion), calls=%async_computation.3 | async-start | bytes 4194304 | tf_op jit(solution)/shard_map/all_to_all | solution.py:431
  667.6 10.3 %collective-permute-start.21 = (bf16[1536,128]{1,0:T(8,128)(2,1)}, bf16[1536,128]{1,0:T(8,128)(2,1)}, u32[]{:S(2)}, u32[]{:S(2)}) collective-permute-start(bf16[1536,128]{1,0:T(8,128)(2,1)} %get-tuple-element.174), channel_id=1, source_target_pairs={{1,0},{2,1},{3,2},{5,4},{6,5},{7,6},{9,8},{10,9},{11,10},{13,12},{... | collective-permute-start | bytes 1179656 | tf_op jit(solution)/shard_map/ppermute | solution.py:379
  670.2 33.8 %all-to-all-start.4 = ((bf16[8,256,384]{2,1,0:T(8,128)(2,1)}), bf16[8,256,384]{2,1,0:T(8,128)(2,1)}, u32[]{:S(2)}, u32[]{:S(2)}) async-start(bf16[8,256,384]{2,1,0:T(8,128)(2,1)} %bitcast.186), calls=%async_computation.4 | async-start | bytes 3145728 | tf_op jit(solution)/shard_map/all_to_all | solution.py:431
  674.7 201.4 %reduce-scatter.11.cloned.1.call-start = ((), (), s32[]{:S(2)}) async-start(), calls=%async_computation.21 | async-start | bytes 1966080 | tf_op jit(solution)/shard_map/reduce_scatter | solution.py:442
  674.7 29.3 %collective-permute-start.24 = (bf16[1536,128]{1,0:T(8,128)(2,1)}, bf16[1536,128]{1,0:T(8,128)(2,1)}, u32[]{:S(2)}, u32[]{:S(2)}) collective-permute-start(bf16[1536,128]{1,0:T(8,128)(2,1)} %get-tuple-element.173), channel_id=1, source_target_pairs={{1,0},{2,1},{3,2},{5,4},{6,5},{7,6},{9,8},{10,9},{11,10},{13,12},{... | collective-permute-start | bytes 1179656 | tf_op jit(solution)/shard_map/ppermute | solution.py:379
  679.9 24.2 %collective-permute-start.22 = (bf16[1536,128]{1,0:T(8,128)(2,1)}, bf16[1536,128]{1,0:T(8,128)(2,1)}, u32[]{:S(2)}, u32[]{:S(2)}) collective-permute-start(bf16[1536,128]{1,0:T(8,128)(2,1)} %add_convert_fusion.3), channel_id=1, source_target_pairs={{1,0},{2,1},{3,2},{5,4},{6,5},{7,6},{9,8},{10,9},{11,10},{13,12},{... | collective-permute-start | bytes 1179656 | tf_op jit(solution)/shard_map/ppermute | solution.py:379
  705.7 14.5 %collective-permute-start.25 = (bf16[1536,128]{1,0:T(8,128)(2,1)S(1)}, bf16[1536,128]{1,0:T(8,128)(2,1)S(1)}, u32[]{:S(2)}, u32[]{:S(2)}) collective-permute-start(bf16[1536,128]{1,0:T(8,128)(2,1)S(1)} %get-tuple-element.172), channel_id=1, source_target_pairs={{1,0},{2,1},{3,2},{5,4},{6,5},{7,6},{9,8},{10,9},{11,10},{13,12},{... | collective-permute-start | bytes 1179656 | tf_op jit(solution)/shard_map/ppermute | solution.py:379
  707.0 23.1 %collective-permute-start.23 = (bf16[1536,128]{1,0:T(8,128)(2,1)S(1)}, bf16[1536,128]{1,0:T(8,128)(2,1)S(1)}, u32[]{:S(2)}, u32[]{:S(2)}) collective-permute-start(bf16[1536,128]{1,0:T(8,128)(2,1)S(1)} %get-tuple-element.171), channel_id=1, source_target_pairs={{1,0},{2,1},{3,2},{5,4},{6,5},{7,6},{9,8},{10,9},{11,10},{13,12},{... | collective-permute-start | bytes 1179656 | tf_op jit(solution)/shard_map/ppermute | solution.py:379
  720.5 12.7 %collective-permute-start.26 = (bf16[1536,128]{1,0:T(8,128)(2,1)S(1)}, bf16[1536,128]{1,0:T(8,128)(2,1)S(1)}, u32[]{:S(2)}, u32[]{:S(2)}) collective-permute-start(bf16[1536,128]{1,0:T(8,128)(2,1)S(1)} %add_convert_fusion), channel_id=1, source_target_pairs={{1,0},{2,1},{3,2},{5,4},{6,5},{7,6},{9,8},{10,9},{11,10},{13,12},{... | collective-permute-start | bytes 1179656 | tf_op jit(solution)/shard_map/ppermute | solution.py:379
  752.2 137.7 %reduce-scatter.7.cloned.1.call-start = ((), (), s32[]{:S(2)}) async-start(), calls=%async_computation.19 | async-start | bytes 2949120 | tf_op jit(solution)/shard_map/reduce_scatter | solution.py:442
  790.6 6.0 collective-permute-start.27
  806.5 31.5 %all-to-all-start.5 = ((bf16[8,256,512]{2,1,0:T(8,128)(2,1)}), bf16[8,256,512]{2,1,0:T(8,128)(2,1)}, u32[]{:S(2)}, u32[]{:S(2)}) async-start(bf16[8,256,512]{2,1,0:T(8,128)(2,1)} %maximum_bitcast_fusion.1), calls=%async_computation.7 | async-start | bytes 4194304 | tf_op jit(solution)/shard_map/all_to_all | solution.py:431
  811.3 86.2 %reduce-scatter.9.cloned.1.call-start = ((), (), s32[]{:S(2)}) async-start(), calls=%async_computation.20 | async-start | bytes 1966080 | tf_op jit(solution)/shard_map/reduce_scatter | solution.py:442
  846.1 1.4 collective-permute-start.28
  847.5 6.5 collective-permute-start.29
  854.0 5.7 collective-permute-start.30
  860.7 9.8 %collective-permute-start.31 = (f32[336,128]{1,0:T(8,128)S(1)}, f32[336,128]{1,0:T(8,128)S(1)}, u32[]{:S(2)}, u32[]{:S(2)}) collective-permute-start(f32[336,128]{1,0:T(8,128)S(1)} %add.230), channel_id=1, source_target_pairs={{0,1},{1,0},{2,3},{3,2},{4,5},{5,4},{6,7},{7,6},{8,9},{9,8},{10,11... | collective-permute-start | bytes 516104 | tf_op jit(solution)/shard_map/ppermute | solution.py:409
  870.5 18.2 %collective-permute-start.32 = (f32[336,128]{1,0:T(8,128)S(1)}, f32[336,128]{1,0:T(8,128)}, u32[]{:S(2)}, u32[]{:S(2)}) collective-permute-start(f32[336,128]{1,0:T(8,128)S(1)} %add.231), channel_id=1, source_target_pairs={{0,2},{1,3},{2,0},{3,1},{4,6},{5,7},{6,4},{7,5},{8,10},{9,11},{10,... | collective-permute-start | bytes 516104 | tf_op jit(solution)/shard_map/ppermute | solution.py:409
  878.1 21.2 %all-to-all-start.7 = ((bf16[8,48,806]{2,1,0:T(8,128)(2,1)}), bf16[8,48,806]{2,1,0:T(8,128)(2,1)S(1)}, u32[]{:S(2)}, u32[]{:S(2)}) async-start(bf16[8,48,806]{2,1,0:T(8,128)(2,1)} %bitcast.56), calls=%async_computation.11 | async-start | bytes 1376256 | tf_op jit(solution)/shard_map/all_to_all | solution.py:486
  899.4 15.0 %all-to-all-start.6 = ((bf16[8,48,806]{2,1,0:T(8,128)(2,1)}), bf16[8,48,806]{2,1,0:T(8,128)(2,1)S(1)}, u32[]{:S(2)}, u32[]{:S(2)}) async-start(bf16[8,48,806]{2,1,0:T(8,128)(2,1)} %bitcast.54), calls=%async_computation.9 | async-start | bytes 1376256 | tf_op jit(solution)/shard_map/all_to_all | solution.py:486
  (75 other events, 509.5 us)
Sparse Core Ops, SparseCore 0:
  12.8 66.3 all-gather.10
  81.7 103.5 all-gather.22
  187.2 58.6 all-gather.24
  247.6 58.6 all-gather.12
  308.7 58.7 all-gather.14
  369.2 91.5 all-gather.16
  549.3 47.7 reduce-scatter.4
  599.0 62.7 all-gather.18
  664.2 66.9 all-gather.20
  752.3 36.8 reduce-scatter.10
  792.1 46.5 reduce-scatter.6
  857.6 39.8 reduce-scatter.8

commit v6 on v5

--- a/solution.py
+++ b/solution.py
@@ -1,5 +1,3 @@
-import functools
-
 import jax
 import jax.numpy as jnp
 from jax import lax
@@ -7,6 +5,7 @@
 from jax.experimental.layout import Layout, with_layout_constraint
 from jax.experimental.pallas import tpu as pltpu
 from jax.sharding import PartitionSpec as P
+
 
 H = 48
 P_SIZE = 64
@@ -391,8 +390,9 @@
         own, factor = local_state[rows], totals[rows]
         incoming = passed_along(own.astype(BF), "ctx", steps)
         for hop in range(hops - 1):
-            if side is not None and chunk == 0 and hop == hops - 2:
-                incoming, side = lax.optimization_barrier((incoming, side))
+            if side is not None and hop == hops - 2:
+                incoming, done = lax.optimization_barrier((incoming, side[chunk]))
+                side = side[:chunk] + [done] + side[chunk + 1 :]
             incoming = passed_along((factor * incoming.astype(F32) + own).astype(BF), "ctx", steps)
         parts.append(incoming)
     return jnp.concatenate(parts, 0), side
@@ -517,9 +517,7 @@
     first = gathered(in_weight[0])
     weights = [(first[:, DI:], first[:, :DI], gathered(out_weight[0]))]
     for k in range(1, LAYERS):
-        w_conv = gathered(in_weight[k][:, DI:])
-        own_out, w_conv = lax.optimization_barrier((out_weight[k], w_conv))
-        weights.append((w_conv, gathered(in_weight[k][:, :DI]), gathered(own_out)))
+        weights.append((gathered(in_weight[k][:, DI:]), gathered(in_weight[k][:, :DI]), gathered(out_weight[k])))
     stream = activations
     kept = []
     for k in range(LAYERS):
@@ -551,35 +549,31 @@
         (stream_in, normed, gate_in, conv_in, halo, raw_steps, steps, col, row, totals, skip, bias, bc,
          incoming, ssm, gnormed) = kept[k]
         grad_bf = grad_stream.astype(BF)
+        if waiting is None:
+            normed_all, grad_all = gathered(by_run(normed)), gathered(grad_bf)
+        else:
+            normed_all = next_normed
+        if k:
+            next_normed = gathered(by_run(kept[k - 1][1]))
         d_gnormed = right_transposed(grad_bf, w_out)
         d_ssm, d_gate, g_gate, local_grad = gate_bwd(ssm, gate_in, d_gnormed, gate_gain[k][None, :], col, bc)
         local_grad, gnormed_cols = lax.optimization_barrier((local_grad, gnormed_cols))
+        side = [[right_transposed(d_gate, w_gate), gate_owners(d_gate)]]
         if waiting is None:
-            tokens = gathered(jnp.concatenate([by_run(normed), grad_bf], 1))
-            normed_all, grad_all = tokens[:, :model], tokens[:, model:]
+            side[0].append(stream)
+            side.append([rows_product(normed_all, side[0][1]).astype(BF), out_parts(gnormed_cols, grad_all)])
         else:
             local_grad, rest_cols = lax.optimization_barrier((local_grad, waiting[1]))
             own_grad, gate_sum = lax.optimization_barrier((grad_bf, waiting[2]))
-            normed_all, grad_all = next_normed, gathered(own_grad)
-        side = [right_transposed(d_gate, w_gate), gate_owners(d_gate)]
+            grad_all = gathered(own_grad)
+            side.append([rows_product(normed_all, side[0][1]).astype(BF), rest_parts(waiting[0], rest_cols)])
+        outgoing, side = carry(totals, local_grad, -1, side)
+        d_normed, part_gate = side[0][0], side[1][0]
         if waiting is None:
-            side.append(stream)
-        outgoing, side = carry(totals, local_grad, -1, side)
-        d_normed, gate_cols = side[:2]
-        if waiting is None:
-            stream = side[2]
-        if k:
-            own_normed, grad_all = lax.optimization_barrier((by_run(kept[k - 1][1]), grad_all))
-            next_normed = gathered(own_normed)
-        part_gate = rows_product(normed_all, gate_cols).astype(BF)
-        part_out = out_parts(gnormed_cols, grad_all)
-        if waiting is None:
-            outgoing, part_gate, part_out = lax.optimization_barrier((outgoing, part_gate, part_out))
+            stream, part_out = side[0][2], side[1][1]
         else:
-            part_rest = rest_parts(waiting[0], rest_cols)
-            outgoing, part_gate, part_out, part_rest = lax.optimization_barrier(
-                (outgoing, part_gate, part_out, part_rest))
-            owned_ins.append(late_sum(part_rest, gate_sum))
+            outgoing, part_out = lax.optimization_barrier((outgoing, out_parts(gnormed_cols, grad_all)))
+            owned_ins.append(late_sum(side[1][1], gate_sum))
         if k:
             outgoing, next_gnormed = lax.optimization_barrier((outgoing, kept[k - 1][-1]))
             gnormed_cols = to_owners(next_gnormed.reshape(rows, lax.axis_size("fsdp"), -1))

time: 934 us -> 934 us (level)
  waiting for transfers between devices: 345 us -> 334 us
    ppermute x28, waiting for transfers between devices: 95.8 us -> 144 us  [passed_along(): lax.ppermute(value, axis, [(source, source + steps) for source in range(i...]
    all_gather x8 -> x9, waiting for transfers between devices: 164 us -> 134 us  [gathered(): return lax.all_gather(value, 'fsdp', axis=0, tiled=True)]
    all_to_all x6, waiting for transfers between devices: 45.8 us -> 30.4 us  [to_owners(): lax.all_to_all(jnp.transpose(split, (1, 0, 2)), 'fsdp', split_axis=0, con...]
    ppermute x5, waiting for transfers between devices: 24.7 us -> 9.5 us  [all_sum(): lax.ppermute(value, axis, [(i, i ^ bit) for i in range(count)])]
    all_to_all x6, starting transfers between devices: 26 us -> 36.2 us  [to_owners(): lax.all_to_all(jnp.transpose(split, (1, 0, 2)), 'fsdp', split_axis=0, con...]
  transfers between devices with their start and end apart: 53 -> 54, of which waited for: 32 -> 31; matrix products, arithmetic and copies ran while one was open for 26% -> 30% of each run, Pallas kernels for 16% -> 16%
where the time goes in v6:
time: 934 us; the launch traced here: 923 us
  waiting for transfers between devices  334 us (36%)
  Pallas kernels  152 us (16%)
  matrix products  136 us (15%)
  starting transfers between devices  123 us (13%)
  local copies, waits for them, and re-layouts  106 us (11%)
  other arithmetic  56.1 us (6%)
  between operations  16 us (2%)
    ppermute x28, waiting for transfers between devices, passed_along(): lax.ppermute(value, axis, [(source, source + steps) for source in range(i...  144 us
    all_gather x9, waiting for transfers between devices, gathered(): return lax.all_gather(value, 'fsdp', axis=0, tiled=True)  134 us
    ppermute x28, starting transfers between devices, passed_along(): lax.ppermute(value, axis, [(source, source + steps) for source in range(i...  77.6 us
    pallas_call x2, Pallas kernels, scan_bwd(): pl.pallas_call(scan_bwd_kernel, grid=(G,), in_specs=conv_specs(rows) + [f...  53.9 us
    dot_general x6, matrix products, right_transposed(): lax.dot_general(left, right, (((1,), (1,)), ((), ())), preferred_element_...  47.7 us
    pallas_call x2, Pallas kernels, gate_bwd(): pl.pallas_call(gate_bwd_kernel, grid=(2, G), in_specs=[block, block, bloc...  46.2 us
    dot_general x6, matrix products, rows_product(): lax.dot_general(left, right, (((0,), (0,)), ((), ())), preferred_element_...  42.7 us
    all_to_all x6, starting transfers between devices, to_owners(): lax.all_to_all(jnp.transpose(split, (1, 0, 2)), 'fsdp', split_axis=0, con...  36.2 us
  transfers between devices with their start and end apart: 54, of which 31 were waited for; matrix products, arithmetic and copies ran while one was open for 30% of the time, Pallas kernels for 16%

profile of v6, /device:TPU:0, one launch (start us, length us, event | category | flops | bytes accessed | tf_op | source)
XLA Modules:
  0.0 923.5 jit_solution(14508452972615003596)
XLA Ops:
  7.2 4.3 slice_bitcast_fusion
  22.8 95.2 %all-gather.25.cloned.1.call-done = bf16[1,1536,6448]{2,1,0:T(8,128)(2,1)} async-done(((bf16[1,192,6448]{2,1,0:T(8,128)(2,1)}), bf16[1,1536,6448]{2,1,0:T(8,128)(2,1)}) %all-gather.25.cloned.1.call-update) | async-done | bytes 19808272 | tf_op jit(solution)/shard_map/all_gather | solution.py:427
  118.0 5.9 fusion.79
  134.3 14.5 %scan_fwd.2 = (f32[256,3072]{1,0:T(8,128)}, f32[3072,128]{1,0:T(8,128)}, f32[256,256]{1,0:T(8,128)}) custom-call(bf16[256,3328]{1,0:T(8,128)(2,1)} %slice.400.conv_ref.conv_bc_ref, bf16[256,3328]{1,0:T(8,128)(2,1)} %slice.400.conv_ref.conv_bc_ref, f32[8,3328]{1,0:T(8,128)} %pad_convert_fusion.1.halo_ref.halo_bc_ref, ...), custom_call_target="tpu_custom_call" | custom-call | tf_op jit(solution)/shard_map/scan_fwd/pallas_call | solution.py:317
  151.8 4.3 collective-permute-start.4
  160.5 4.7 collective-permute-done.4
  167.2 5.3 collective-permute-start.5
  173.6 7.4 collective-permute-done.5
  182.6 4.4 collective-permute-start.2
  191.0 5.4 collective-permute-done.2
  196.7 4.9 collective-permute-start.3
  201.6 7.9 fusion.14.gate_ref
  212.4 11.7 %gate_fwd.2 = (f32[256,3072]{1,0:T(8,128)}, bf16[256,3072]{1,0:T(8,128)(2,1)}) custom-call(f32[256,3072]{1,0:T(8,128)} %get-tuple-element.74.y_ref, f32[256,3072]{1,0:T(8,128)} %fusion.14.gate_ref, bf16[3072,128]{1,0:T(8,128)(2,1)} %copy-done.11, f32[256,256]{1,0:T(8,128)} %get-tuple-element.76.bc_ref, f32[12,256,8]{2,1,0:T(8,128)} %copy.217.col_ref, ...), custom_call_target="tpu_custom_call" | custom-call | tf_op jit(solution)/shard_map/gate_fwd/pallas_call | solution.py:330
  224.1 5.9 multiply_reduce_fusion.4
  232.6 11.6 %all-gather.13.cloned.1.call-done = bf16[1536,3376]{1,0:T(8,128)(2,1)} async-done(((bf16[192,3376]{1,0:T(8,128)(2,1)}), bf16[1536,3376]{1,0:T(8,128)(2,1)}) %all-gather.13.cloned.1.call-update) | async-done | bytes 10371088 | tf_op jit(solution)/shard_map/all_gather | solution.py:427
  244.2 5.9 fusion.80
  260.4 14.5 %scan_fwd.3 = (f32[256,3072]{1,0:T(8,128)}, f32[3072,128]{1,0:T(8,128)}, f32[256,256]{1,0:T(8,128)}) custom-call(bf16[256,3328]{1,0:T(8,128)(2,1)} %slice.411.conv_ref.conv_bc_ref, bf16[256,3328]{1,0:T(8,128)(2,1)} %slice.411.conv_ref.conv_bc_ref, f32[8,3328]{1,0:T(8,128)} %pad_convert_fusion.halo_ref.halo_bc_ref, ...), custom_call_target="tpu_custom_call" | custom-call | tf_op jit(solution)/shard_map/scan_fwd/pallas_call | solution.py:317
  277.9 4.3 collective-permute-start.11
  286.0 5.2 collective-permute-done.11
  293.3 5.2 collective-permute-start.12
  299.7 7.5 collective-permute-done.12
  309.5 4.4 collective-permute-start.9
  313.9 4.1 collective-permute-start.13
  318.0 5.3 collective-permute-done.9
  324.4 4.6 collective-permute-start.10
  329.0 8.6 fusion.81.gate_ref
  340.5 11.5 %gate_fwd.3 = (f32[256,3072]{1,0:T(8,128)}, bf16[256,3072]{1,0:T(8,128)(2,1)}) custom-call(f32[256,3072]{1,0:T(8,128)} %get-tuple-element.78.y_ref, f32[256,3072]{1,0:T(8,128)} %fusion.81.gate_ref, bf16[3072,128]{1,0:T(8,128)(2,1)} %copy-done.12, f32[256,256]{1,0:T(8,128)} %get-tuple-element.80.bc_ref, f32[12,256,8]{2,1,0:T(8,128)} %copy.224.col_ref, ...), custom_call_target="tpu_custom_call" | custom-call | tf_op jit(solution)/shard_map/gate_fwd/pallas_call | solution.py:330
  354.8 4.4 all-to-all-start
  359.2 7.8 all-gather.29.cloned.1.call-done
  367.0 8.1 fusion.2.dn_ref
  375.1 23.2 %gate_bwd.2 = (f32[256,3072]{1,0:T(8,128)}, bf16[256,3072]{1,0:T(8,128)(2,1)}, f32[1,3072]{1,0:T(1,128)}, f32[3072,128]{1,0:T(8,128)}) custom-call(f32[256,3072]{1,0:T(8,128)} %get-tuple-element.81.ssm_ref, f32[256,3072]{1,0:T(8,128)} %fusion.81.gate_ref, f32[256,3072]{1,0:T(8,128)} %fusion.2.dn_ref, f32[1,3072]{1,0:T(1,128)} %get-tuple-element.202.gain_ref, ...), custom_call_target="tpu_custom_call" | custom-call | tf_op jit(solution)/shard_map/gate_bwd/pallas_call | solution.py:345
  401.2 7.5 fusion.21
  408.7 7.4 all-to-all-start.1
  418.2 8.0 fusion.82
  432.9 6.9 convolution_convert_fusion.2
  452.7 19.6 %all-gather.17.cloned.1.call-done = bf16[2048,1536]{0,1:T(8,128)(2,1)} async-done(((bf16[256,1536]{0,1:T(8,128)(2,1)}), bf16[2048,1536]{0,1:T(8,128)(2,1)}) %all-gather.17.cloned.1.call-update) | async-done | bytes 6291472 | tf_op jit(solution)/shard_map/all_gather | solution.py:427
  472.3 6.7 convolution_convert_fusion.3
  489.3 24.7 %collective-permute-done.16 = bf16[1536,128]{1,0:T(8,128)(2,1)S(1)} collective-permute-done((bf16[1536,128]{1,0:T(8,128)(2,1)}, bf16[1536,128]{1,0:T(8,128)(2,1)S(1)}, u32[]{:S(2)}, u32[]{:S(2)}) %collective-permute-start.16) | collective-permute-done | bytes 393248 | tf_op jit(solution)/shard_map/ppermute | solution.py:378
  514.1 27.7 %collective-permute-done.19 = bf16[1536,128]{1,0:T(8,128)(2,1)S(1)} collective-permute-done((bf16[1536,128]{1,0:T(8,128)(2,1)S(1)}, bf16[1536,128]{1,0:T(8,128)(2,1)S(1)}, u32[]{:S(2)}, u32[]{:S(2)}) %collective-permute-start.19) | collective-permute-done | bytes 393248 | tf_op jit(solution)/shard_map/ppermute | solution.py:378
  544.0 3.6 all-to-all-start.2
  548.4 27.0 %scan_bwd.2 = (f32[256,3072]{1,0:T(8,128)}, f32[8,3072]{1,0:T(8,128)}, f32[8,3072]{1,0:T(8,128)}, f32[256,256]{1,0:T(8,128)}, f32[8,256]{1,0:T(8,128)}, /*index=...) custom-call(bf16[256,3328]{1,0:T(8,128)(2,1)} %slice.411.conv_ref.conv_bc_ref, ...), custom_call_target="tpu_custom_call" | custom-call | tf_op jit(solution)/shard_map/scan_bwd/pallas_call | solution.py:362
  594.5 6.8 multiply_reduce_fusion
  611.0 4.5 all-to-all-start.3
  615.6 8.1 fusion.4.dn_ref
  623.6 23.0 %gate_bwd.3 = (f32[256,3072]{1,0:T(8,128)}, bf16[256,3072]{1,0:T(8,128)(2,1)}, f32[1,3072]{1,0:T(1,128)}, f32[3072,128]{1,0:T(8,128)}) custom-call(f32[256,3072]{1,0:T(8,128)} %get-tuple-element.102.ssm_ref, f32[256,3072]{1,0:T(8,128)} %fusion.14.gate_ref, f32[256,3072]{1,0:T(8,128)} %fusion.4.dn_ref, f32[1,3072]{1,0:T(1,128)} %get-tuple-element.203.gain_ref, ...), custom_call_target="tpu_custom_call" | custom-call | tf_op jit(solution)/shard_map/gate_bwd/pallas_call | solution.py:345
  649.3 4.5 all-to-all-start.4
  656.0 8.0 fusion.12
  670.6 14.2 %all-to-all-done.4 = bf16[8,256,384]{2,1,0:T(8,128)(2,1)} async-done(((bf16[8,256,384]{2,1,0:T(8,128)(2,1)}), bf16[8,256,384]{2,1,0:T(8,128)(2,1)}, u32[]{:S(2)}, u32[]{:S(2)}) %all-to-all-start.4) | async-done | bytes 1572896 | tf_op jit(solution)/shard_map/all_to_all | solution.py:431
  684.7 7.8 convolution_convert_fusion.1
  696.3 6.1 fusion.83
  712.8 17.4 %collective-permute-done.23 = bf16[1536,128]{1,0:T(8,128)(2,1)} collective-permute-done((bf16[1536,128]{1,0:T(8,128)(2,1)}, bf16[1536,128]{1,0:T(8,128)(2,1)}, u32[]{:S(2)}, u32[]{:S(2)}) %collective-permute-start.23) | collective-permute-done | bytes 393248 | tf_op jit(solution)/shard_map/ppermute | solution.py:378
  730.2 16.9 %collective-permute-done.26 = bf16[1536,128]{1,0:T(8,128)(2,1)S(1)} collective-permute-done((bf16[1536,128]{1,0:T(8,128)(2,1)}, bf16[1536,128]{1,0:T(8,128)(2,1)S(1)}, u32[]{:S(2)}, u32[]{:S(2)}) %collective-permute-start.26) | collective-permute-done | bytes 393248 | tf_op jit(solution)/shard_map/ppermute | solution.py:378
  749.2 7.0 convolution_convert_fusion
  759.8 26.9 %scan_bwd.3 = (f32[256,3072]{1,0:T(8,128)}, f32[8,3072]{1,0:T(8,128)}, f32[8,3072]{1,0:T(8,128)}, f32[256,256]{1,0:T(8,128)}, f32[8,256]{1,0:T(8,128)}, /*index=...) custom-call(bf16[256,3328]{1,0:T(8,128)(2,1)} %slice.400.conv_ref.conv_bc_ref, ...), custom_call_target="tpu_custom_call" | custom-call | tf_op jit(solution)/shard_map/scan_bwd/pallas_call | solution.py:362
  810.2 11.8 %all-to-all-start.5 = ((bf16[8,256,512]{2,1,0:T(8,128)(2,1)}), bf16[8,256,512]{2,1,0:T(8,128)(2,1)}, u32[]{:S(2)}, u32[]{:S(2)}) async-start(bf16[8,256,512]{2,1,0:T(8,128)(2,1)} %maximum_bitcast_fusion.1), calls=%async_computation.7 | async-start | bytes 4194304 | tf_op jit(solution)/shard_map/all_to_all | solution.py:431
  823.5 8.8 multiply_reduce_fusion.1
  832.5 16.2 %all-to-all-done.5 = bf16[8,256,512]{2,1,0:T(8,128)(2,1)} async-done(((bf16[8,256,512]{2,1,0:T(8,128)(2,1)}), bf16[8,256,512]{2,1,0:T(8,128)(2,1)}, u32[]{:S(2)}, u32[]{:S(2)}) %all-to-all-start.5) | async-done | bytes 2097184 | tf_op jit(solution)/shard_map/all_to_all | solution.py:431
  848.8 8.1 fusion.84
  859.7 3.5 all-to-all-start.7
  864.7 10.0 %all-to-all-done.7 = bf16[8,48,806]{2,1,0:T(8,128)(2,1)S(1)} async-done(((bf16[8,48,806]{2,1,0:T(8,128)(2,1)}), bf16[8,48,806]{2,1,0:T(8,128)(2,1)S(1)}, u32[]{:S(2)}, u32[]{:S(2)}) %all-to-all-start.7) | async-done | bytes 619040 | tf_op jit(solution)/shard_map/all_to_all | solution.py:486
  884.6 5.6 collective-permute-done.30
  890.4 3.4 fusion.32
  898.9 3.7 all-to-all-start.6
  909.5 4.6 all-to-all-done.6
  (477 shorter events, 223.7 us)
Async XLA Ops:
  7.2 110.8 %all-gather.25.cloned.1.call-start = ((), (), s32[]{:S(2)}) async-start(), calls=%async_computation.22 | async-start | bytes 22560768 | tf_op jit(solution)/shard_map/all_gather | solution.py:427
  11.5 212.6 %all-gather.27.cloned.1.call-start = ((), (), s32[]{:S(2)}) async-start(), calls=%async_computation.23 | async-start | bytes 10616832 | tf_op jit(solution)/shard_map/all_gather | solution.py:427
  14.8 229.4 %all-gather.13.cloned.1.call-start = ((), (), s32[]{:S(2)}) async-start(), calls=%async_computation.12 | async-start | bytes 11943936 | tf_op jit(solution)/shard_map/all_gather | solution.py:427
  16.0 313.0 %all-gather.15.cloned.1.call-start = ((), (), s32[]{:S(2)}) async-start(), calls=%async_computation.13 | async-start | bytes 10616832 | tf_op jit(solution)/shard_map/all_gather | solution.py:427
  17.2 349.8 %all-gather.29.cloned.1.call-start = ((), (), s32[]{:S(2)}) async-start(), calls=%async_computation.24 | async-start | bytes 10616832 | tf_op jit(solution)/shard_map/all_gather | solution.py:427
  17.8 415.1 %all-gather.19.cloned.1.call-start = ((), (), s32[]{:S(2)}) async-start(), calls=%async_computation.15 | async-start | bytes 7077888 | tf_op jit(solution)/shard_map/all_gather | solution.py:427
  19.7 452.7 %all-gather.17.cloned.1.call-start = ((), (), s32[]{:S(2)}) async-start(), calls=%async_computation.14 | async-start | bytes 7077888 | tf_op jit(solution)/shard_map/all_gather | solution.py:427
  20.3 103.6 %copy-start.55 = (f32[256]{0:T(256)}, f32[256]{0:T(256)S(1)}, u32[]{:S(2)}) copy-start(f32[256]{0:T(256)S(1)} %fusion.53) | copy-start | bytes 3076
  20.3 108.2 %copy-start.70 = (f32[48]{0:T(128)}, f32[48]{0:T(128)S(1)}, u32[]{:S(2)}) copy-start(f32[48]{0:T(128)S(1)} %get-tuple-element.209) | copy-start | bytes 580
  20.3 234.4 %copy-start.74 = (f32[48]{0:T(128)}, f32[48]{0:T(128)S(1)}, u32[]{:S(2)}) copy-start(f32[48]{0:T(128)S(1)} %get-tuple-element.208) | copy-start | bytes 580
  20.3 108.4 %copy-start.72 = (f32[48]{0:T(128)}, f32[48]{0:T(128)S(1)}, u32[]{:S(2)}) copy-start(f32[48]{0:T(128)S(1)} %get-tuple-element.207) | copy-start | bytes 580
  20.3 234.5 %copy-start.75 = (f32[48]{0:T(128)}, f32[48]{0:T(128)S(1)}, u32[]{:S(2)}) copy-start(f32[48]{0:T(128)S(1)} %get-tuple-element.206) | copy-start | bytes 580
  21.2 102.7 %copy-start.43 = (f32[1536]{0:T(1024)}, f32[1536]{0:T(1024)S(1)}, u32[]{:S(2)}) copy-start(f32[1536]{0:T(1024)S(1)} %get-tuple-element.150) | copy-start | bytes 18436
  21.4 102.4 %copy-start.15 = (bf16[256,1536]{1,0:T(8,128)(2,1)}, bf16[256,1536]{1,0:T(8,128)(2,1)S(1)}, u32[]{:S(2)}) copy-start(bf16[256,1536]{1,0:T(8,128)(2,1)S(1)} %multiply_convert_fusion.1) | copy-start | bytes 2359300
  125.1 8.6 collective-permute-start
  151.8 13.3 %collective-permute-start.4 = (bf16[1536,128]{1,0:T(8,128)(2,1)}, bf16[1536,128]{1,0:T(8,128)(2,1)}, u32[]{:S(2)}, u32[]{:S(2)}) collective-permute-start(bf16[1536,128]{1,0:T(8,128)(2,1)} %get-tuple-element.175), channel_id=1, source_target_pairs={{0,1},{1,2},{2,3},{4,5},{5,6},{6,7},{8,9},{9,10},{10,11},{12,13},{... | collective-permute-start | bytes 1179656 | tf_op jit(solution)/shard_map/ppermute | solution.py:378
  157.1 16.5 %collective-permute-start.1 = (bf16[1536,128]{1,0:T(8,128)(2,1)}, bf16[1536,128]{1,0:T(8,128)(2,1)}, u32[]{:S(2)}, u32[]{:S(2)}) collective-permute-start(bf16[1536,128]{1,0:T(8,128)(2,1)} %get-tuple-element.176), channel_id=1, source_target_pairs={{0,1},{1,2},{2,3},{4,5},{5,6},{6,7},{8,9},{9,10},{10,11},{12,13},{... | collective-permute-start | bytes 1179656 | tf_op jit(solution)/shard_map/ppermute | solution.py:378
  167.2 13.8 %collective-permute-start.5 = (bf16[1536,128]{1,0:T(8,128)(2,1)}, bf16[1536,128]{1,0:T(8,128)(2,1)}, u32[]{:S(2)}, u32[]{:S(2)}) collective-permute-start(bf16[1536,128]{1,0:T(8,128)(2,1)} %add_convert_fusion.13), channel_id=1, source_target_pairs={{0,1},{1,2},{2,3},{4,5},{5,6},{6,7},{8,9},{9,10},{10,11},{12,13},{... | collective-permute-start | bytes 1179656 | tf_op jit(solution)/shard_map/ppermute | solution.py:378
  173.3 28.3 %copy-start.16 = (bf16[256,1536]{1,0:T(8,128)(2,1)S(1)}, bf16[256,1536]{1,0:T(8,128)(2,1)}, u32[]{:S(2)}) copy-start(bf16[256,1536]{1,0:T(8,128)(2,1)} %copy-done.15) | copy-start | bytes 2359300
  182.6 13.9 %collective-permute-start.2 = (bf16[1536,128]{1,0:T(8,128)(2,1)S(1)}, bf16[1536,128]{1,0:T(8,128)(2,1)S(1)}, u32[]{:S(2)}, u32[]{:S(2)}) collective-permute-start(bf16[1536,128]{1,0:T(8,128)(2,1)S(1)} %get-tuple-element.174), channel_id=1, source_target_pairs={{0,1},{1,2},{2,3},{4,5},{5,6},{6,7},{8,9},{9,10},{10,11},{12,13},{... | collective-permute-start | bytes 1179656 | tf_op jit(solution)/shard_map/ppermute | solution.py:378
  187.6 23.8 %collective-permute-start.6 = (bf16[1536,128]{1,0:T(8,128)(2,1)S(1)}, bf16[1536,128]{1,0:T(8,128)(2,1)S(1)}, u32[]{:S(2)}, u32[]{:S(2)}) collective-permute-start(bf16[1536,128]{1,0:T(8,128)(2,1)S(1)} %get-tuple-element.173), channel_id=1, source_target_pairs={{0,1},{1,2},{2,3},{4,5},{5,6},{6,7},{8,9},{9,10},{10,11},{12,13},{... | collective-permute-start | bytes 1179656 | tf_op jit(solution)/shard_map/ppermute | solution.py:378
  196.7 14.7 %collective-permute-start.3 = (bf16[1536,128]{1,0:T(8,128)(2,1)S(1)}, bf16[1536,128]{1,0:T(8,128)(2,1)S(1)}, u32[]{:S(2)}, u32[]{:S(2)}) collective-permute-start(bf16[1536,128]{1,0:T(8,128)(2,1)S(1)} %add_convert_fusion.14), channel_id=1, source_target_pairs={{0,1},{1,2},{2,3},{4,5},{5,6},{6,7},{8,9},{9,10},{10,11},{12,13},{... | collective-permute-start | bytes 1179656 | tf_op jit(solution)/shard_map/ppermute | solution.py:378
  251.3 8.5 collective-permute-start.7
  277.9 13.4 %collective-permute-start.11 = (bf16[1536,128]{1,0:T(8,128)(2,1)}, bf16[1536,128]{1,0:T(8,128)(2,1)}, u32[]{:S(2)}, u32[]{:S(2)}) collective-permute-start(bf16[1536,128]{1,0:T(8,128)(2,1)} %get-tuple-element.171), channel_id=1, source_target_pairs={{0,1},{1,2},{2,3},{4,5},{5,6},{6,7},{8,9},{9,10},{10,11},{12,13},{... | collective-permute-start | bytes 1179656 | tf_op jit(solution)/shard_map/ppermute | solution.py:378
  282.7 17.0 %collective-permute-start.8 = (bf16[1536,128]{1,0:T(8,128)(2,1)}, bf16[1536,128]{1,0:T(8,128)(2,1)}, u32[]{:S(2)}, u32[]{:S(2)}) collective-permute-start(bf16[1536,128]{1,0:T(8,128)(2,1)} %get-tuple-element.172), channel_id=1, source_target_pairs={{0,1},{1,2},{2,3},{4,5},{5,6},{6,7},{8,9},{9,10},{10,11},{12,13},{... | collective-permute-start | bytes 1179656 | tf_op jit(solution)/shard_map/ppermute | solution.py:378
  293.3 13.9 %collective-permute-start.12 = (bf16[1536,128]{1,0:T(8,128)(2,1)}, bf16[1536,128]{1,0:T(8,128)(2,1)}, u32[]{:S(2)}, u32[]{:S(2)}) collective-permute-start(bf16[1536,128]{1,0:T(8,128)(2,1)} %add_convert_fusion.9), channel_id=1, source_target_pairs={{0,1},{1,2},{2,3},{4,5},{5,6},{6,7},{8,9},{9,10},{10,11},{12,13},{... | collective-permute-start | bytes 1179656 | tf_op jit(solution)/shard_map/ppermute | solution.py:378
  309.5 13.9 %collective-permute-start.9 = (bf16[1536,128]{1,0:T(8,128)(2,1)S(1)}, bf16[1536,128]{1,0:T(8,128)(2,1)S(1)}, u32[]{:S(2)}, u32[]{:S(2)}) collective-permute-start(bf16[1536,128]{1,0:T(8,128)(2,1)S(1)} %get-tuple-element.170), channel_id=1, source_target_pairs={{0,1},{1,2},{2,3},{4,5},{5,6},{6,7},{8,9},{9,10},{10,11},{12,13},{... | collective-permute-start | bytes 1179656 | tf_op jit(solution)/shard_map/ppermute | solution.py:378
  313.9 24.6 %collective-permute-start.13 = (bf16[1536,128]{1,0:T(8,128)(2,1)}, bf16[1536,128]{1,0:T(8,128)(2,1)}, u32[]{:S(2)}, u32[]{:S(2)}) collective-permute-start(bf16[1536,128]{1,0:T(8,128)(2,1)} %get-tuple-element.169), channel_id=1, source_target_pairs={{0,1},{1,2},{2,3},{4,5},{5,6},{6,7},{8,9},{9,10},{10,11},{12,13},{... | collective-permute-start | bytes 1179656 | tf_op jit(solution)/shard_map/ppermute | solution.py:378
  324.4 14.1 %collective-permute-start.10 = (bf16[1536,128]{1,0:T(8,128)(2,1)}, bf16[1536,128]{1,0:T(8,128)(2,1)S(1)}, u32[]{:S(2)}, u32[]{:S(2)}) collective-permute-start(bf16[1536,128]{1,0:T(8,128)(2,1)} %add_convert_fusion.10), channel_id=1, source_target_pairs={{0,1},{1,2},{2,3},{4,5},{5,6},{6,7},{8,9},{9,10},{10,11},{12,13},{... | collective-permute-start | bytes 1179656 | tf_op jit(solution)/shard_map/ppermute | solution.py:378
  354.8 53.9 %all-to-all-start = ((bf16[8,256,384]{2,1,0:T(8,128)(2,1)}), bf16[8,256,384]{2,1,0:T(8,128)(2,1)}, u32[]{:S(2)}, u32[]{:S(2)}) async-start(bf16[8,256,384]{2,1,0:T(8,128)(2,1)} %bitcast.182), calls=%async_computation | async-start | bytes 3145728 | tf_op jit(solution)/shard_map/all_to_all | solution.py:431
  408.7 36.9 %all-to-all-start.1 = ((bf16[8,256,384]{2,1,0:T(8,128)(2,1)}), bf16[8,256,384]{2,1,0:T(8,128)(2,1)}, u32[]{:S(2)}, u32[]{:S(2)}) async-start(bf16[8,256,384]{2,1,0:T(8,128)(2,1)} %bitcast.188), calls=%async_computation.1 | async-start | bytes 3145728 | tf_op jit(solution)/shard_map/all_to_all | solution.py:431
  416.0 187.2 %reduce-scatter.5.cloned.1.call-start = ((), (), s32[]{:S(2)}) async-start(), calls=%async_computation.17 | async-start | bytes 2949120 | tf_op jit(solution)/shard_map/reduce_scatter | solution.py:442
  416.9 13.4 %collective-permute-start.14 = (bf16[1536,128]{1,0:T(8,128)(2,1)S(1)}, bf16[1536,128]{1,0:T(8,128)(2,1)S(1)}, u32[]{:S(2)}, u32[]{:S(2)}) collective-permute-start(bf16[1536,128]{1,0:T(8,128)(2,1)S(1)} %get-tuple-element.168), channel_id=1, source_target_pairs={{1,0},{2,1},{3,2},{5,4},{6,5},{7,6},{9,8},{10,9},{11,10},{13,12},{... | collective-permute-start | bytes 1179656 | tf_op jit(solution)/shard_map/ppermute | solution.py:378
  426.2 22.7 %collective-permute-start.17 = (bf16[1536,128]{1,0:T(8,128)(2,1)}, bf16[1536,128]{1,0:T(8,128)(2,1)}, u32[]{:S(2)}, u32[]{:S(2)}) collective-permute-start(bf16[1536,128]{1,0:T(8,128)(2,1)} %get-tuple-element.167), channel_id=1, source_target_pairs={{1,0},{2,1},{3,2},{5,4},{6,5},{7,6},{9,8},{10,9},{11,10},{13,12},{... | collective-permute-start | bytes 1179656 | tf_op jit(solution)/shard_map/ppermute | solution.py:378
  431.4 17.6 %collective-permute-start.15 = (bf16[1536,128]{1,0:T(8,128)(2,1)}, bf16[1536,128]{1,0:T(8,128)(2,1)}, u32[]{:S(2)}, u32[]{:S(2)}) collective-permute-start(bf16[1536,128]{1,0:T(8,128)(2,1)} %add_convert_fusion.7), channel_id=1, source_target_pairs={{1,0},{2,1},{3,2},{5,4},{6,5},{7,6},{9,8},{10,9},{11,10},{13,12},{... | collective-permute-start | bytes 1179656 | tf_op jit(solution)/shard_map/ppermute | solution.py:378
  451.4 27.7 %collective-permute-start.18 = (bf16[1536,128]{1,0:T(8,128)(2,1)}, bf16[1536,128]{1,0:T(8,128)(2,1)}, u32[]{:S(2)}, u32[]{:S(2)}) collective-permute-start(bf16[1536,128]{1,0:T(8,128)(2,1)} %get-tuple-element.166), channel_id=1, source_target_pairs={{1,0},{2,1},{3,2},{5,4},{6,5},{7,6},{9,8},{10,9},{11,10},{13,12},{... | collective-permute-start | bytes 1179656 | tf_op jit(solution)/shard_map/ppermute | solution.py:378
  480.8 189.8 %all-gather.21.cloned.1.call-start = ((), (), s32[]{:S(2)}) async-start(), calls=%async_computation.16 | async-start | bytes 7077888 | tf_op jit(solution)/shard_map/all_gather | solution.py:427
  485.3 57.4 %copy-start.25 = (bf16[256,3072]{1,0:T(8,128)(2,1)S(1)}, bf16[256,3072]{1,0:T(8,128)(2,1)}, u32[]{:S(2)}) copy-start(bf16[256,3072]{1,0:T(8,128)(2,1)} %get-tuple-element.94) | copy-start | bytes 4718596
  485.3 28.8 %collective-permute-start.16 = (bf16[1536,128]{1,0:T(8,128)(2,1)}, bf16[1536,128]{1,0:T(8,128)(2,1)S(1)}, u32[]{:S(2)}, u32[]{:S(2)}) collective-permute-start(bf16[1536,128]{1,0:T(8,128)(2,1)} %get-tuple-element.165), channel_id=1, source_target_pairs={{1,0},{2,1},{3,2},{5,4},{6,5},{7,6},{9,8},{10,9},{11,10},{13,12},{... | collective-permute-start | bytes 1179656 | tf_op jit(solution)/shard_map/ppermute | solution.py:378
  488.0 53.7 %collective-permute-start.19 = (bf16[1536,128]{1,0:T(8,128)(2,1)S(1)}, bf16[1536,128]{1,0:T(8,128)(2,1)S(1)}, u32[]{:S(2)}, u32[]{:S(2)}) collective-permute-start(bf16[1536,128]{1,0:T(8,128)(2,1)S(1)} %add_convert_fusion.4), channel_id=1, source_target_pairs={{1,0},{2,1},{3,2},{5,4},{6,5},{7,6},{9,8},{10,9},{11,10},{13,12},{... | collective-permute-start | bytes 1179656 | tf_op jit(solution)/shard_map/ppermute | solution.py:378
  544.0 45.0 %all-to-all-start.2 = ((bf16[8,256,384]{2,1,0:T(8,128)(2,1)}), bf16[8,256,384]{2,1,0:T(8,128)(2,1)S(1)}, u32[]{:S(2)}, u32[]{:S(2)}) async-start(bf16[8,256,384]{2,1,0:T(8,128)(2,1)} %bitcast.178), calls=%async_computation.2 | async-start | bytes 3145728 | tf_op jit(solution)/shard_map/all_to_all | solution.py:431
  547.6 201.6 %all-gather.23.cloned.1.call-start = ((), (), s32[]{:S(2)}) async-start(), calls=%async_computation.18 | async-start | bytes 7077888 | tf_op jit(solution)/shard_map/all_gather | solution.py:427
  585.3 6.3 collective-permute-start.20
  611.0 38.3 %all-to-all-start.3 = ((bf16[8,256,512]{2,1,0:T(8,128)(2,1)}), bf16[8,256,512]{2,1,0:T(8,128)(2,1)}, u32[]{:S(2)}, u32[]{:S(2)}) async-start(bf16[8,256,512]{2,1,0:T(8,128)(2,1)} %maximum_bitcast_fusion), calls=%async_computation.3 | async-start | bytes 4194304 | tf_op jit(solution)/shard_map/all_to_all | solution.py:431
  649.3 35.4 %all-to-all-start.4 = ((bf16[8,256,384]{2,1,0:T(8,128)(2,1)}), bf16[8,256,384]{2,1,0:T(8,128)(2,1)}, u32[]{:S(2)}, u32[]{:S(2)}) async-start(bf16[8,256,384]{2,1,0:T(8,128)(2,1)} %bitcast.189), calls=%async_computation.4 | async-start | bytes 3145728 | tf_op jit(solution)/shard_map/all_to_all | solution.py:431
  653.8 203.1 %reduce-scatter.11.cloned.1.call-start = ((), (), s32[]{:S(2)}) async-start(), calls=%async_computation.21 | async-start | bytes 1966080 | tf_op jit(solution)/shard_map/reduce_scatter | solution.py:442
  654.7 13.4 %collective-permute-start.21 = (bf16[1536,128]{1,0:T(8,128)(2,1)S(1)}, bf16[1536,128]{1,0:T(8,128)(2,1)S(1)}, u32[]{:S(2)}, u32[]{:S(2)}) collective-permute-start(bf16[1536,128]{1,0:T(8,128)(2,1)S(1)} %get-tuple-element.164), channel_id=1, source_target_pairs={{1,0},{2,1},{3,2},{5,4},{6,5},{7,6},{9,8},{10,9},{11,10},{13,12},{... | collective-permute-start | bytes 1179656 | tf_op jit(solution)/shard_map/ppermute | solution.py:378
  664.0 28.6 %collective-permute-start.24 = (bf16[1536,128]{1,0:T(8,128)(2,1)}, bf16[1536,128]{1,0:T(8,128)(2,1)}, u32[]{:S(2)}, u32[]{:S(2)}) collective-permute-start(bf16[1536,128]{1,0:T(8,128)(2,1)} %get-tuple-element.163), channel_id=1, source_target_pairs={{1,0},{2,1},{3,2},{5,4},{6,5},{7,6},{9,8},{10,9},{11,10},{13,12},{... | collective-permute-start | bytes 1179656 | tf_op jit(solution)/shard_map/ppermute | solution.py:378
  669.1 23.5 %collective-permute-start.22 = (bf16[1536,128]{1,0:T(8,128)(2,1)}, bf16[1536,128]{1,0:T(8,128)(2,1)}, u32[]{:S(2)}, u32[]{:S(2)}) collective-permute-start(bf16[1536,128]{1,0:T(8,128)(2,1)} %add_convert_fusion.3), channel_id=1, source_target_pairs={{1,0},{2,1},{3,2},{5,4},{6,5},{7,6},{9,8},{10,9},{11,10},{13,12},{... | collective-permute-start | bytes 1179656 | tf_op jit(solution)/shard_map/ppermute | solution.py:378
  694.9 10.1 %collective-permute-start.25 = (bf16[1536,128]{1,0:T(8,128)(2,1)S(1)}, bf16[1536,128]{1,0:T(8,128)(2,1)S(1)}, u32[]{:S(2)}, u32[]{:S(2)}) collective-permute-start(bf16[1536,128]{1,0:T(8,128)(2,1)S(1)} %get-tuple-element.162), channel_id=1, source_target_pairs={{1,0},{2,1},{3,2},{5,4},{6,5},{7,6},{9,8},{10,9},{11,10},{13,12},{... | collective-permute-start | bytes 1179656 | tf_op jit(solution)/shard_map/ppermute | solution.py:378
  705.7 190.1 %reduce-scatter.7.cloned.1.call-start = ((), (), s32[]{:S(2)}) async-start(), calls=%async_computation.19 | async-start | bytes 2949120 | tf_op jit(solution)/shard_map/reduce_scatter | solution.py:442
  706.1 24.1 %collective-permute-start.23 = (bf16[1536,128]{1,0:T(8,128)(2,1)}, bf16[1536,128]{1,0:T(8,128)(2,1)}, u32[]{:S(2)}, u32[]{:S(2)}) collective-permute-start(bf16[1536,128]{1,0:T(8,128)(2,1)} %get-tuple-element.161), channel_id=1, source_target_pairs={{1,0},{2,1},{3,2},{5,4},{6,5},{7,6},{9,8},{10,9},{11,10},{13,12},{... | collective-permute-start | bytes 1179656 | tf_op jit(solution)/shard_map/ppermute | solution.py:378
  709.4 37.7 %collective-permute-start.26 = (bf16[1536,128]{1,0:T(8,128)(2,1)}, bf16[1536,128]{1,0:T(8,128)(2,1)S(1)}, u32[]{:S(2)}, u32[]{:S(2)}) collective-permute-start(bf16[1536,128]{1,0:T(8,128)(2,1)} %add_convert_fusion), channel_id=1, source_target_pairs={{1,0},{2,1},{3,2},{5,4},{6,5},{7,6},{9,8},{10,9},{11,10},{13,12},{... | collective-permute-start | bytes 1179656 | tf_op jit(solution)/shard_map/ppermute | solution.py:378
  710.8 38.4 %copy-start.38 = (f32[8,3328]{1,0:T(8,128)}, f32[8,3328]{1,0:T(8,128)S(1)}, u32[]{:S(2)}) copy-start(f32[8,3328]{1,0:T(8,128)S(1)} %constant_dynamic-update-slice_fusion.6) | copy-start | bytes 319492
  793.6 6.8 collective-permute-start.27
  810.2 38.5 %all-to-all-start.5 = ((bf16[8,256,512]{2,1,0:T(8,128)(2,1)}), bf16[8,256,512]{2,1,0:T(8,128)(2,1)}, u32[]{:S(2)}, u32[]{:S(2)}) async-start(bf16[8,256,512]{2,1,0:T(8,128)(2,1)} %maximum_bitcast_fusion.1), calls=%async_computation.7 | async-start | bytes 4194304 | tf_op jit(solution)/shard_map/all_to_all | solution.py:431
  822.0 75.0 %reduce-scatter.9.cloned.1.call-start = ((), (), s32[]{:S(2)}) async-start(), calls=%async_computation.20 | async-start | bytes 1966080 | tf_op jit(solution)/shard_map/reduce_scatter | solution.py:442
  859.7 15.0 %all-to-all-start.7 = ((bf16[8,48,806]{2,1,0:T(8,128)(2,1)}), bf16[8,48,806]{2,1,0:T(8,128)(2,1)S(1)}, u32[]{:S(2)}, u32[]{:S(2)}) async-start(bf16[8,48,806]{2,1,0:T(8,128)(2,1)} %bitcast.55), calls=%async_computation.11 | async-start | bytes 1376256 | tf_op jit(solution)/shard_map/all_to_all | solution.py:486
  863.3 11.6 %collective-permute-start.28 = (f32[336,128]{1,0:T(8,128)S(1)}, f32[336,128]{1,0:T(8,128)S(1)}, u32[]{:S(2)}, u32[]{:S(2)}) collective-permute-start(f32[336,128]{1,0:T(8,128)S(1)} %pad_bitcast_fusion), channel_id=1, source_target_pairs={{0,4},{4,0},{8,12},{12,8},{16,20},{20,16},{24,28},{28,24},{1,5},{5... | collective-permute-start | bytes 516104 | tf_op jit(solution)/shard_map/ppermute | solution.py:409
  875.6 7.5 collective-permute-start.29
  884.0 6.2 collective-permute-start.30
  890.3 5.5 collective-permute-start.31
  895.8 8.8 collective-permute-start.32
  898.9 15.1 %all-to-all-start.6 = ((bf16[8,48,806]{2,1,0:T(8,128)(2,1)}), bf16[8,48,806]{2,1,0:T(8,128)(2,1)S(1)}, u32[]{:S(2)}, u32[]{:S(2)}) async-start(bf16[8,48,806]{2,1,0:T(8,128)(2,1)} %bitcast.53), calls=%async_computation.9 | async-start | bytes 1376256 | tf_op jit(solution)/shard_map/all_to_all | solution.py:486
  (79 other events, 448.5 us)
Sparse Core Ops, SparseCore 0:
  11.6 106.2 all-gather.24
  119.8 58.6 all-gather.26
  180.5 63.6 all-gather.12
  245.9 58.6 all-gather.14
  306.9 60.0 all-gather.28
  368.8 49.7 all-gather.18
  420.4 51.8 all-gather.16
  480.9 64.5 reduce-scatter.4
  547.4 53.2 all-gather.20
  605.3 75.9 all-gather.22
  705.9 45.6 reduce-scatter.10
  791.8 50.3 reduce-scatter.6
  857.0 31.7 reduce-scatter.8
